TPU v7x, 32 devices: a whole 2x2x4 slice. The times are simulated.
32 devices in a mesh: dp: 16 (over z, y, x), mp: 2 (over core).
Axes of the slice: x: 2, y: 2, z: 4, core: 2. Of those that a mesh axis runs over, the one named last changes fastest.
Arguments:
- pixels: bfloat16 [16, 13, 256, 256], P('dp'), may hold values from -6 to 6
- band_count: int32 [16], P('dp'), may hold values from 1 to 13
- wavelengths: int32 [16, 13], P('dp'), may hold values from 40 to 249
- size_class: int32 [16], P('dp'), may hold values from 0 to 2
- token_keep: int32 [16, 256], P('dp'), may hold values 0 or 1
- hyp_attn: float32 [4, 128, 128], replicated, may hold values from -0.75 to 0.75
- hyp_mlp_in: float32 [128, 2048], replicated, may hold values from -0.5 to 0.5
- hyp_mlp_out: float32 [2048, 128], replicated, may hold values from -0.125 to 0.125
- hyp_gain: float32 [2, 128], replicated, may hold values from 0.5 to 1.5
- hyp_shift: float32 [2, 128], replicated, may hold values from -4 to 4
- bias_token: float32 [128], replicated, may hold values from -6 to 6
- kern_weight: float32 [128, 768, 256], P(None, 'dp'), may hold values from -0.009765625 to 0.009765625
- kern_bias: float32 [768, 256], P('dp'), may hold values from -0.125 to 0.125
- patch_bias_weight: float32 [128, 768], replicated, may hold values from -0.5 to 0.5
- norm_gain: float32 [2, 768], replicated, may hold values from 0.5 to 1.5
- norm_shift: float32 [2, 768], replicated, may hold values from -4 to 4
- attn_in: float32 [3, 768, 768], P(None, 'dp', 'mp'), may hold values from -0.21875 to 0.21875
- attn_in_bias: float32 [2, 768], P(None, 'mp'), may hold values from -4 to 4
- attn_out: float32 [768, 768], P('dp', 'mp'), may hold values from -0.625 to 0.625
- attn_out_bias: float32 [768], replicated, may hold values from -4 to 4
- mlp_in: float32 [768, 3072], P('dp', 'mp'), may hold values from -0.21875 to 0.21875
- mlp_in_bias: float32 [3072], P('mp'), may hold values from -4 to 4
- mlp_out: float32 [768, 3072], P('dp', 'mp'), may hold values from -0.109375 to 0.109375
- mlp_out_bias: float32 [768], replicated, may hold values from -4 to 4
- cotangent: bfloat16 [16, 256, 768], P('dp'), may hold values from -6 to 6
Outputs:
- layer_out: bfloat16 [16, 256, 768], P('dp')
- pixel_grad: bfloat16 [16, 13, 256, 256], P('dp')
- grad_hyp_attn: float32 [4, 128, 128], replicated
- grad_hyp_mlp_in: float32 [128, 2048], replicated
- grad_hyp_mlp_out: float32 [2048, 128], replicated
- grad_hyp_gain: float32 [2, 128], replicated
- grad_hyp_shift: float32 [2, 128], replicated
- grad_bias_token: float32 [128], replicated
- grad_kern_weight: float32 [128, 768, 256], P(None, 'dp')
- grad_kern_bias: float32 [768, 256], P('dp')
- grad_patch_bias_weight: float32 [128, 768], replicated
- grad_norm_gain: float32 [2, 768], replicated
- grad_norm_shift: float32 [2, 768], replicated
- grad_attn_in: float32 [3, 768, 768], P(None, 'dp', 'mp')
- grad_attn_in_bias: float32 [2, 768], P(None, 'mp')
- grad_attn_out: float32 [768, 768], P('dp', 'mp')
- grad_attn_out_bias: float32 [768], replicated
- grad_mlp_in: float32 [768, 3072], P('dp', 'mp')
- grad_mlp_in_bias: float32 [3072], P('mp')
- grad_mlp_out: float32 [768, 3072], P('dp', 'mp')
- grad_mlp_out_bias: float32 [768], replicated
Inputs may be any that keep to these rules, and one draw needn't show every extreme that they name: Bands 0 to band_count[s] - 1 of slot s are present.
All inputs are finite; a program needn't handle non-finite values. No bound on the sum of `token_keep` on one device may be relied on, other than what follows from the above.
Results may differ from a plain program's by a relative error of at most 0.013.
Values may be sent and summed in bfloat16 or wider, within the bound.
A program may use at most 192 MiB of HBM per device.

v0:
```python
from functools import partial
import math

import jax
import jax.numpy as jnp
from jax import lax
from jax.sharding import PartitionSpec as P

HEAD_DIM = 64
HYP_HEADS = 4


vit_epsilon = 1e-06
hyper_epsilon = 1e-05


def exact_einsum(pattern, left_side, right_side):
    return jnp.einsum(
        pattern,
        left_side,
        right_side,
        precision=lax.Precision.HIGHEST,
        preferred_element_type=jnp.float32,
    )


def fast_einsum(pattern, left_side, right_side):
    return jnp.einsum(pattern, left_side, right_side, preferred_element_type=jnp.float32)


def norm_rows(values, gain_row, shift_row, epsilon):
    center = values - jnp.mean(values, axis=-1, keepdims=True)
    spread = jnp.mean(center * center, axis=-1, keepdims=True)
    return center * lax.rsqrt(spread + epsilon) * gain_row + shift_row


def exact_gelu(values):
    return jax.nn.gelu(values, approximate=False)


def wave_embedding(wavelengths, model_width):
    half_width = model_width // 2
    frequency = 10000.0 ** (-jnp.arange(half_width, dtype=jnp.float32) * 2.0 / model_width)
    angles = wavelengths.astype(jnp.float32)[..., None] * frequency
    return jnp.concatenate([jnp.sin(angles), jnp.cos(angles)], axis=-1)


def hyper_slot(
    embedding, band_valid, hyp_attn, hyp_mlp_in, hyp_mlp_out, hyp_gain, hyp_shift, bias_token
):
    model_width = embedding.shape[-1]
    sequence = jnp.concatenate([embedding, bias_token[None, :]], axis=0)
    keys_valid = jnp.concatenate([band_valid, jnp.ones((1,), dtype=bool)])
    length = sequence.shape[0]
    head_size = model_width // HYP_HEADS
    query_rows = exact_einsum("te,ef->tf", sequence, hyp_attn[0]).reshape(
        length, HYP_HEADS, head_size
    )
    key_rows = exact_einsum("te,ef->tf", sequence, hyp_attn[1]).reshape(
        length, HYP_HEADS, head_size
    )
    value_rows = exact_einsum("te,ef->tf", sequence, hyp_attn[2]).reshape(
        length, HYP_HEADS, head_size
    )
    scores = exact_einsum("qhd,khd->hqk", query_rows, key_rows) * (1.0 / math.sqrt(head_size))
    scores = jnp.where(keys_valid[None, None, :], scores, -1e30)
    weights = jax.nn.softmax(scores, axis=-1)
    mixed_rows = exact_einsum("hqk,khd->qhd", weights, value_rows).reshape(length, model_width)
    first_rows = norm_rows(
        sequence + exact_einsum("te,ef->tf", mixed_rows, hyp_attn[3]),
        hyp_gain[0],
        hyp_shift[0],
        hyper_epsilon,
    )
    inner_rows = exact_gelu(exact_einsum("te,ef->tf", first_rows, hyp_mlp_in))
    second_rows = norm_rows(
        first_rows + exact_einsum("tf,fe->te", inner_rows, hyp_mlp_out),
        hyp_gain[1],
        hyp_shift[1],
        hyper_epsilon,
    )
    return (second_rows[:-1] + embedding, second_rows[-1])


def hyper_all(
    embed_rows, valid_rows, attn_w, mlp_first, mlp_second, gain_rows, shift_rows, token_row, bias_w
):
    code_vals, tail_rows = jax.vmap(hyper_slot, in_axes=(0, 0, None, None, None, None, None, None))(
        embed_rows, valid_rows, attn_w, mlp_first, mlp_second, gain_rows, shift_rows, token_row
    )
    return (code_vals, exact_einsum("se,ec->sc", tail_rows, bias_w))


def per_device(
    pixels,
    band_count,
    wavelengths,
    size_class,
    token_keep,
    hyp_attn,
    hyp_mlp_in,
    hyp_mlp_out,
    hyp_gain,
    hyp_shift,
    bias_token,
    kern_weight,
    kern_bias,
    patch_bias_weight,
    norm_gain,
    norm_shift,
    attn_in,
    attn_in_bias,
    attn_out,
    attn_out_bias,
    mlp_in,
    mlp_in_bias,
    mlp_out,
    mlp_out_bias,
    cotangent,
):
    slot_count, band_total, row_total, pix_size = pixels.shape
    model_width = norm_gain.shape[1]
    hyper_width = hyp_attn.shape[1]
    tokens = slot_count * row_total
    embedding = wave_embedding(wavelengths, hyper_width)
    band_valid = jnp.arange(band_total)[None, :] < band_count[:, None]
    live_rows = jnp.where(
        size_class == 0,
        row_total * 49 // 256,
        jnp.where(size_class == 1, row_total * 196 // 256, row_total),
    )
    position = jnp.arange(row_total)
    row_valid = position[None, :] < live_rows[:, None]
    key_valid = row_valid & ((token_keep == 1) | (position[None, :] == 0))
    row_scale = row_valid.astype(jnp.float32).reshape(tokens, 1)
    band_mask = band_valid.astype(jnp.bfloat16)[:, :, None, None]
    hyper_local = partial(hyper_all, embedding, band_valid)
    (code_vals, patch_bias), hyper_back = jax.vjp(
        hyper_local,
        hyp_attn,
        hyp_mlp_in,
        hyp_mlp_out,
        hyp_gain,
        hyp_shift,
        bias_token,
        patch_bias_weight,
    )
    code_rows = code_vals.astype(jnp.bfloat16).reshape(slot_count * band_total, hyper_width)
    all_codes = lax.all_gather(code_rows, "dp", axis=0, tiled=True)
    kern_low = kern_weight.astype(jnp.bfloat16)
    local_full = (fast_einsum("ne,ecp->ncp", all_codes, kern_low) + kern_bias).astype(jnp.bfloat16)
    kernel = lax.all_to_all(local_full, "dp", split_axis=0, concat_axis=1, tiled=True)
    kernel = kernel.reshape(slot_count, band_total, model_width, pix_size)
    masked_pixels = pixels * band_mask
    embedded = fast_einsum("sbtp,sbcp->stc", masked_pixels, kernel) + patch_bias[:, None, :]
    embedded = embedded.reshape(tokens, model_width)
    weight_shards = (
        attn_in.astype(jnp.bfloat16),
        attn_out.astype(jnp.bfloat16),
        mlp_in.astype(jnp.bfloat16),
        mlp_out.astype(jnp.bfloat16),
    )
    gathered_in, gathered_out, gathered_up, gathered_down = (
        lax.all_gather(weight_shards[0], "dp", axis=1, tiled=True),
        lax.all_gather(weight_shards[1], "dp", axis=0, tiled=True),
        lax.all_gather(weight_shards[2], "dp", axis=0, tiled=True),
        lax.all_gather(weight_shards[3], "dp", axis=0, tiled=True),
    )
    local_heads = gathered_in.shape[2] // HEAD_DIM
    head_grid = (slot_count, row_total, local_heads, HEAD_DIM)
    score_scale = 1.0 / math.sqrt(HEAD_DIM)
    key_open = key_valid[:, None, None, :]
    norm_one = partial(norm_rows, epsilon=vit_epsilon)
    normed_a, first_back = jax.vjp(norm_one, embedded, norm_gain[0], norm_shift[0])
    normed_a = normed_a.astype(jnp.bfloat16)
    input_bias = jnp.stack([attn_in_bias[0], jnp.zeros_like(attn_in_bias[0]), attn_in_bias[1]])[
        :, None, :
    ]
    projected = (fast_einsum("nd,jde->jne", normed_a, gathered_in) + input_bias).astype(
        jnp.bfloat16
    )
    query_rows = projected[0].reshape(head_grid)
    key_rows = projected[1].reshape(head_grid)
    value_rows = projected[2].reshape(head_grid)
    scores = jnp.where(
        key_open, fast_einsum("sqhd,skhd->shqk", query_rows, key_rows) * score_scale, -1e30
    )
    row_peak = jnp.max(scores, axis=-1, keepdims=True)
    exp_scores = jnp.exp(scores - row_peak)
    prob_total = jnp.sum(exp_scores, axis=-1, keepdims=True)
    log_total = row_peak + jnp.log(prob_total)
    prob_low = (exp_scores / prob_total).astype(jnp.bfloat16)
    context = (
        fast_einsum("shqk,skhd->sqhd", prob_low, value_rows)
        .reshape(tokens, local_heads * HEAD_DIM)
        .astype(jnp.bfloat16)
    )
    head_part = fast_einsum("ne,de->nd", context, gathered_out)
    middle = embedded + lax.psum(head_part, "mp") + attn_out_bias
    normed_b, second_back = jax.vjp(norm_one, middle, norm_gain[1], norm_shift[1])
    normed_b = normed_b.astype(jnp.bfloat16)
    pre_act = fast_einsum("nd,df->nf", normed_b, gathered_up) + mlp_in_bias
    activation, gelu_back = jax.vjp(exact_gelu, pre_act)
    activation = activation.astype(jnp.bfloat16)
    unit_part = fast_einsum("nf,df->nd", activation, gathered_down)
    final_rows = (
        middle + lax.psum(unit_part.astype(jnp.bfloat16), "mp").astype(jnp.float32) + mlp_out_bias
    ) * row_scale
    layer_out = final_rows.astype(jnp.bfloat16).reshape(slot_count, row_total, model_width)
    gathered_in, gathered_out, gathered_up, gathered_down = (
        lax.all_gather(weight_shards[0], "dp", axis=1, tiled=True),
        lax.all_gather(weight_shards[1], "dp", axis=0, tiled=True),
        lax.all_gather(weight_shards[2], "dp", axis=0, tiled=True),
        lax.all_gather(weight_shards[3], "dp", axis=0, tiled=True),
    )
    out_grad = cotangent.reshape(tokens, model_width).astype(jnp.float32) * row_scale
    out_grad_low = out_grad.astype(jnp.bfloat16)
    grad_mlp_out_bias = jnp.sum(out_grad, axis=0)
    grad_down = fast_einsum("nd,nf->df", out_grad_low, activation)
    act_grad = fast_einsum("nd,df->nf", out_grad_low, gathered_down).astype(jnp.bfloat16)
    pre_grad = gelu_back(act_grad.astype(jnp.float32))[0].astype(jnp.bfloat16)
    grad_mlp_in_bias = jnp.sum(pre_grad, axis=0, dtype=jnp.float32)
    grad_up = fast_einsum("nd,nf->df", normed_b, pre_grad)
    second_part = fast_einsum("nf,df->nd", pre_grad, gathered_up)
    middle_in, gain_second, shift_second = second_back(lax.psum(second_part, "mp"))
    middle_grad = out_grad + middle_in
    attended_grad = middle_grad.astype(jnp.bfloat16)
    grad_attn_out_bias = jnp.sum(attended_grad, axis=0, dtype=jnp.float32)
    grad_proj = fast_einsum("nd,ne->de", attended_grad, context)
    context_grad = (
        fast_einsum("nd,de->ne", attended_grad, gathered_out)
        .astype(jnp.bfloat16)
        .reshape(head_grid)
    )
    scores_again = jnp.where(
        key_open, fast_einsum("sqhd,skhd->shqk", query_rows, key_rows) * score_scale, -1e30
    )
    prob_full = jnp.exp(scores_again - log_total)
    prob_grad = fast_einsum("sqhd,skhd->shqk", context_grad, value_rows)
    row_inner = jnp.sum(prob_full * prob_grad, axis=-1, keepdims=True)
    score_grad = (prob_full * (prob_grad - row_inner)).astype(jnp.bfloat16)
    query_grad = fast_einsum("shqk,skhd->sqhd", score_grad, key_rows) * score_scale
    key_grad = fast_einsum("shqk,sqhd->skhd", score_grad, query_rows) * score_scale
    value_grad = fast_einsum("shqk,sqhd->skhd", prob_low, context_grad)
    qkv_grad = (
        jnp.stack([query_grad, key_grad, value_grad])
        .reshape(3, tokens, local_heads * HEAD_DIM)
        .astype(jnp.bfloat16)
    )
    grad_in_bias = jnp.stack(
        [
            jnp.sum(qkv_grad[0], axis=0, dtype=jnp.float32),
            jnp.sum(qkv_grad[2], axis=0, dtype=jnp.float32),
        ]
    )
    grad_in = fast_einsum("nd,jne->jde", normed_a, qkv_grad)
    first_part = fast_einsum("jne,jde->nd", qkv_grad, gathered_in)
    embed_in, gain_first, shift_first = first_back(lax.psum(first_part, "mp"))
    embed_grad = (
        (middle_grad + embed_in).astype(jnp.bfloat16).reshape(slot_count, row_total, model_width)
    )
    patch_bias_grad = jnp.sum(embed_grad, axis=1, dtype=jnp.float32)
    band_float = band_valid.astype(jnp.float32)[:, :, None, None]
    pixel_grad = (fast_einsum("stc,sbcp->sbtp", embed_grad, kernel) * band_float).astype(
        jnp.bfloat16
    )
    kernel_grad = (
        fast_einsum("stc,sbtp->sbcp", embed_grad, masked_pixels)
        .astype(jnp.bfloat16)
        .reshape(slot_count * band_total, model_width, pix_size)
    )
    local_grad = lax.all_to_all(kernel_grad, "dp", split_axis=1, concat_axis=0, tiled=True)
    grad_kern_weight = fast_einsum("ne,ncp->ecp", all_codes, local_grad)
    grad_kern_bias = jnp.sum(local_grad, axis=0, dtype=jnp.float32)
    code_part = fast_einsum("ncp,ecp->ne", local_grad, kern_low)
    grad_attn_in, grad_attn_out, grad_mlp_in, grad_mlp_out = (
        lax.psum_scatter(grad_in, "dp", scatter_dimension=1, tiled=True),
        lax.psum_scatter(grad_proj, "dp", scatter_dimension=0, tiled=True),
        lax.psum_scatter(grad_up, "dp", scatter_dimension=0, tiled=True),
        lax.psum_scatter(grad_down, "dp", scatter_dimension=0, tiled=True),
    )
    norms_gain = jnp.stack([gain_first, gain_second])
    norms_shift = jnp.stack([shift_first, shift_second])
    code_grad = lax.psum_scatter(code_part, "dp", scatter_dimension=0, tiled=True).reshape(
        slot_count, band_total, hyper_width
    )
    local_hyper = hyper_back((code_grad, patch_bias_grad))
    summed = lax.psum(
        (
            local_hyper[0],
            local_hyper[1],
            local_hyper[2],
            local_hyper[3],
            local_hyper[4],
            local_hyper[5],
            local_hyper[6],
            norms_gain,
            norms_shift,
            grad_in_bias,
            grad_attn_out_bias,
            grad_mlp_in_bias,
            grad_mlp_out_bias,
        ),
        "dp",
    )
    hyper_grads = summed[:7]
    others = summed[7:]
    return (
        layer_out,
        pixel_grad,
        hyper_grads[0],
        hyper_grads[1],
        hyper_grads[2],
        hyper_grads[3],
        hyper_grads[4],
        hyper_grads[5],
        grad_kern_weight,
        grad_kern_bias,
        hyper_grads[6],
        others[0],
        others[1],
        grad_attn_in,
        others[2],
        grad_attn_out,
        others[3],
        grad_mlp_in,
        others[4],
        grad_mlp_out,
        others[5],
    )


def solution(mesh):
    return jax.shard_map(
        per_device,
        mesh=mesh,
        in_specs=(
            P("dp", None, None, None),
            P("dp"),
            P("dp", None),
            P("dp"),
            P("dp", None),
            P(),
            P(),
            P(),
            P(),
            P(),
            P(),
            P(None, "dp", None),
            P("dp", None),
            P(),
            P(),
            P(),
            P(None, "dp", "mp"),
            P(None, "mp"),
            P("dp", "mp"),
            P(),
            P("dp", "mp"),
            P("mp"),
            P("dp", "mp"),
            P(),
            P("dp", None, None),
        ),
        out_specs=(
            P("dp", None, None),
            P("dp", None, None, None),
            P(),
            P(),
            P(),
            P(),
            P(),
            P(),
            P(None, "dp", None),
            P("dp", None),
            P(),
            P(),
            P(),
            P(None, "dp", "mp"),
            P(None, "mp"),
            P("dp", "mp"),
            P(),
            P("dp", "mp"),
            P("mp"),
            P("dp", "mp"),
            P(),
        ),
        check_vma=False,
    )
```

profile of v0, /device:TPU:0, one launch (start us, length us, event | category | flops | bytes accessed | tf_op | source)
XLA Modules:
  0.0 1387.8 jit_solution(8111671895934261146)
XLA Ops:
  9.7 1.6 fusion.136
  18.4 42.9 %all-gather = bf16[1,208,128]{2,0,1:T(2,128)(2,1)S(1)} all-gather(bf16[1,13,128]{2,0,1:T(2,128)(2,1)S(1)} %copy.152), channel_id=2, replica_groups=mesh['dp'=16,'mp'=2] {'dp'}, dimensions={1}, use_global_device_ids=true | all-gather | bytes 56576 | tf_op jit(solution)/shard_map/all_gather | solution.py:149
  61.4 3.2 convert_element_type.166
  64.6 1.7 copy-done.4
  66.2 1.5 add_convert_fusion
  67.8 4.1 copy.154
  72.0 4.7 all-to-all-start
  79.9 134.4 %all_gather.21 = bf16[768,384]{1,0:T(8,128)(2,1)} all-gather(bf16[48,384]{1,0:T(8,128)(2,1)S(1)} %convert_element_type.177), channel_id=1, replica_groups=mesh['dp'=16,'mp'=2] {'dp'}, dimensions={0}, use_global_device_ids=true | all-gather | bytes 626688 | tf_op jit(solution)/shard_map/all_gather | solution.py:165
  214.3 3.1 copy.155
  217.4 1.6 fusion.142
  220.5 2.3 fusion.29
  226.9 1.3 fusion.144
  230.3 32.6 %all-reduce.21.cloned.1.call-done = f32[256,768]{1,0:T(8,128)} async-done(((f32[256,768]{1,0:T(8,128)}), f32[256,768]{1,0:T(8,128)}) %all-reduce.21.cloned.1.call-update) | async-done | bytes 786448 | tf_op jit(solution)/shard_map/psum | solution.py:199
  263.0 1.6 fusion.134
  266.5 63.8 %all-gather.7.cloned.1.call-done = bf16[768,1536]{1,0:T(8,128)(2,1)} async-done(((bf16[48,1536]{1,0:T(8,128)(2,1)}), bf16[768,1536]{1,0:T(8,128)(2,1)}) %all-gather.7.cloned.1.call-update) | async-done | bytes 2359312 | tf_op jit(solution)/shard_map/all_gather | solution.py:166
  330.2 7.0 multiply_convert_fusion.1
  337.3 57.7 %all-gather.9.cloned.1.call-done = bf16[768,1536]{1,0:T(8,128)(2,1)} async-done(((bf16[48,1536]{1,0:T(8,128)(2,1)}), bf16[768,1536]{1,0:T(8,128)(2,1)}) %all-gather.9.cloned.1.call-update) | async-done | bytes 2359312 | tf_op jit(solution)/shard_map/all_gather | solution.py:167
  395.0 4.7 convert_reduce_fusion.1
  400.6 1.7 fusion.145
  402.3 1.3 log_add_fusion
  403.6 3.5 convolution_convert_fusion.1
  407.3 13.1 all-reduce.25.cloned.1.call-done
  420.4 2.0 multiply_reduce_fusion.1
  423.7 19.2 %all-reduce.23.cloned.1.call-done = bf16[256,768]{1,0:T(8,128)(2,1)} async-done(((bf16[256,768]{1,0:T(8,128)(2,1)}), bf16[256,768]{1,0:T(8,128)(2,1)}) %all-reduce.23.cloned.1.call-update) | async-done | bytes 393232 | tf_op jit(solution)/shard_map/psum | solution.py:207
  442.9 2.5 fusion.132
  449.0 1.7 copy.160
  450.8 2.3 convolution_convert_fusion.2
  453.0 1.5 multiply_reduce_fusion
  457.6 3.2 convolution_bitcast_fusion.1
  460.9 20.5 %all-reduce.27.cloned.1.call-done = f32[256,768]{1,0:T(8,128)} async-done(((f32[256,768]{1,0:T(8,128)}), f32[256,768]{1,0:T(8,128)}) %all-reduce.27.cloned.1.call-update) | async-done | bytes 786448 | tf_op jit(solution)/shard_map/psum | solution.py:258
  481.4 2.1 multiply_reduce_fusion.2
  486.9 4.2 convert_bitcast_fusion
  491.1 8.6 copy.169
  499.7 6.8 all-to-all-start.1
  506.8 1.3 fusion.138
  511.2 3.7 convolution_bitcast_fusion
  514.9 6.3 copy.180
  522.1 104.6 %all-to-all-done.1 = bf16[13,768,256]{2,0,1:T(8,128)(2,1)} async-done(((bf16[13,768,256]{2,0,1:T(8,128)(2,1)}), bf16[13,768,256]{2,0,1:T(8,128)(2,1)}, u32[]{:S(2)}, u32[]{:S(2)}) %all-to-all-start.1) | async-done | bytes 5111840 | tf_op jit(solution)/shard_map/all_to_all | solution.py:272
  626.6 5.2 copy.171
  631.8 2.3 copy-done.1
  634.1 4.4 fusion.32
  638.5 61.0 %fusion = f32[16,128]{1,0:T(8,128)S(1)} fusion(f32[208,128]{1,0:T(8,128)S(1)} %fusion.32), kind=kCustom, calls=%all-reduce-scatter | all-reduce-scatter fusion | flops 32769 | bytes 115200
  699.5 1.3 collective-permute-start.1
  700.8 3.6 collective-permute-start
  704.4 1.5 collective-permute-start.2
  708.6 2.4 multiply_add_fusion
  711.0 1.5 fusion.73
  714.5 2.1 fusion.97
  716.6 3.0 fusion.67
  722.5 1.4 fusion.146
  725.1 3.1 fusion.125
  729.6 3.1 fusion.49
  733.9 4.2 fusion.18
  738.1 2.5 copy.181
  740.6 4.6 fusion.1
  745.2 6.3 copy.182
  751.6 4.8 copy.170
  756.5 1.5 convert_reduce_fusion
  758.8 79.3 %all-reduce.13 = (f32[2,128]{1,0:T(2,128)}, f32[2,128]{1,0:T(2,128)}, f32[128]{0:T(128)}, f32[2,768]{1,0:T(2,128)}, f32[2,768]{1,0:T(2,128)}, /*index=5*/f32[2,3...) all-reduce(f32[2,128]{1,0:T(2,128)S(1)} %pad_add_fusion.3, ...), channel_id=1, replica_groups=mesh['dp'=16,'mp'=2] {'dp'}, use_global_device_ids=true, to_apply=%region_33.34 | all-reduce | flops 7552 | bytes 60416 | tf_op jit(solution)/shard_map/psum | solution.py:288
  838.1 125.9 %all-reduce.29.cloned.1.call-done = (f32[4,128,128]{2,1,0:T(8,128)}, f32[128,2048]{1,0:T(8,128)}, f32[2048,128]{1,0:T(8,128)}, f32[128,768]{1,0:T(8,128)}, f32[3,768,384]{2,0,1:T(4,128)}) async-done(((f32[4,128,128]{2,1,0:T(8,128)}, f32[128,2048]{1,0:T(8,128)}, f32[2048,128]{1,0:T(8,128)}, f32[128,768]{1,0:T(8,128)}, f32[3,768,384]{2,0,1:T(4,128)}), (f32[4,128,128]{2,1,0:T(8,128)}, f32[128,2048]{1,0:T(8,128)}, ...) | async-done | bytes 6291472 | tf_op jit(solution)/shard_map/psum | solution.py:288
  965.8 126.9 %reduce-scatter.6.cloned.1.call-done = f32[48,384]{1,0:T(8,128)} async-done(((f32[768,384]{1,0:T(8,128)}), f32[48,384]{1,0:T(8,128)}) %reduce-scatter.6.cloned.1.call-update) | async-done | bytes 73744 | tf_op jit(solution)/shard_map/reduce_scatter | solution.py:278
  1092.7 142.0 %reduce-scatter.8.cloned.1.call-done = f32[48,1536]{1,0:T(8,128)} async-done(((f32[768,1536]{1,0:T(8,128)}), f32[48,1536]{1,0:T(8,128)}) %reduce-scatter.8.cloned.1.call-update) | async-done | bytes 294928 | tf_op jit(solution)/shard_map/reduce_scatter | solution.py:279
  1234.6 141.9 %reduce-scatter.10.cloned.1.call-done = f32[48,1536]{1,0:T(8,128)} async-done(((f32[768,1536]{1,0:T(8,128)}), f32[48,1536]{1,0:T(8,128)}) %reduce-scatter.10.cloned.1.call-update) | async-done | bytes 294928 | tf_op jit(solution)/shard_map/reduce_scatter | solution.py:280
  1376.5 1.7 copy.226
  (407 shorter events, 52.0 us)
Async XLA Ops:
  7.2 8.6 copy-start
  7.2 6.7 copy-start.110
  7.2 8.5 copy-start.114
  7.2 8.5 copy-start.115
  7.2 9.2 copy-start.126
  11.8 5.7 copy-start.51
  12.2 5.3 copy-start.47
  12.6 4.9 copy-start.49
  12.9 4.6 copy-start.73
  17.8 46.8 %copy-start.123 = (f32[14]{0:T(128)}, f32[14]{0:T(128)S(1)}, u32[]{:S(2)}) copy-start(f32[14]{0:T(128)S(1)} %multiply_reduce_fusion.8) | copy-start | bytes 172
  18.3 61.1 %copy-start.62 = (f32[1,14,128]{2,1,0:T(8,128)}, f32[1,14,128]{2,1,0:T(8,128)S(1)}, u32[]{:S(2)}) copy-start(f32[1,14,128]{2,1,0:T(8,128)S(1)} %add_bitcast_fusion) | copy-start | bytes 21508
  61.4 4.9 copy-start.63
  71.9 4.8 copy-start.44
  71.9 6.2 copy-start.59
  71.9 6.9 copy-start.113
  71.9 7.4 copy-start.101
  71.9 7.4 copy-start.102
  71.9 7.5 copy-start.28
  72.0 7.8 copy-start.107
  72.0 142.3 %all-to-all-start = ((bf16[208,48,256]{2,1,0:T(8,128)(2,1)}), bf16[208,48,256]{2,1,0:T(8,128)(2,1)}, u32[]{:S(2)}, u32[]{:S(2)}) async-start(bf16[208,48,256]{2,1,0:T(8,128)(2,1)} %copy.154), calls=%async_computation | async-start | bytes 10223616 | tf_op jit(solution)/shard_map/all_to_all | solution.py:152
  76.7 143.2 %all-gather.5.cloned.1.call-start = ((), (), s32[]{:S(2)}) async-start(), calls=%async_computation.5 | async-start | bytes 1880064 | tf_op jit(solution)/shard_map/all_gather | solution.py:164
  77.5 185.5 %all-reduce.21.cloned.1.call-start = ((), (), s32[]{:S(2)}) async-start(), calls=%async_computation.6 | async-start | bytes 1572864 | tf_op jit(solution)/shard_map/psum | solution.py:199
  78.8 138.5 %copy-start.118 = (bf16[13]{0:T(256)(128)(2,1)}, bf16[13]{0:T(256)(128)(2,1)S(1)}, u32[]{:S(2)}) copy-start(bf16[13]{0:T(256)(128)(2,1)S(1)} %get-tuple-element.189) | copy-start | bytes 82
  79.4 140.5 %copy-start.60 = (f32[768]{0:T(1024)}, f32[768]{0:T(1024)S(1)}, u32[]{:S(2)}) copy-start(f32[768]{0:T(1024)S(1)} %get-tuple-element.192) | copy-start | bytes 9220
  79.4 140.5 %copy-start.77 = (f32[768]{0:T(1024)}, f32[768]{0:T(1024)S(1)}, u32[]{:S(2)}) copy-start(f32[768]{0:T(1024)S(1)} %get-tuple-element.120) | copy-start | bytes 9220
  228.2 102.1 %all-gather.7.cloned.1.call-start = ((), (), s32[]{:S(2)}) async-start(), calls=%async_computation.7 | async-start | bytes 2506752 | tf_op jit(solution)/shard_map/all_gather | solution.py:166
  229.0 166.0 %all-gather.9.cloned.1.call-start = ((), (), s32[]{:S(2)}) async-start(), calls=%async_computation.8 | async-start | bytes 2506752 | tf_op jit(solution)/shard_map/all_gather | solution.py:167
  229.7 190.7 %all-reduce.25.cloned.1.call-start = ((), (), s32[]{:S(2)}) async-start(), calls=%async_computation.10 | async-start | bytes 1572864 | tf_op jit(solution)/shard_map/psum | solution.py:225
  395.0 5.6 copy-start.125
  402.3 40.6 %all-reduce.23.cloned.1.call-start = ((), (), s32[]{:S(2)}) async-start(), calls=%async_computation.9 | async-start | bytes 786432 | tf_op jit(solution)/shard_map/psum | solution.py:207
  403.6 16.8 %copy-start.65 = (f32[256]{0:T(256)S(1)}, f32[256]{0:T(256)}, u32[]{:S(2)}) copy-start(f32[256]{0:T(256)} %copy-done.64) | copy-start | bytes 3076
  407.1 35.8 %copy-start.67 = (f32[256]{0:T(256)S(1)}, f32[256]{0:T(256)}, u32[]{:S(2)}) copy-start(f32[256]{0:T(256)} %compare_convert_fusion) | copy-start | bytes 3076
  407.1 74.3 %all-reduce.27.cloned.1.call-start = ((), (), s32[]{:S(2)}) async-start(), calls=%async_computation.11 | async-start | bytes 1572864 | tf_op jit(solution)/shard_map/psum | solution.py:258
  447.2 5.9 copy-start.54
  456.6 4.3 copy-start.33
  457.6 23.8 %copy-start.3 = (f32[256,768]{1,0:T(8,128)S(1)}, f32[256,768]{1,0:T(8,128)}, u32[]{:S(2)}) copy-start(f32[256,768]{1,0:T(8,128)} %copy-done.2) | copy-start | bytes 2359300
  457.6 23.8 %copy-start.61 = (f32[768]{0:T(1024)S(1)}, f32[768]{0:T(1024)}, u32[]{:S(2)}) copy-start(f32[768]{0:T(1024)} %copy-done.60) | copy-start | bytes 9220
  457.6 23.8 %copy-start.72 = (f32[256]{0:T(256)S(1)}, f32[256]{0:T(256)}, u32[]{:S(2)}) copy-start(f32[256]{0:T(256)} %copy-done.71) | copy-start | bytes 3076
  499.7 126.9 %all-to-all-start.1 = ((bf16[13,768,256]{2,0,1:T(8,128)(2,1)}), bf16[13,768,256]{2,0,1:T(8,128)(2,1)}, u32[]{:S(2)}, u32[]{:S(2)}) async-start(bf16[13,768,256]{2,0,1:T(8,128)(2,1)} %copy.169), calls=%async_computation.1 | async-start | bytes 12582912 | tf_op jit(solution)/shard_map/all_to_all | solution.py:272
  506.5 457.4 %all-reduce.29.cloned.1.call-start = ((), (), s32[]{:S(2)}) async-start(), calls=%async_computation.15 | async-start | bytes 14942208 | tf_op jit(solution)/shard_map/psum | solution.py:288
  514.9 6.3 copy-start.120
  626.6 7.5 copy-start.5
  634.1 71.9 %copy-start.29 = (f32[128,768]{1,0:T(8,128)S(1)}, f32[128,768]{1,0:T(8,128)}, u32[]{:S(2)}) copy-start(f32[128,768]{1,0:T(8,128)} %param.38) | copy-start | bytes 1179652
  634.1 73.4 %copy-start.95 = (f32[14]{0:T(128)S(1)}, f32[14]{0:T(128)}, u32[]{:S(2)}) copy-start(f32[14]{0:T(128)} %copy-done.94) | copy-start | bytes 172
  634.1 73.4 %copy-start.97 = (f32[128]{0:T(128)S(1)}, f32[128]{0:T(128)}, u32[]{:S(2)}) copy-start(f32[128]{0:T(128)} %copy-done.96) | copy-start | bytes 1540
  634.1 73.4 %copy-start.106 = (f32[14]{0:T(128)S(1)}, f32[14]{0:T(128)}, u32[]{:S(2)}) copy-start(f32[14]{0:T(128)} %copy-done.105) | copy-start | bytes 172
  634.1 74.1 %copy-start.124 = (f32[14]{0:T(128)S(1)}, f32[14]{0:T(128)}, u32[]{:S(2)}) copy-start(f32[14]{0:T(128)} %copy-done.123) | copy-start | bytes 172
  634.1 74.3 %copy-start.46 = (f32[14,2048]{1,0:T(8,128)S(1)}, f32[14,2048]{1,0:T(8,128)}, u32[]{:S(2)}) copy-start(f32[14,2048]{1,0:T(8,128)} %copy-done.45) | copy-start | bytes 344068
  699.5 7.6 collective-permute-start.1
  700.8 6.3 collective-permute-start
  704.4 2.6 collective-permute-start.2
  708.5 4.3 copy-start.43
  708.5 4.7 copy-start.42
  708.5 4.7 copy-start.52
  708.5 4.7 copy-start.74
  708.5 4.7 copy-start.93
  708.6 4.9 copy-start.50
  708.6 4.9 copy-start.99
  708.6 4.9 copy-start.117
  721.5 371.1 %reduce-scatter.6.cloned.1.call-start = ((), (), s32[]{:S(2)}) async-start(), calls=%async_computation.12 | async-start | bytes 1253376 | tf_op jit(solution)/shard_map/reduce_scatter | solution.py:278
  724.0 510.6 %reduce-scatter.8.cloned.1.call-start = ((), (), s32[]{:S(2)}) async-start(), calls=%async_computation.13 | async-start | bytes 5013504 | tf_op jit(solution)/shard_map/reduce_scatter | solution.py:279
  728.3 648.2 %reduce-scatter.10.cloned.1.call-start = ((), (), s32[]{:S(2)}) async-start(), calls=%async_computation.14 | async-start | bytes 5013504 | tf_op jit(solution)/shard_map/reduce_scatter | solution.py:280
  963.9 414.2 %copy-start.32 = (f32[128,2048]{1,0:T(8,128)S(1)}, f32[128,2048]{1,0:T(8,128)}, u32[]{:S(2)}) copy-start(f32[128,2048]{1,0:T(8,128)} %get-tuple-element.197) | copy-start | bytes 3145732
  965.1 414.1 %copy-start.31 = (f32[2048,128]{1,0:T(8,128)S(1)}, f32[2048,128]{1,0:T(8,128)}, u32[]{:S(2)}) copy-start(f32[2048,128]{1,0:T(8,128)} %get-tuple-element.198) | copy-start | bytes 3145732
  (80 other events, 143.4 us)
Sparse Core Ops, SparseCore 0:
  80.8 105.2 all-gather.4
  228.3 34.6 all-reduce.20
  266.7 63.4 all-gather.6
  333.9 61.0 all-gather.8
  402.4 18.0 all-reduce.24
  423.2 19.6 all-reduce.22
  461.0 20.3 all-reduce.26
  721.6 242.2 all-reduce.28
  970.0 122.6 reduce-scatter.5
  1099.1 135.5 reduce-scatter.7
  1240.4 136.0 reduce-scatter.9
where the time goes:
time: 1400 us; the launch traced here: 1390 us
  waiting for transfers between devices  849 us (61%)
  blocking collectives  318 us (23%)
  matrix products  79.3 us (6%)
  local copies, waits for them, and re-layouts  73.3 us (5%)
  other arithmetic  30.8 us (2%)
  starting transfers between devices  19.3 us (1%)
  between operations  18.5 us (1%)
    reduce_scatter x1, waiting for transfers between devices, per_device(): lax.psum_scatter(grad_up, 'dp', scatter_dimension=0, tiled=True)  142 us
    reduce_scatter x1, waiting for transfers between devices, per_device(): lax.psum_scatter(grad_down, 'dp', scatter_dimension=0, tiled=True)  142 us
    all_gather x1, blocking collectives, per_device(): lax.all_gather(weight_shards[1], 'dp', axis=0, tiled=True)  134 us
    reduce_scatter x1, waiting for transfers between devices, per_device(): lax.psum_scatter(grad_proj, 'dp', scatter_dimension=0, tiled=True)  127 us
    psum x1, waiting for transfers between devices, per_device(): lax.psum((local_hyper[0], local_hyper[1], local_hyper[2], local_hyper[3],...  126 us
    all_to_all x1, waiting for transfers between devices, per_device(): lax.all_to_all(kernel_grad, 'dp', split_axis=1, concat_axis=0, tiled=True)  105 us
    psum x1, blocking collectives, per_device(): lax.psum((local_hyper[0], local_hyper[1], local_hyper[2], local_hyper[3],...  79.3 us
    all_gather x1, waiting for transfers between devices, per_device(): lax.all_gather(weight_shards[2], 'dp', axis=0, tiled=True)  63.8 us
  transfers between devices with their start and end apart: 16, of which 12 were waited for; matrix products, arithmetic and copies ran while one was open for 5% of the time, Pallas kernels for 0%

commit v1 on v0

v1 whole, which is shorter than its diff:
```python
from functools import partial
import math

import jax
import jax.numpy as jnp
from jax import lax
from jax.experimental import pallas as pl
from jax.experimental.pallas import tpu as pltpu
from jax.sharding import PartitionSpec as P

HEAD_DIM = 64
HYP_HEADS = 4
MESH = pl.DeviceIdType.MESH
ANY = pl.BlockSpec(memory_space=pl.ANY)
VMEM = pl.BlockSpec(memory_space=pltpu.VMEM)
BIG_VMEM = 56 * 1024 * 1024

vit_epsilon = 1e-06
hyper_epsilon = 1e-05


def factors_of(n):
    return {16: (4, 2, 2), 128: (4, 8, 4)}.get(n, (n,))


def coords(me, grid):
    out = []
    for size in reversed(grid):
        out.append(lax.rem(me, size))
        me = me // size
    return out[::-1]


def device_at(position, grid, offset):
    index = 0
    for place, size, step in zip(position, grid, offset):
        index = index * size + (lax.rem(place + step, size) if step else place)
    return index


def offsets_in(grid, dims):
    out = [()]
    for dim, size in enumerate(grid):
        out = [o + (i,) for o in out for i in range(size if dim in dims else 1)]
    return out


def along(grid, dim, step):
    return tuple(step if d == dim else 0 for d in range(len(grid)))


def minus(a, b, grid):
    return tuple((i - j) % size for i, j, size in zip(a, b, grid))


def orders_of(grid):
    return [(0, 1, 2), (0, 2, 1)] if len(grid) == 3 else [tuple(range(len(grid)))]


def greet_all(n, me, mp, partner):
    sem = pltpu.get_barrier_semaphore()
    for k in range(1, n):
        pl.semaphore_signal(sem, inc=1, device_id=(lax.rem(me + k, n), mp), device_id_type=MESH)
    if partner:
        pl.semaphore_signal(sem, inc=1, device_id=(me, 1 - mp), device_id_type=MESH)
    pl.semaphore_wait(sem, n if partner else n - 1)


def remote(src, dst, send, recv, device):
    copy = pltpu.make_async_remote_copy(
        src_ref=src, dst_ref=dst, send_sem=send, recv_sem=recv, device_id=device, device_id_type=MESH
    )
    copy.start()
    return copy


def params(collective, limit=None):
    return pltpu.CompilerParams(collective_id=collective, has_side_effects=True, vmem_limit_bytes=limit)


def share_kernel(n, x_ref, o_ref, local, send, recv):
    me, mp = lax.axis_index("dp"), lax.axis_index("mp")
    greet_all(n, me, mp, False)
    own = pltpu.make_async_copy(x_ref, o_ref.at[me], local)
    own.start()
    copies = []
    for k in range(1, n):
        there = (lax.rem(me + k, n), mp)
        copies.append(remote(x_ref, o_ref.at[me], send.at[k - 1], recv.at[k - 1], there))
    own.wait()
    for copy in copies:
        copy.wait()


def share(x, n):
    return pl.pallas_call(
        partial(share_kernel, n),
        out_shape=jax.ShapeDtypeStruct((n,) + x.shape, x.dtype),
        in_specs=[VMEM],
        out_specs=VMEM,
        scratch_shapes=[
            pltpu.SemaphoreType.DMA,
            pltpu.SemaphoreType.DMA((n - 1,)),
            pltpu.SemaphoreType.DMA((n - 1,)),
        ],
        compiler_params=params(0),
        name="share",
    )(x)


def fetch_kernel(n, grid, direct, kern, attn, mlp, kern_o, attn_o, mlp_o, local, a_send, a_recv, g_send, g_recv):
    me, mp = lax.axis_index("dp"), lax.axis_index("mp")
    here = coords(me, grid)
    greet_all(n, me, mp, False)
    bands, rows = kern.shape[0] // n, kern.shape[1]
    orders = orders_of(grid)
    everyone = offsets_in(grid, range(len(grid)))
    index = {o: i for i, o in enumerate(everyone)}

    def kern_slot():
        if direct:
            return kern_o.at[:, pl.ds(pl.multiple_of(rows * me, 16), rows)]
        return kern_o.at[me]

    own = [
        pltpu.make_async_copy(kern.at[pl.ds(bands * me, bands)], kern_slot(), local.at[0]),
        pltpu.make_async_copy(attn, attn_o.at[me], local.at[1]),
        pltpu.make_async_copy(mlp, mlp_o.at[me], local.at[2]),
    ]
    pieces = []
    for src, dst in ((attn, attn_o), (mlp, mlp_o)):
        width = src.shape[1] // len(orders)
        for half, order in enumerate(orders):
            pieces.append((src, dst, pl.ds(half * width, width), order, len(pieces)))
    sends, count, seen = [], [0] * len(pieces), set()

    def send(piece, shard, step):
        src, dst, lanes, _, p = piece
        owner = device_at(here, grid, shard)
        there = device_at(here, grid, step)
        held = dst.at[owner, :, lanes] if any(shard) else src.at[:, lanes]
        slot = index[minus(shard, step, grid)]
        sends.append(
            remote(held, dst.at[owner, :, lanes], g_send.at[p, count[p]], g_recv.at[p, slot], (there, mp))
        )
        count[p] += 1

    def arrive(piece, shard):
        _, dst, lanes, _, p = piece
        if any(shard) and (p, shard) not in seen:
            seen.add((p, shard))
            block = dst.at[device_at(here, grid, shard), :, lanes]
            pltpu.make_async_copy(block, block, g_recv.at[p, index[shard]]).wait()

    def stage(number, piece):
        order = piece[3]
        for shard in sorted(offsets_in(grid, order[:number]), key=sum):
            arrive(piece, shard)
            for k in range(1, grid[order[number]]):
                send(piece, shard, along(grid, order[number], k))

    for piece in pieces:
        stage(0, piece)
    exchange = []
    for i, step in enumerate(sorted(everyone[1:], key=sum, reverse=True)):
        there = device_at(here, grid, step)
        exchange.append(
            remote(kern.at[pl.ds(bands * there, bands)], kern_slot(), a_send.at[i], a_recv.at[i], (there, mp))
        )
    for copy in own:
        copy.start()
    for number in range(1, len(grid)):
        for piece in pieces:
            stage(number, piece)
    for piece in pieces:
        for shard in everyone:
            arrive(piece, shard)
    for copy in sends:
        copy.wait_send()
    for copy in exchange:
        copy.wait()
    for copy in own:
        copy.wait()


def fetch(kern, attn, mlp, n):
    grid = factors_of(n)
    bands, (_, rows, pixels) = kern.shape[0] // n, kern.shape
    direct = rows % 16 == 0
    pieces = 2 * len(orders_of(grid))
    kern_shape = (bands, rows * n, pixels) if direct else (n, bands, rows, pixels)
    kernel, attn_all, mlp_all = pl.pallas_call(
        partial(fetch_kernel, n, grid, direct),
        out_shape=[
            jax.ShapeDtypeStruct(kern_shape, kern.dtype),
            jax.ShapeDtypeStruct((n,) + attn.shape, attn.dtype),
            jax.ShapeDtypeStruct((n,) + mlp.shape, mlp.dtype),
        ],
        in_specs=[ANY] * 3,
        out_specs=[ANY] * 3,
        scratch_shapes=[
            pltpu.SemaphoreType.DMA((3,)),
            pltpu.SemaphoreType.DMA((n - 1,)),
            pltpu.SemaphoreType.DMA((n - 1,)),
            pltpu.SemaphoreType.DMA((pieces, n - 1)),
            pltpu.SemaphoreType.DMA((pieces, n)),
        ],
        compiler_params=params(1),
        name="fetch",
    )(kern, attn, mlp)
    if not direct:
        kernel = kernel.transpose(1, 0, 2, 3).reshape(bands, rows * n, pixels)
    return kernel, attn_all.reshape(n * rows, -1), mlp_all.reshape(n * rows, -1)


def reduce_kernel(
    n, grid, direct, kern, attn, mlp, kern_o, attn_o, mlp_o,
    attn_sum, mlp_sum, attn_in, mlp_in, local, a_send, a_recv, f_send, f_recv, g_send, g_recv,
):
    me, mp = lax.axis_index("dp"), lax.axis_index("mp")
    here = coords(me, grid)
    greet_all(n, me, mp, True)
    rows, pixels = kern_o.shape[2], kern.shape[-1]
    depth = len(grid)
    orders = [order[::-1] for order in orders_of(grid)]
    everyone = offsets_in(grid, range(depth))
    half_lanes = pl.ds(pl.multiple_of(mp * pixels, pixels), pixels)

    def block_for(there):
        if direct:
            return kern.at[:, pl.ds(pl.multiple_of(rows * there, 16), rows)]
        return kern.at[there]

    pieces = []
    for src, acc, inbox, out in ((attn, attn_sum, attn_in, attn_o), (mlp, mlp_sum, mlp_in, mlp_o)):
        width = src.shape[2] // len(orders)
        for half, order in enumerate(orders):
            pieces.append((src, acc, inbox, out, pl.ds(half * width, width), order, len(pieces)))
    slots = {}
    for which, order in enumerate(orders):
        number = 0
        for t in range(depth):
            rest = sorted(offsets_in(grid, order[t + 1 :]), key=sum, reverse=True)
            for shard in rest:
                for k in range(1, grid[order[t]]):
                    slots[which, t, shard, k] = number
                    number += 1
    sends = []

    def send_stage(t, piece):
        src, acc, inbox, _, lanes, order, p = piece
        held = src if t == 0 else acc
        for shard in sorted(offsets_in(grid, order[t + 1 :]), key=sum, reverse=True):
            for k in range(1, grid[order[t]]):
                step = along(grid, order[t], k)
                target = tuple(i + j for i, j in zip(shard, step))
                owner = device_at(here, grid, target)
                slot = slots[p % len(orders), t, shard, grid[order[t]] - k]
                sends.append(
                    remote(
                        held.at[owner, :, lanes], inbox.at[slot, :, lanes],
                        g_send.at[p, slot], g_recv.at[p, slot], (device_at(here, grid, step), mp),
                    )
                )

    def add_stage(t, piece):
        src, acc, inbox, out, lanes, order, p = piece
        held = src if t == 0 else acc
        for shard in sorted(offsets_in(grid, order[t + 1 :]), key=sum, reverse=True):
            owner = device_at(here, grid, shard)
            total = held[owner, :, lanes].astype(jnp.float32)
            for k in range(1, grid[order[t]]):
                slot = slots[p % len(orders), t, shard, k]
                block = inbox.at[slot, :, lanes]
                pltpu.make_async_copy(block, block, g_recv.at[p, slot]).wait()
                total = total + inbox[slot, :, lanes].astype(jnp.float32)
            if t == depth - 1:
                out[:, lanes] = total
            else:
                acc[owner, :, lanes] = total.astype(acc.dtype)

    for piece in pieces:
        send_stage(0, piece)
    exchange = []
    far = sorted(everyone[1:], key=sum, reverse=True)
    for i, step in enumerate(far):
        there = device_at(here, grid, step)
        exchange.append(
            remote(
                block_for(there), kern_o.at[me, :, :, half_lanes], a_send.at[i], a_recv.at[i], (there, mp)
            )
        )
    own = pltpu.make_async_copy(block_for(me), kern_o.at[me, :, :, half_lanes], local)
    own.start()
    forwards = [
        remote(block_for(me), kern_o.at[me, :, :, half_lanes], f_send.at[n - 1], f_recv.at[n - 1], (me, 1 - mp))
    ]
    for t in range(depth):
        for piece in pieces:
            add_stage(t, piece)
            if t + 1 < depth:
                send_stage(t + 1, piece)
    for i in reversed(range(n - 1)):
        source = device_at(here, grid, minus((0,) * depth, far[i], grid))
        block = kern_o.at[source, :, :, half_lanes]
        exchange[i].wait_recv()
        forwards.append(remote(block, block, f_send.at[i], f_recv.at[i], (me, 1 - mp)))
    for copy in exchange:
        copy.wait_send()
    for copy in forwards:
        copy.wait()
    for copy in sends:
        copy.wait_send()
    own.wait()


def reduce(kern, attn, mlp, n, rows):
    grid = factors_of(n)
    bands, _, pixels = kern.shape
    direct = rows % 16 == 0
    if not direct:
        kern = kern.reshape(bands, n, rows, pixels).transpose(1, 0, 2, 3)
    pieces = 2 * len(orders_of(grid))
    return pl.pallas_call(
        partial(reduce_kernel, n, grid, direct),
        out_shape=[
            jax.ShapeDtypeStruct((n, bands, rows, 2 * pixels), kern.dtype),
            jax.ShapeDtypeStruct(attn.shape[1:], jnp.float32),
            jax.ShapeDtypeStruct(mlp.shape[1:], jnp.float32),
        ],
        in_specs=[ANY, VMEM, VMEM],
        out_specs=[ANY, VMEM, VMEM],
        scratch_shapes=[
            pltpu.VMEM(attn.shape, attn.dtype),
            pltpu.VMEM(mlp.shape, mlp.dtype),
            pltpu.VMEM((n - 1,) + attn.shape[1:], attn.dtype),
            pltpu.VMEM((n - 1,) + mlp.shape[1:], mlp.dtype),
            pltpu.SemaphoreType.DMA,
            pltpu.SemaphoreType.DMA((n - 1,)),
            pltpu.SemaphoreType.DMA((n - 1,)),
            pltpu.SemaphoreType.DMA((n,)),
            pltpu.SemaphoreType.DMA((n,)),
            pltpu.SemaphoreType.DMA((pieces, n - 1)),
            pltpu.SemaphoreType.DMA((pieces, n - 1)),
        ],
        compiler_params=params(2, BIG_VMEM),
        name="reduce",
    )(kern, attn, mlp)


def pair_kernel(steps, x_ref, o_ref, inbox, send, recv):
    me, mp = lax.axis_index("dp"), lax.axis_index("mp")
    there = (me, 1 - mp)
    sem = pltpu.get_barrier_semaphore()
    pl.semaphore_signal(sem, inc=1, device_id=there, device_id_type=MESH)
    pl.semaphore_wait(sem, 1)
    rows = x_ref.shape[0] // steps
    copies = []
    for i in range(steps):
        part = pl.ds(i * rows, rows)
        copies.append(remote(x_ref.at[part], inbox.at[part], send.at[i], recv.at[i], there))
    for i, copy in enumerate(copies):
        part = pl.ds(i * rows, rows)
        copy.wait_recv()
        total = x_ref[part].astype(jnp.float32) + inbox[part].astype(jnp.float32)
        o_ref[part] = total.astype(o_ref.dtype)
    for copy in copies:
        copy.wait_send()


def pair_sum(x):
    steps = 4
    return pl.pallas_call(
        partial(pair_kernel, steps),
        out_shape=jax.ShapeDtypeStruct(x.shape, x.dtype),
        in_specs=[VMEM],
        out_specs=VMEM,
        scratch_shapes=[
            pltpu.VMEM(x.shape, x.dtype),
            pltpu.SemaphoreType.DMA((steps,)),
            pltpu.SemaphoreType.DMA((steps,)),
        ],
        compiler_params=params(3 if x.dtype == jnp.float32 else 5),
        name="pair_sum",
    )(x)


def total_kernel(n, x_ref, o_ref, inbox, send, recv, back_send, back_recv):
    me, mp = lax.axis_index("dp"), lax.axis_index("mp")
    greet_all(n, me, mp, False)
    copies = []
    for k in range(1, n):
        there = lax.rem(me + k, n)
        copies.append(remote(x_ref.at[there], inbox.at[k - 1], send.at[k - 1], recv.at[k - 1], (there, mp)))
    total = x_ref[me]
    for k, copy in enumerate(copies):
        copy.wait_recv()
        total = total + inbox[k]
    o_ref[me] = total
    for k in range(1, n):
        there = lax.rem(me + k, n)
        copies.append(remote(o_ref.at[me], o_ref.at[me], back_send.at[k - 1], back_recv.at[k - 1], (there, mp)))
    for copy in copies[: n - 1]:
        copy.wait_send()
    for copy in copies[n - 1 :]:
        copy.wait()


def total_over_slots(x, n):
    return pl.pallas_call(
        partial(total_kernel, n),
        out_shape=jax.ShapeDtypeStruct(x.shape, x.dtype),
        in_specs=[VMEM],
        out_specs=VMEM,
        scratch_shapes=[pltpu.VMEM((n - 1,) + x.shape[1:], x.dtype)] + [pltpu.SemaphoreType.DMA((n - 1,))] * 4,
        compiler_params=params(4),
        name="total",
    )(x)


def exact_einsum(pattern, left_side, right_side):
    return jnp.einsum(
        pattern,
        left_side,
        right_side,
        precision=lax.Precision.HIGHEST,
        preferred_element_type=jnp.float32,
    )


def fast_einsum(pattern, left_side, right_side):
    return jnp.einsum(pattern, left_side, right_side, preferred_element_type=jnp.float32)


def norm_rows(values, gain_row, shift_row, epsilon):
    center = values - jnp.mean(values, axis=-1, keepdims=True)
    spread = jnp.mean(center * center, axis=-1, keepdims=True)
    return center * lax.rsqrt(spread + epsilon) * gain_row + shift_row


def exact_gelu(values):
    return jax.nn.gelu(values, approximate=False)


def wave_embedding(wavelengths, model_width):
    half_width = model_width // 2
    frequency = 10000.0 ** (-jnp.arange(half_width, dtype=jnp.float32) * 2.0 / model_width)
    angles = wavelengths.astype(jnp.float32)[..., None] * frequency
    return jnp.concatenate([jnp.sin(angles), jnp.cos(angles)], axis=-1)


def hyper_all(
    embedding, band_valid, hyp_attn, hyp_mlp_in, hyp_mlp_out, hyp_gain, hyp_shift, bias_token, bias_w
):
    slots, bands, width = embedding.shape
    length, head_size = bands + 1, width // HYP_HEADS
    sequence = jnp.concatenate([embedding, jnp.broadcast_to(bias_token, (slots, 1, width))], axis=1)
    keys_valid = jnp.concatenate([band_valid, jnp.ones((slots, 1), dtype=bool)], axis=1)
    heads = (slots, length, HYP_HEADS, head_size)
    query_rows = exact_einsum("ste,ef->stf", sequence, hyp_attn[0]).reshape(heads)
    key_rows = exact_einsum("ste,ef->stf", sequence, hyp_attn[1]).reshape(heads)
    value_rows = exact_einsum("ste,ef->stf", sequence, hyp_attn[2]).reshape(heads)
    scores = exact_einsum("sqhd,skhd->shqk", query_rows, key_rows) * (1.0 / math.sqrt(head_size))
    scores = jnp.where(keys_valid[:, None, None, :], scores, -1e30)
    weights = jax.nn.softmax(scores, axis=-1)
    mixed_rows = exact_einsum("shqk,skhd->sqhd", weights, value_rows).reshape(slots, length, width)
    first_rows = norm_rows(
        sequence + exact_einsum("ste,ef->stf", mixed_rows, hyp_attn[3]),
        hyp_gain[0],
        hyp_shift[0],
        hyper_epsilon,
    )
    inner_rows = exact_gelu(exact_einsum("ste,ef->stf", first_rows, hyp_mlp_in))
    second_rows = norm_rows(
        first_rows + exact_einsum("stf,fe->ste", inner_rows, hyp_mlp_out),
        hyp_gain[1],
        hyp_shift[1],
        hyper_epsilon,
    )
    return second_rows[:, :-1] + embedding, exact_einsum("se,ec->sc", second_rows[:, -1], bias_w)


def per_device(
    n,
    pixels,
    band_count,
    wavelengths,
    size_class,
    token_keep,
    hyp_attn,
    hyp_mlp_in,
    hyp_mlp_out,
    hyp_gain,
    hyp_shift,
    bias_token,
    kern_weight,
    kern_bias,
    patch_bias_weight,
    norm_gain,
    norm_shift,
    attn_in,
    attn_in_bias,
    attn_out,
    attn_out_bias,
    mlp_in,
    mlp_in_bias,
    mlp_out,
    mlp_out_bias,
    cotangent,
):
    me, mp = lax.axis_index("dp"), lax.axis_index("mp")
    slot_count, band_total, tokens, pix_size = pixels.shape
    model_width = norm_gain.shape[1]
    hyper_width, rows, _ = kern_weight.shape
    half = pix_size // 2
    low = jnp.bfloat16

    facts = jnp.concatenate([wavelengths[0], band_count])
    facts = jnp.broadcast_to(jnp.pad(facts, (0, 128 - band_total - 1)), (8, 128))
    facts = share(facts, n)[:, 0]
    embedding = wave_embedding(facts[:, :band_total], hyper_width)
    every_band = jnp.arange(band_total)[None, :] < facts[:, band_total][:, None]
    (code_vals, patch_bias), hyper_back = jax.vjp(
        partial(hyper_all, embedding, every_band),
        hyp_attn,
        hyp_mlp_in,
        hyp_mlp_out,
        hyp_gain,
        hyp_shift,
        bias_token,
        patch_bias_weight,
    )
    all_codes = code_vals.astype(low).reshape(n * band_total, hyper_width)
    patch_bias = lax.dynamic_slice_in_dim(patch_bias, me, 1, 0)

    kern_low = kern_weight.astype(low)
    half_weight = lax.dynamic_slice_in_dim(kern_low, mp * half, half, 2)
    half_bias = lax.dynamic_slice_in_dim(kern_bias, mp * half, half, 1)
    half_kernels = (fast_einsum("ne,ecp->ncp", all_codes, half_weight) + half_bias).astype(low)

    inner = attn_in.shape[2]
    units = mlp_in.shape[1]
    attn_shard = jnp.concatenate([attn_in[0], attn_in[1], attn_in[2], attn_out], axis=1).astype(low)
    mlp_shard = jnp.concatenate([mlp_in, mlp_out], axis=1).astype(low)
    kernel, attn_all, mlp_all = fetch(half_kernels, attn_shard, mlp_shard, n)
    weight_qkv, weight_out = attn_all[:, : 3 * inner], attn_all[:, 3 * inner :]
    weight_up, weight_down = mlp_all[:, :units], mlp_all[:, units:]

    band_valid = jnp.arange(band_total) < band_count[0]
    live_rows = jnp.where(
        size_class[0] == 0, tokens * 49 // 256, jnp.where(size_class[0] == 1, tokens * 196 // 256, tokens)
    )
    position = jnp.arange(tokens)
    row_valid = position < live_rows
    key_valid = row_valid & ((token_keep[0] == 1) | (position == 0))
    row_scale = row_valid.astype(jnp.float32)[:, None]
    half_pixels = lax.dynamic_slice_in_dim(pixels[0], mp * half, half, 2)
    masked_pixels = half_pixels * band_valid.astype(low)[:, None, None]

    embedded = pair_sum(fast_einsum("btp,bcp->tc", masked_pixels, kernel)) + patch_bias

    local_heads = inner // HEAD_DIM
    head_grid = (tokens, local_heads, HEAD_DIM)
    score_scale = 1.0 / math.sqrt(HEAD_DIM)
    key_open = key_valid[None, None, :]
    norm_one = partial(norm_rows, epsilon=vit_epsilon)
    normed_a, first_back = jax.vjp(norm_one, embedded, norm_gain[0], norm_shift[0])
    normed_a = normed_a.astype(low)
    input_bias = jnp.concatenate([attn_in_bias[0], jnp.zeros_like(attn_in_bias[0]), attn_in_bias[1]])
    projected = (fast_einsum("nd,de->ne", normed_a, weight_qkv) + input_bias).astype(low)
    query_rows = projected[:, :inner].reshape(head_grid)
    key_rows = projected[:, inner : 2 * inner].reshape(head_grid)
    value_rows = projected[:, 2 * inner :].reshape(head_grid)
    scores = jnp.where(key_open, fast_einsum("qhd,khd->hqk", query_rows, key_rows) * score_scale, -1e30)
    row_peak = jnp.max(scores, axis=-1, keepdims=True)
    exp_scores = jnp.exp(scores - row_peak)
    prob_full = exp_scores / jnp.sum(exp_scores, axis=-1, keepdims=True)
    prob_low = prob_full.astype(low)
    context = fast_einsum("hqk,khd->qhd", prob_low, value_rows).reshape(tokens, inner).astype(low)
    middle = embedded + pair_sum(fast_einsum("ne,de->nd", context, weight_out)) + attn_out_bias
    normed_b, second_back = jax.vjp(norm_one, middle, norm_gain[1], norm_shift[1])
    normed_b = normed_b.astype(low)
    pre_act = fast_einsum("nd,df->nf", normed_b, weight_up) + mlp_in_bias
    activation, gelu_back = jax.vjp(exact_gelu, pre_act)
    activation = activation.astype(low)
    unit_part = fast_einsum("nf,df->nd", activation, weight_down).astype(low)
    final_rows = (middle + pair_sum(unit_part).astype(jnp.float32) + mlp_out_bias) * row_scale
    layer_out = final_rows.astype(low)[None]

    out_grad = cotangent[0].astype(jnp.float32) * row_scale
    out_grad_low = out_grad.astype(low)
    grad_mlp_out_bias = jnp.sum(out_grad, axis=0)
    grad_down = fast_einsum("nd,nf->df", out_grad_low, activation)
    act_grad = fast_einsum("nd,df->nf", out_grad_low, weight_down).astype(low)
    pre_grad = gelu_back(act_grad.astype(jnp.float32))[0].astype(low)
    grad_mlp_in_bias = jnp.sum(pre_grad, axis=0, dtype=jnp.float32)
    grad_up = fast_einsum("nd,nf->df", normed_b, pre_grad)
    second_part = fast_einsum("nf,df->nd", pre_grad, weight_up)
    middle_in, gain_second, shift_second = second_back(pair_sum(second_part))
    middle_grad = out_grad + middle_in
    attended_grad = middle_grad.astype(low)
    grad_attn_out_bias = jnp.sum(attended_grad, axis=0, dtype=jnp.float32)
    grad_proj = fast_einsum("nd,ne->de", attended_grad, context)
    context_grad = fast_einsum("nd,de->ne", attended_grad, weight_out).astype(low).reshape(head_grid)
    prob_grad = fast_einsum("qhd,khd->hqk", context_grad, value_rows)
    row_inner = jnp.sum(prob_full * prob_grad, axis=-1, keepdims=True)
    score_grad = (prob_full * (prob_grad - row_inner)).astype(low)
    query_grad = fast_einsum("hqk,khd->qhd", score_grad, key_rows) * score_scale
    key_grad = fast_einsum("hqk,qhd->khd", score_grad, query_rows) * score_scale
    value_grad = fast_einsum("hqk,qhd->khd", prob_low, context_grad)
    qkv_grad = jnp.concatenate(
        [g.reshape(tokens, inner).astype(low) for g in (query_grad, key_grad, value_grad)], axis=1
    )
    bias_sums = jnp.sum(qkv_grad, axis=0, dtype=jnp.float32)
    grad_in = fast_einsum("nd,ne->de", normed_a, qkv_grad)
    first_part = fast_einsum("ne,de->nd", qkv_grad, weight_qkv)
    embed_in, gain_first, shift_first = first_back(pair_sum(first_part))
    embed_grad = (middle_grad + embed_in).astype(low)
    patch_bias_grad = jnp.sum(embed_grad, axis=0, dtype=jnp.float32)

    half_grad = fast_einsum("tc,btp->bcp", embed_grad, masked_pixels).astype(low)
    attn_grads = jnp.concatenate([grad_in.astype(low), grad_proj.astype(low)], axis=1).reshape(n, rows, -1)
    mlp_grads = jnp.concatenate([grad_up.astype(low), grad_down.astype(low)], axis=1).reshape(n, rows, -1)
    local_grad, attn_sum, mlp_sum = reduce(half_grad, attn_grads, mlp_grads, n, rows)
    local_grad = local_grad.reshape(n * band_total, rows, pix_size)
    grad_attn_in = jnp.stack([attn_sum[:, i * inner : (i + 1) * inner] for i in range(3)])
    grad_attn_out = attn_sum[:, 3 * inner :]
    grad_mlp_in, grad_mlp_out = mlp_sum[:, :units], mlp_sum[:, units:]

    code_part = fast_einsum("ncp,ecp->ne", local_grad, kern_low).reshape(n, band_total, hyper_width)

    small = (
        gain_first,
        gain_second,
        shift_first,
        shift_second,
        bias_sums[:inner],
        bias_sums[2 * inner :],
        grad_attn_out_bias,
        grad_mlp_in_bias,
        grad_mlp_out_bias,
    )
    flat = jnp.concatenate([v.reshape(-1) for v in small])
    lanes = 128
    per_slot = -(-flat.size // (n * lanes))
    flat = jnp.pad(flat, (0, n * per_slot * lanes - flat.size)).reshape(n, per_slot, lanes)
    patch_rows = patch_bias_grad.reshape(1, -1, lanes) * (jnp.arange(n) == me).astype(jnp.float32)[:, None, None]
    packed = jnp.concatenate([code_part, patch_rows, flat], axis=1)
    used = packed.shape[1]
    packed = jnp.pad(packed, ((0, 0), (0, -used % 8), (0, 0)))
    packed = total_over_slots(packed, n)
    code_grad = packed[:, :band_total]
    patch_grad = packed[:, band_total : band_total + model_width // lanes].reshape(n, model_width)
    flat = packed[:, used - per_slot : used].reshape(-1)
    split = []
    start = 0
    for v in small:
        split.append(flat[start : start + v.size])
        start += v.size
    hyper_grads = hyper_back((code_grad, patch_grad))

    pixel_half = fast_einsum("tc,bcp->btp", embed_grad, kernel) * band_valid.astype(jnp.float32)[:, None, None]
    pixel_grad = lax.all_gather(pixel_half.astype(low), "mp", axis=2, tiled=True)[None]
    grad_kern_weight = fast_einsum("ne,ncp->ecp", all_codes, local_grad)
    grad_kern_bias = jnp.sum(local_grad, axis=0, dtype=jnp.float32)
    return (
        layer_out,
        pixel_grad,
        hyper_grads[0],
        hyper_grads[1],
        hyper_grads[2],
        hyper_grads[3],
        hyper_grads[4],
        hyper_grads[5],
        grad_kern_weight,
        grad_kern_bias,
        hyper_grads[6],
        jnp.stack([split[0], split[1]]),
        jnp.stack([split[2], split[3]]),
        grad_attn_in,
        jnp.stack([split[4], split[5]]),
        grad_attn_out,
        split[6],
        grad_mlp_in,
        split[7],
        grad_mlp_out,
        split[8],
    )


def solution(mesh):
    return jax.shard_map(
        partial(per_device, mesh.shape["dp"]),
        mesh=mesh,
        in_specs=(
            P("dp", None, None, None),
            P("dp"),
            P("dp", None),
            P("dp"),
            P("dp", None),
            P(),
            P(),
            P(),
            P(),
            P(),
            P(),
            P(None, "dp", None),
            P("dp", None),
            P(),
            P(),
            P(),
            P(None, "dp", "mp"),
            P(None, "mp"),
            P("dp", "mp"),
            P(),
            P("dp", "mp"),
            P("mp"),
            P("dp", "mp"),
            P(),
            P("dp", None, None),
        ),
        out_specs=(
            P("dp", None, None),
            P("dp", None, None, None),
            P(),
            P(),
            P(),
            P(),
            P(),
            P(),
            P(None, "dp", None),
            P("dp", None),
            P(),
            P(),
            P(),
            P(None, "dp", "mp"),
            P(None, "mp"),
            P("dp", "mp"),
            P(),
            P("dp", "mp"),
            P("mp"),
            P("dp", "mp"),
            P(),
        ),
        check_vma=False,
    )
```

time: 1400 us -> 518 us (0.37)
  waiting for transfers between devices: 849 us -> 0.02 us
  blocking collectives: 318 us -> 0 us
  Pallas kernels: 0 us -> 295 us
  local copies, waits for them, and re-layouts: 73.3 us -> 47.7 us
  other arithmetic: 30.8 us -> 50.7 us
  starting transfers between devices: 19.3 us -> 0.04 us
  matrix products: 79.3 us -> 97 us
    reduce_scatter x3 -> x0, waiting for transfers between devices: 411 us -> none  [the longest x1 142 us: per_device(): lax.psum_scatter(grad_up, 'dp', scatter_dimension=0, tiled=True)]
    pallas_call x0 -> x9, Pallas kernels: none -> 295 us  [the longest x1 139 us: reduce(): pl.pallas_call(partial(reduce_kernel, n, grid, direct), out_shape=[jax.Sh...]
    psum x5 -> x0, waiting for transfers between devices: 211 us -> none  [the longest x1 126 us: per_device(): lax.psum((local_hyper[0], local_hyper[1], local_hyper[2], local_hyper[3],...]
    all_gather x2 -> x0, blocking collectives: 177 us -> none  [the longest x1 134 us: per_device(): lax.all_gather(weight_shards[1], 'dp', axis=0, tiled=True)]
    all_gather x3 -> x1, waiting for transfers between devices: 122 us -> 0.01 us  [per_device(): lax.all_gather(pixel_half.astype(low), 'mp', axis=2, tiled=True)[None]]
    all_to_all x2 -> x0, waiting for transfers between devices: 105 us -> none  [the longest x1 105 us: per_device(): lax.all_to_all(kernel_grad, 'dp', split_axis=1, concat_axis=0, tiled=True)]
    psum x1 -> x0, blocking collectives: 79.3 us -> none  [per_device(): lax.psum((local_hyper[0], local_hyper[1], local_hyper[2], local_hyper[3],...]
    unnamed x1 -> x0, blocking collectives: 61 us -> none
  transfers between devices with their start and end apart: 16 -> 1, of which waited for: 12 -> 0; matrix products, arithmetic and copies ran while one was open for 5% -> 18% of each run, Pallas kernels for 0% -> 31%
where the time goes in v1:
time: 518 us; the launch traced here: 509 us
  Pallas kernels  295 us (57%)
  matrix products  97 us (19%)
  other arithmetic  50.7 us (10%)
  local copies, waits for them, and re-layouts  47.7 us (9%)
  between operations  18.1 us (3%)
    pallas_call x1, Pallas kernels, reduce(): pl.pallas_call(partial(reduce_kernel, n, grid, direct), out_shape=[jax.Sh...  139 us
    pallas_call x1, Pallas kernels, fetch(): pl.pallas_call(partial(fetch_kernel, n, grid, direct), out_shape=[jax.Sha...  104 us
    dot_general x23, matrix products, fast_einsum(): jnp.einsum(pattern, left_side, right_side, preferred_element_type=jnp.flo...  51.3 us
    dot_general x27, matrix products, exact_einsum(): jnp.einsum(pattern, left_side, right_side, precision=lax.Precision.HIGHES...  43.4 us
    unnamed x307, local copies, waits for them, and re-layouts  26.8 us
    pallas_call x5, Pallas kernels, pair_sum(): pl.pallas_call(partial(pair_kernel, steps), out_shape=jax.ShapeDtypeStruc...  21.3 us
    pallas_call x1, Pallas kernels, total_over_slots(): pl.pallas_call(partial(total_kernel, n), out_shape=jax.ShapeDtypeStruct(x...  20.1 us
    pallas_call x1, Pallas kernels, share(): pl.pallas_call(partial(share_kernel, n), out_shape=jax.ShapeDtypeStruct((...  11 us
  transfers between devices with their start and end apart: 1, of which 0 were waited for; matrix products, arithmetic and copies ran while one was open for 18% of the time, Pallas kernels for 31%

profile of v1, /device:TPU:0, one launch (start us, length us, event | category | flops | bytes accessed | tf_op | source)
XLA Modules:
  0.0 508.6 jit_solution(2404993533311340740)
XLA Ops:
  9.3 11.0 %share.1 = s32[16,8,128]{2,1,0:T(8,128)} custom-call(s32[8,128]{1,0:T(8,128)} %broadcast_in_dim.127.x_ref), custom_call_target="tpu_custom_call" | custom-call | tf_op jit(solution)/shard_map/share/pallas_call | solution.py:96
  21.4 1.6 fusion.143
  32.0 2.5 fusion.60
  34.6 4.1 fusion.19
  38.8 1.7 fusion.53
  42.6 7.9 %copy.249 = bf16[128,48,256]{2,0,1:T(8,128)(2,1)} copy(f32[128,48,256]{2,1,0:T(8,128)} %param.36) | data formatting | bytes 9437184 | tf_op args[11]
  51.2 2.2 fusion.34
  53.4 3.1 fusion.5.kern
  58.0 103.9 %fetch.1 = (bf16[13,768,128]{2,1,0:T(8,128)(2,1)}, bf16[16,48,1536]{2,1,0:T(8,128)(2,1)}, bf16[16,48,3072]{2,1,0:T(8,128)(2,1)}) custom-call(bf16[208,48,128]{2,1,0:T(8,128)(2,1)} %fusion.5.kern, bf16[48,1536]{1,0:T(8,128)(2,1)} %pad_maximum_fusion.5.attn, bf16[48,3072]{1,0:T(8,128)(2,1)} %pad_maximum_fusion.3.mlp), custom_call_target="tpu_custom_call" | custom-call | tf_op jit(solution)/shard_map/fetch/pallas_call | solution.py:192
  161.9 3.5 convolution_bitcast_fusion.2.x_ref
  165.5 4.5 pair_sum.5
  170.3 1.3 add_reduce_fusion
  171.6 1.4 multiply_reduce_fusion.6
  174.2 2.3 fusion.10
  180.5 2.3 fusion.148
  182.9 1.4 convolution_convert_fusion.7
  184.9 2.4 fusion.69.x_ref
  187.3 4.4 pair_sum.6
  191.8 1.3 fusion.138
  194.0 6.9 %multiply_convert_fusion.2 = (bf16[256,1536]{1,0:T(8,128)(2,1)}, f32[256,1536]{1,0:T(8,128)S(1)}, f32[256,1536]{1,0:T(8,128)S(1)}) fusion(f32[1536]{0:T(1024)S(1)} %copy-done.143, bf16[768,3072]{1,0:T(8,128)(2,1)} %bitcast.292, f32[256,768]{1,0:T(8,128)S(1)} %get-tuple-element.109, f32[768]{0:T(1024)S(1)} %copy-done.104, f32[768]{0:T(1024)S(1)} %copy-done.89, ...), kind=kOutput, calls=%fused_computation.62 | convolution fusion | flops 630915072 | bytes 7092224 | tf_op jit(solution)/shard_map/nd,df->nf/dot_general | solution.py:432
  201.0 1.9 convert_reduce_fusion.1
  203.8 1.7 fusion.16.x_ref
  205.5 4.5 pair_sum.8
  210.0 2.1 multiply_reduce_fusion.1
  212.0 1.3 multiply_multiply_fusion.16
  213.3 3.2 fusion.41.x_ref
  216.5 3.6 pair_sum.7
  220.1 2.5 fusion.136
  224.3 2.1 convolution_convert_fusion.6
  226.4 1.7 copy.121
  228.1 1.9 convolution_convert_fusion.5
  233.3 1.6 fusion.36.x_ref
  234.9 4.4 pair_sum.9
  239.4 2.6 multiply_reduce_fusion.2
  245.5 1.8 fusion.40
  248.4 3.8 convert_bitcast_fusion.kern
  256.4 1.7 pad_maximum_fusion.1
  258.1 2.8 pad_maximum_fusion
  260.9 138.6 %reduce.26 = (bf16[16,13,48,256]{3,2,1,0:T(8,128)(2,1)}, f32[48,1536]{1,0:T(8,128)}, f32[48,3072]{1,0:T(8,128)}) custom-call(bf16[13,768,128]{2,1,0:T(8,128)(2,1)} %convert_bitcast_fusion.kern, bf16[16,48,1536]{2,1,0:T(8,128)(2,1)} %bitcast.245, bf16[16,48,3072]{2,1,0:T(8,128)(2,1)} %bitcast.244), custom_call_target="tpu_custom_call" | custom-call | tf_op jit(solution)/shard_map/reduce/pallas_call | solution.py:324
  399.5 5.6 %fusion.47 = f32[16,13,128]{2,0,1:T(8,128)S(1)} fusion(bf16[128,48,256]{2,0,1:T(8,128)(2,1)S(1)} %copy-done.6, bf16[16,13,48,256]{3,2,1,0:T(8,128)(2,1)} %get-tuple-element.30), kind=kOutput, calls=%fused_computation.105 | convolution fusion | flops 654311424 | bytes 8364032 | tf_op jit(solution)/shard_map/ncp,ecp->ne/dot_general | solution.py:432
  406.0 20.1 %total.1 = f32[16,24,128]{2,1,0:T(8,128)} custom-call(f32[16,24,128]{2,1,0:T(8,128)} %select_maximum_fusion.x_ref), custom_call_target="tpu_custom_call" | custom-call | tf_op jit(solution)/shard_map/total/pallas_call | solution.py:410
  428.7 1.7 multiply_reduce_fusion.9
  431.5 4.6 multiply_add_fusion
  436.2 1.6 fusion.55
  439.2 1.3 multiply_reduce_fusion.7
  441.7 1.6 convolution_bitcast_fusion.4
  443.2 1.8 convolution_bitcast_fusion.5
  445.0 1.2 convolution_bitcast_fusion.11
  447.3 1.9 convolution_bitcast_fusion.8
  449.3 1.8 fusion.99
  451.1 1.2 copy.199
  453.2 1.9 convolution_bitcast_fusion.9
  455.2 1.8 fusion.101
  457.0 1.2 copy.198
  459.1 1.9 convolution_bitcast_fusion.10
  462.2 4.7 fusion.7
  469.1 6.3 %copy.155 = f32[128,48,256]{2,1,0:T(8,128)} copy(f32[128,48,256]{2,0,1:T(8,128)S(1)} %fusion.7) | data formatting | bytes 12582912
  479.1 1.5 fusion.115
  481.3 1.6 pad_add_fusion
  483.5 3.4 convolution_bitcast_fusion.1
  486.9 1.3 fusion.109
  488.1 4.2 convert_reduce_fusion
  492.4 4.4 convolution_bitcast_fusion
  497.7 3.6 copy.154
  (432 shorter events, 54.5 us)
Async XLA Ops:
  7.2 24.8 %copy-start = (f32[128,2048]{1,0:T(8,128)S(1)}, f32[128,2048]{1,0:T(8,128)}, u32[]{:S(2)}) copy-start(f32[128,2048]{1,0:T(8,128)} %param.31) | copy-start | bytes 3145732
  7.2 490.5 %all-gather.2.cloned.1.call-start = ((), (), s32[]{:S(2)}) async-start(), calls=%async_computation | async-start | bytes 2555904 | tf_op jit(solution)/shard_map/all_gather | solution.py:663
  24.5 5.3 %copy-start.16 = (f32[16,14,128]{2,1,0:T(8,128)}, f32[16,14,128]{2,1,0:T(8,128)S(1)}, u32[]{:S(2)}) copy-start(f32[16,14,128]{2,1,0:T(8,128)S(1)} %pad_maximum_fusion.6) | copy-start | bytes 344068
  29.8 4.7 copy-start.48
  31.3 9.1 %copy-start.65 = (f32[16,14]{1,0:T(8,128)}, f32[16,14]{1,0:T(8,128)S(1)}, u32[]{:S(2)}) copy-start(f32[16,14]{1,0:T(8,128)S(1)} %fusion.116) | copy-start | bytes 2692
  31.4 9.1 %copy-start.102 = (f32[128]{0:T(128)}, f32[128]{0:T(128)S(1)}, u32[]{:S(2)}) copy-start(f32[128]{0:T(128)S(1)} %get-tuple-element.160) | copy-start | bytes 1540
  31.4 9.6 %copy-start.117 = (f32[128]{0:T(128)}, f32[128]{0:T(128)S(1)}, u32[]{:S(2)}) copy-start(f32[128]{0:T(128)S(1)} %get-tuple-element.161) | copy-start | bytes 1540
  41.8 8.7 %copy-start.45 = (bf16[16,13,128]{2,1,0:T(8,128)(2,1)}, bf16[16,13,128]{2,1,0:T(8,128)(2,1)S(1)}, u32[]{:S(2)}) copy-start(bf16[16,13,128]{2,1,0:T(8,128)(2,1)S(1)} %fusion.83) | copy-start | bytes 159748
  42.5 8.0 %copy-start.88 = (f32[48,384]{1,0:T(8,128)S(1)}, f32[48,384]{1,0:T(8,128)}, u32[]{:S(2)}) copy-start(f32[48,384]{1,0:T(8,128)} %param.43) | copy-start | bytes 221188
  42.5 8.0 %copy-start.64 = (f32[3,48,384]{2,1,0:T(8,128)S(1)}, f32[3,48,384]{2,1,0:T(8,128)}, u32[]{:S(2)}) copy-start(f32[3,48,384]{2,1,0:T(8,128)} %param.41) | copy-start | bytes 663556
  42.5 8.0 %copy-start.60 = (f32[48,1536]{1,0:T(8,128)S(1)}, f32[48,1536]{1,0:T(8,128)}, u32[]{:S(2)}) copy-start(f32[48,1536]{1,0:T(8,128)} %param.47) | copy-start | bytes 884740
  42.5 8.1 %copy-start.61 = (f32[48,1536]{1,0:T(8,128)S(1)}, f32[48,1536]{1,0:T(8,128)}, u32[]{:S(2)}) copy-start(f32[48,1536]{1,0:T(8,128)} %param.45) | copy-start | bytes 884740
  42.5 8.1 %copy-start.136 = (f32[2,384]{1,0:T(2,128)S(1)}, f32[2,384]{1,0:T(2,128)}, u32[]{:S(2)}) copy-start(f32[2,384]{1,0:T(2,128)} %param.42) | copy-start | bytes 9220
  42.6 8.7 %copy-start.119 = (f32[48,256]{1,0:T(8,128)S(1)}, f32[48,256]{1,0:T(8,128)}, u32[]{:S(2)}) copy-start(f32[48,256]{1,0:T(8,128)} %param.37) | copy-start | bytes 147460
  51.2 110.7 %copy-start.141 = (bf16[13]{0:T(256)(128)(2,1)}, bf16[13]{0:T(256)(128)(2,1)S(1)}, u32[]{:S(2)}) copy-start(bf16[13]{0:T(256)(128)(2,1)S(1)} %get-tuple-element.159) | copy-start | bytes 82
  56.6 105.3 %copy-start.55 = (bf16[1,13,256,256]{3,2,1,0:T(8,128)(2,1)S(1)}, bf16[1,13,256,256]{3,2,1,0:T(8,128)(2,1)}, u32[]{:S(2)}) copy-start(bf16[1,13,256,256]{3,2,1,0:T(8,128)(2,1)} %param.25) | copy-start | bytes 5111812
  161.9 8.0 %copy-start.82 = (f32[16,1,128]{2,1,0:T(1,128)S(1)}, f32[16,1,128]{2,1,0:T(1,128)}, u32[]{:S(2)}) copy-start(f32[16,1,128]{2,1,0:T(1,128)} %slice.211) | copy-start | bytes 24580
  165.5 4.5 copy-start.25
  165.5 8.1 %copy-start.130 = (f32[2,768]{1,0:T(2,128)S(1)}, f32[2,768]{1,0:T(2,128)}, u32[]{:S(2)}) copy-start(f32[2,768]{1,0:T(2,128)} %param.40) | copy-start | bytes 18436
  165.5 8.1 %copy-start.131 = (f32[2,768]{1,0:T(2,128)S(1)}, f32[2,768]{1,0:T(2,128)}, u32[]{:S(2)}) copy-start(f32[2,768]{1,0:T(2,128)} %param.39) | copy-start | bytes 18436
  169.9 4.3 copy-start.1
  170.3 6.2 %copy-start.72 = (f32[768]{0:T(1024)}, f32[768]{0:T(1024)S(1)}, u32[]{:S(2)}) copy-start(f32[768]{0:T(1024)S(1)} %dynamic-slice_reduce_fusion) | copy-start | bytes 9220
  171.6 4.9 copy-start.113
  184.9 6.8 %copy-start.73 = (f32[768]{0:T(1024)S(1)}, f32[768]{0:T(1024)}, u32[]{:S(2)}) copy-start(f32[768]{0:T(1024)} %copy-done.72) | copy-start | bytes 9220
  184.9 6.8 %copy-start.133 = (f32[768]{0:T(1024)S(1)}, f32[768]{0:T(1024)}, u32[]{:S(2)}) copy-start(f32[768]{0:T(1024)} %param.44) | copy-start | bytes 9220
  193.1 7.8 %copy-start.96 = (f32[256]{0:T(256)}, f32[256]{0:T(256)S(1)}, u32[]{:S(2)}) copy-start(f32[256]{0:T(256)S(1)} %broadcast_multiply_fusion.3) | copy-start | bytes 3076
  193.2 7.8 %slice-start = ((s8[4718592]{0:T(1024)(128)(4,1)}), s8[4194304]{0:T(1024)(128)(4,1)S(1)}, s32[]{:S(2)}) async-start(s8[4718592]{0:T(1024)(128)(4,1)} %bitcast.294), calls=%async_computation.1 | async-start | bytes 8388608
  193.4 7.5 %copy-start.115 = (f32[256]{0:T(256)}, f32[256]{0:T(256)S(1)}, u32[]{:S(2)}) copy-start(f32[256]{0:T(256)S(1)} %fusion.125) | copy-start | bytes 3076
  194.0 7.0 %copy-start.12 = (bf16[1,256,768]{2,1,0:T(8,128)(2,1)S(1)}, bf16[1,256,768]{2,1,0:T(8,128)(2,1)}, u32[]{:S(2)}) copy-start(bf16[1,256,768]{2,1,0:T(8,128)(2,1)} %param.49) | copy-start | bytes 1179652
  194.0 7.0 %copy-start.98 = (f32[256]{0:T(256)S(1)}, f32[256]{0:T(256)}, u32[]{:S(2)}) copy-start(f32[256]{0:T(256)} %get-tuple-element.165) | copy-start | bytes 3076
  194.0 7.0 %slice-start.1 = ((s8[4718592]{0:T(1024)(128)(4,1)}), s8[524288]{0:T(1024)(128)(4,1)S(1)}, s32[]{:S(2)}) async-start(s8[4718592]{0:T(1024)(128)(4,1)} %bitcast.294), calls=%async_computation.2 | async-start | bytes 1048576
  205.5 7.8 %copy-start.43 = (bf16[256,1536]{1,0:T(8,128)(2,1)S(1)}, bf16[256,1536]{1,0:T(8,128)(2,1)}, u32[]{:S(2)}) copy-start(bf16[256,1536]{1,0:T(8,128)(2,1)} %get-tuple-element.106) | copy-start | bytes 2359300
  239.3 4.5 copy-start.14
  239.3 4.5 copy-start.100
  239.3 4.5 copy-start.121
  248.3 4.3 copy-start.42
  248.3 4.3 copy-start.71
  248.3 4.3 copy-start.74
  248.3 4.3 copy-start.94
  248.3 4.3 copy-start.114
  248.4 4.3 copy-start.125
  248.4 4.3 copy-start.135
  260.9 138.6 %copy-start.6 = (bf16[128,48,256]{2,0,1:T(8,128)(2,1)S(1)}, bf16[128,48,256]{2,0,1:T(8,128)(2,1)}, u32[]{:S(2)}) copy-start(bf16[128,48,256]{2,0,1:T(8,128)(2,1)} %copy.249) | copy-start | bytes 9437188
  399.5 5.7 %copy-start.106 = (f32[768]{0:T(1024)S(1)}, f32[768]{0:T(1024)}, u32[]{:S(2)}) copy-start(f32[768]{0:T(1024)} %get-tuple-element.98) | copy-start | bytes 9220
  399.5 27.6 %copy-start.26 = (f32[128,768]{1,0:T(8,128)S(1)}, f32[128,768]{1,0:T(8,128)}, u32[]{:S(2)}) copy-start(f32[128,768]{1,0:T(8,128)} %param.38) | copy-start | bytes 1179652
  399.5 28.0 %copy-start.9 = (f32[16,14,128]{2,1,0:T(8,128)S(1)}, f32[16,14,128]{2,1,0:T(8,128)}, u32[]{:S(2)}) copy-start(f32[16,14,128]{2,1,0:T(8,128)} %copy-done.8) | copy-start | bytes 344068
  399.5 28.0 %copy-start.118 = (f32[128]{0:T(128)S(1)}, f32[128]{0:T(128)}, u32[]{:S(2)}) copy-start(f32[128]{0:T(128)} %copy-done.117) | copy-start | bytes 1540
  399.5 28.0 %copy-start.132 = (pred[14]{0:T(512)(128)(4,1)S(1)}, pred[14]{0:T(512)(128)(4,1)}, u32[]{:S(2)}) copy-start(pred[14]{0:T(512)(128)(4,1)} %constant.47.clone.1) | copy-start | bytes 46
  405.2 23.5 %copy-start.87 = (f32[16,14]{1,0:T(8,128)S(1)}, f32[16,14]{1,0:T(8,128)}, u32[]{:S(2)}) copy-start(f32[16,14]{1,0:T(8,128)} %copy-done.86) | copy-start | bytes 2692
  405.2 23.5 %copy-start.78 = (f32[16,14]{1,0:T(8,128)S(1)}, f32[16,14]{1,0:T(8,128)}, u32[]{:S(2)}) copy-start(f32[16,14]{1,0:T(8,128)} %copy-done.77) | copy-start | bytes 2692
  431.5 6.4 %copy-start.52 = (f32[16,14,128]{2,1,0:T(8,128)}, f32[16,14,128]{2,1,0:T(8,128)S(1)}, u32[]{:S(2)}) copy-start(f32[16,14,128]{2,1,0:T(8,128)S(1)} %broadcast_add_fusion.1) | copy-start | bytes 344068
  438.6 6.4 %copy-start.54 = (f32[16,14,128]{2,1,0:T(8,128)}, f32[16,14,128]{2,1,0:T(8,128)S(1)}, u32[]{:S(2)}) copy-start(f32[16,14,128]{2,1,0:T(8,128)S(1)} %broadcast_add_fusion) | copy-start | bytes 344068
  452.3 9.9 %copy-start.46 = (bf16[16,13,128]{2,1,0:T(8,128)(2,1)S(1)}, bf16[16,13,128]{2,1,0:T(8,128)(2,1)}, u32[]{:S(2)}) copy-start(bf16[16,13,128]{2,1,0:T(8,128)(2,1)} %copy-done.45) | copy-start | bytes 159748
  469.1 6.4 %copy-start.62 = (f32[48,1536]{1,0:T(8,128)S(1)}, f32[48,1536]{1,0:T(8,128)}, u32[]{:S(2)}) copy-start(f32[48,1536]{1,0:T(8,128)} %get-tuple-element.31) | copy-start | bytes 884740
  469.1 7.7 %copy-start.138 = (f32[128]{0:T(128)S(1)}, f32[128]{0:T(128)}, u32[]{:S(2)}) copy-start(f32[128]{0:T(128)} %get-tuple-element.84) | copy-start | bytes 1540
  469.1 12.2 %copy-start.91 = (f32[1,128,128]{2,1,0:T(8,128)S(1)}, f32[1,128,128]{2,1,0:T(8,128)}, u32[]{:S(2)}) copy-start(f32[1,128,128]{2,1,0:T(8,128)} %convolution_bitcast_fusion.11) | copy-start | bytes 196612
  469.1 12.2 %copy-start.92 = (f32[1,128,128]{2,1,0:T(8,128)S(1)}, f32[1,128,128]{2,1,0:T(8,128)}, u32[]{:S(2)}) copy-start(f32[1,128,128]{2,1,0:T(8,128)} %convolution_bitcast_fusion.8) | copy-start | bytes 196612
  469.1 13.8 %copy-start.137 = (f32[128]{0:T(128)S(1)}, f32[128]{0:T(128)}, u32[]{:S(2)}) copy-start(f32[128]{0:T(128)} %get-tuple-element.88) | copy-start | bytes 1540
  469.1 14.4 %copy-start.51 = (f32[16,14,128]{2,1,0:T(8,128)S(1)}, f32[16,14,128]{2,1,0:T(8,128)}, u32[]{:S(2)}) copy-start(f32[16,14,128]{2,1,0:T(8,128)} %copy-done.50) | copy-start | bytes 344068
  481.3 5.6 %copy-start.57 = (f32[16,6,128]{2,1,0:T(8,128)S(1)}, f32[16,6,128]{2,1,0:T(8,128)}, u32[]{:S(2)}) copy-start(f32[16,6,128]{2,1,0:T(8,128)} %copy-done.56) | copy-start | bytes 147460
  481.3 5.6 %copy-start.83 = (f32[16,1,128]{2,1,0:T(1,128)S(1)}, f32[16,1,128]{2,1,0:T(1,128)}, u32[]{:S(2)}) copy-start(f32[16,1,128]{2,1,0:T(1,128)} %slice.211) | copy-start | bytes 24580
  488.1 4.3 copy-start.5
  488.1 4.3 copy-start.53
  492.4 4.4 copy-start.47
  (85 other events, 166.6 us)
Sparse Core Ops, SparseCore 0:
  247.5 24.4 all-gather.1

commit v2 on v0

v2 whole, which is shorter than its diff:
```python
from functools import partial
import math

import jax
import jax.numpy as jnp
from jax import lax
from jax.experimental import pallas as pl
from jax.experimental.pallas import tpu as pltpu
from jax.sharding import PartitionSpec as P

HEAD_DIM = 64
HYP_HEADS = 4
MESH = pl.DeviceIdType.MESH
ANY = pl.BlockSpec(memory_space=pl.ANY)
VMEM = pl.BlockSpec(memory_space=pltpu.VMEM)
BIG_VMEM = 58 * 1024 * 1024

vit_epsilon = 1e-06
hyper_epsilon = 1e-05


def factors_of(n):
    return {16: (4, 2, 2), 128: (4, 8, 4)}.get(n, (n,))


def coords(me, grid):
    out = []
    for size in reversed(grid):
        out.append(lax.rem(me, size))
        me = me // size
    return out[::-1]


def device_at(position, grid, offset):
    index = 0
    for place, size, step in zip(position, grid, offset):
        index = index * size + (lax.rem(place + step, size) if step else place)
    return index


def offsets_in(grid, dims):
    out = [()]
    for dim, size in enumerate(grid):
        out = [o + (i,) for o in out for i in range(size if dim in dims else 1)]
    return out


def along(grid, dim, step):
    return tuple(step if d == dim else 0 for d in range(len(grid)))


def minus(a, b, grid):
    return tuple((i - j) % size for i, j, size in zip(a, b, grid))


def orders_of(grid):
    return [(0, 1, 2), (0, 2, 1)] if len(grid) == 3 else [tuple(range(len(grid)))]


def greet(n, me, mp, both):
    sem = pltpu.get_barrier_semaphore()
    for k in range(1, n):
        pl.semaphore_signal(sem, inc=1, device_id=(lax.rem(me + k, n), mp), device_id_type=MESH)
    if both:
        for k in range(n):
            pl.semaphore_signal(sem, inc=1, device_id=(lax.rem(me + k, n), 1 - mp), device_id_type=MESH)
    pl.semaphore_wait(sem, 2 * n - 1 if both else n - 1)


def remote(src, dst, send, recv, device):
    copy = pltpu.make_async_remote_copy(
        src_ref=src, dst_ref=dst, send_sem=send, recv_sem=recv, device_id=device, device_id_type=MESH
    )
    copy.start()
    return copy


def params(collective, limit=None):
    return pltpu.CompilerParams(collective_id=collective, has_side_effects=True, vmem_limit_bytes=limit)


NN, NT, TN = ((1,), (0,)), ((1,), (1,)), ((0,), (0,))
GROUP = 16
SPAN = 16


def dot(a, b, contract):
    return lax.dot_general(a, b, (contract, ((), ())), preferred_element_type=jnp.float32)


def exact(a, b, contract=NN):
    return lax.dot_general(
        a, b, (contract, ((), ())), precision=lax.Precision.HIGHEST, preferred_element_type=jnp.float32
    )


def lanes_at(i, width):
    return pl.ds(pl.multiple_of(i * width, width), width)


def row_mean(x):
    return jnp.mean(x, axis=-1, keepdims=True)


def row_sum(x):
    return jnp.sum(x, axis=-1, keepdims=True)


def all_rows(x):
    return jnp.sum(x, axis=0, keepdims=True)


def column_sums(x):
    return dot(jnp.ones((8, x.shape[0]), x.dtype), x, NN)[:1]


def normal_parts(x):
    return 0.5 + 0.5 * lax.erf(x * math.sqrt(0.5)), jnp.exp(-0.5 * x * x) * (1.0 / math.sqrt(2.0 * math.pi))


def normed(x, epsilon):
    center = x - row_mean(x)
    r = lax.rsqrt(row_mean(center * center) + epsilon)
    return center * r, r


def norm_back(hat, r, d_y, gain_row):
    u = d_y * gain_row
    return r * (u - row_mean(u) - hat * row_mean(u * hat)), all_rows(d_y * hat), all_rows(d_y)


def tiled(rows):
    return -(-rows // 8) * 8


def first_rows(ref, rows):
    return ref if ref.shape[-2] == rows else ref.at[:, pl.ds(0, rows)]


def arrived(block, sem):
    pltpu.make_async_copy(block, block, sem).wait()


SEQ, QUERY, KEY, VALUE, MIXED, HAT_A, FIRST, HAT_B, SECOND, SCALE_A, SCALE_B = range(11)


def head_masks(width):
    lane = lax.broadcasted_iota(jnp.int32, (1, width), 1)
    size = width // HYP_HEADS
    return [((lane >= h * size) & (lane < (h + 1) * size)).astype(jnp.float32) for h in range(HYP_HEADS)]


def generator_forward(facts, g, w_attn, w_in, w_out, gain, shift, rows, wide, prob):
    count, width = GROUP * SPAN, facts.shape[-1]
    block = facts[pl.ds(g * GROUP, GROUP)]
    seq = block[:, :SPAN].reshape(count, width)
    valid = block[:, SPAN:].reshape(count, width)
    columns = dot(jnp.ones((8, width), jnp.bfloat16), valid.astype(jnp.bfloat16), NT)[:1]
    slot = [lax.shift_right_logical(lax.broadcasted_iota(jnp.int32, (count, count), d), 4) for d in range(2)]
    allowed = (slot[0] == slot[1]) & (columns > 0.5)
    rows[SEQ] = seq
    for i in range(3):
        rows[QUERY + i] = exact(seq, w_attn[i])
    scale = 1.0 / math.sqrt(width // HYP_HEADS)
    mixed = jnp.zeros((count, width), jnp.float32)
    for h, mask in enumerate(head_masks(width)):
        scores = jnp.where(allowed, exact(rows[QUERY] * mask, rows[KEY], NT) * scale, -1e30)
        raised = jnp.exp(scores - jnp.max(scores, axis=-1, keepdims=True))
        weights = raised / row_sum(raised)
        prob[h] = weights
        mixed = mixed + exact(weights, rows[VALUE] * mask)
    rows[MIXED] = mixed
    hat, r = normed(seq + exact(mixed, w_attn[3]), hyper_epsilon)
    rows[HAT_A] = hat
    rows[SCALE_A] = jnp.broadcast_to(r, (count, width))
    rows[FIRST] = hat * gain[0:1] + shift[0:1]
    tile = 512

    @pl.loop(0, w_in.shape[1] // tile)
    def _(j):
        cols = lanes_at(j, tile)
        pre = exact(rows[FIRST], w_in[:, cols])
        phi, density = normal_parts(pre)
        wide[0, :, cols] = pre * phi
        wide[1, :, cols] = phi + pre * density

    rows[SECOND] = rows[FIRST]

    @pl.loop(0, w_in.shape[1] // tile)
    def _(j):
        cols = lanes_at(j, tile)
        rows[SECOND] = rows[SECOND] + exact(wide[0, :, cols], w_out[cols])

    hat, r = normed(rows[SECOND], hyper_epsilon)
    rows[HAT_B] = hat
    rows[SCALE_B] = jnp.broadcast_to(r, (count, width))
    rows[SECOND] = hat * gain[1:2] + shift[1:2]


def generator_backward(d_second, put, w_attn, w_in, w_out, gain, rows, wide, prob, d_mlp, outs):
    g_attn, g_in, g_out, g_gain, g_shift, g_token = outs
    width = d_second.shape[1]
    d_sum, gain_b, shift_b = norm_back(rows[HAT_B], rows[SCALE_B], d_second, gain[1:2])
    put(g_gain, slice(1, 2), gain_b)
    put(g_shift, slice(1, 2), shift_b)
    d_mlp[0] = d_sum
    d_mlp[1] = d_sum
    tile = 512

    @pl.loop(0, w_in.shape[1] // tile)
    def _(j):
        cols = lanes_at(j, tile)
        put(g_out, cols, exact(wide[0, :, cols], d_mlp[0], TN))
        d_pre = exact(d_mlp[0], w_out[cols], NT) * wide[1, :, cols]
        put(g_in, (slice(None), cols), exact(rows[FIRST], d_pre, TN))
        d_mlp[1] = d_mlp[1] + exact(d_pre, w_in[:, cols], NT)

    d_res, gain_a, shift_a = norm_back(rows[HAT_A], rows[SCALE_A], d_mlp[1], gain[0:1])
    put(g_gain, slice(0, 1), gain_a)
    put(g_shift, slice(0, 1), shift_a)
    put(g_attn, 3, exact(rows[MIXED], d_res, TN))
    d_mixed = exact(d_res, w_attn[3], NT)
    scale = 1.0 / math.sqrt(width // HYP_HEADS)
    d_q = jnp.zeros_like(d_res)
    d_k, d_v = d_q, d_q
    for h, mask in enumerate(head_masks(width)):
        p, d_m = prob[h], d_mixed * mask
        d_p = exact(d_m, rows[VALUE], NT)
        d_s = p * (d_p - row_sum(p * d_p)) * scale
        d_q = d_q + exact(d_s, rows[KEY] * mask)
        d_k = d_k + exact(d_s, rows[QUERY] * mask, TN)
        d_v = d_v + exact(p, d_m, TN)
    d_seq = d_res
    for i, grad in enumerate((d_q, d_k, d_v)):
        put(g_attn, i, exact(rows[SEQ], grad, TN))
        d_seq = d_seq + exact(grad, w_attn[i], NT)
    d_mlp[0] = d_seq


def generator_scratch(width, units):
    f32, count = jnp.float32, GROUP * SPAN
    return [(11, count, width), (2, count, units), (HYP_HEADS, count, count)], f32


def front_kernel(
    n, grid, direct, bands,
    facts_own, w_attn, w_in, w_out, gain, shift, patch_w, kern_w, kern_b, attn, mlp,
    kern_o, attn_o, mlp_o, facts, patch_o, codes_o, rows_o, wide_o, prob_o,
    second, w_half, b_half, k32, k16, local, f_send, f_recv, a_send, a_recv, g_send, g_recv,
):
    me, mp = lax.axis_index("dp"), lax.axis_index("mp")
    here = coords(me, grid)
    low = jnp.bfloat16
    rows, half = kern_w.shape[1], kern_w.shape[2] // 2
    lanes = lanes_at(mp, half)
    orders = orders_of(grid)
    depth = len(grid)
    everyone = offsets_in(grid, range(depth))
    index = {o: i for i, o in enumerate(everyone)}
    zero = (0,) * depth

    def kern_slot():
        if direct:
            return kern_o.at[:, pl.ds(pl.multiple_of(rows * me, 16), rows)]
        return kern_o.at[me]

    load = pltpu.make_async_copy(kern_w.at[:, :, lanes], first_rows(w_half, rows), local.at[0])
    load.start()
    own = [
        pltpu.make_async_copy(attn, attn_o.at[me], local.at[1]),
        pltpu.make_async_copy(mlp, mlp_o.at[me], local.at[2]),
    ]
    for copy in own:
        copy.start()
    greet(n, me, mp, False)
    shares = []
    for k in range(1, n):
        there = (lax.rem(me + k, n), mp)
        shares.append(remote(facts_own, facts.at[me], f_send.at[k - 1], f_recv.at[k - 1], there))
    facts[me] = facts_own[...]

    pieces = []
    for src, dst in ((attn, attn_o), (mlp, mlp_o)):
        width = src.shape[1] // len(orders)
        for part, order in enumerate(orders):
            pieces.append((src, dst, pl.ds(part * width, width), order, len(pieces)))
    sends, count, seen = [], [0] * len(pieces), set()

    def send(piece, shard, step):
        src, dst, cols, _, p = piece
        owner = device_at(here, grid, shard)
        there = device_at(here, grid, step)
        held = dst.at[owner, :, cols] if any(shard) else src.at[:, cols]
        slot = index[minus(shard, step, grid)]
        sends.append(
            remote(held, dst.at[owner, :, cols], g_send.at[p, count[p]], g_recv.at[p, slot], (there, mp))
        )
        count[p] += 1

    def arrive(piece, shard):
        _, dst, cols, _, p = piece
        if any(shard) and (p, shard) not in seen:
            seen.add((p, shard))
            arrived(dst.at[device_at(here, grid, shard), :, cols], g_recv.at[p, index[shard]])

    def stage(number, piece, own_shard):
        order = piece[3]
        for shard in sorted(offsets_in(grid, order[:number]), key=sum):
            if any(shard) != own_shard:
                arrive(piece, shard)
                for k in range(1, grid[order[number]]):
                    send(piece, shard, along(grid, order[number], k))

    for piece in pieces:
        for number in range(depth):
            stage(number, piece, True)

    for copy in shares:
        copy.wait_recv()
    position = lax.broadcasted_iota(jnp.int32, (GROUP * SPAN, facts.shape[-1]), 0)
    is_band = lax.rem(position, SPAN) < bands
    for g in range(n // GROUP):
        generator_forward(facts, g, w_attn, w_in, w_out, gain, shift, rows_o, wide_o, prob_o)
        group = pl.ds(g * GROUP * SPAN, GROUP * SPAN)
        second[group] = rows_o[SECOND]
        codes_o[group] = jnp.where(is_band, rows_o[SECOND] + rows_o[SEQ], 0.0).astype(low)
    patch_o[...] = exact(second[pl.ds(pl.multiple_of(me * SPAN, SPAN), SPAN)], patch_w[...])

    half_pieces = len(pieces) // 2
    for piece in pieces[:half_pieces]:
        stage(1, piece, False)

    load.wait()
    b_half[...] = kern_b[:, lanes]
    step = tiled(rows)
    w_rows = w_half.reshape(w_half.shape[0] * step, half)
    k_rows = k32.reshape(n * SPAN * step, half)

    @pl.loop(0, rows // 2)
    def _(j):
        both = [w_rows[pl.ds(2 * j + i, w_half.shape[0], stride=step), :].astype(low) for i in range(2)]
        made = dot(codes_o[...], jnp.concatenate(both, axis=1), NN)
        for i in range(2):
            c = 2 * j + i
            k_rows[pl.ds(c, n * SPAN, stride=step), :] = made[:, i * half : (i + 1) * half] + b_half[pl.ds(c, 1)]

    exchange = []
    for i, away in enumerate(sorted(everyone[1:], key=sum, reverse=True)):
        there = device_at(here, grid, away)
        k16[there] = k32[there, :bands, :rows].astype(low)
        exchange.append(remote(k16.at[there], kern_slot(), a_send.at[i], a_recv.at[i], (there, mp)))
    k16[me] = k32[me, :bands, :rows].astype(low)
    own.append(pltpu.make_async_copy(k16.at[me], kern_slot(), local.at[3]))
    own[-1].start()

    for piece in pieces[half_pieces:]:
        stage(1, piece, False)
    for number in range(2, depth):
        for piece in pieces:
            stage(number, piece, False)
    for piece in pieces:
        for shard in everyone:
            arrive(piece, shard)
    for copy in sends + shares:
        copy.wait_send()
    for copy in exchange:
        copy.wait()
    for copy in own:
        copy.wait()


def front(n, bands, facts_own, w_attn, w_in, w_out, gain, shift, patch_w, kern_w, kern_b, attn, mlp):
    grid = factors_of(n)
    hyper_width, rows, pixels = kern_w.shape
    half = pixels // 2
    direct = rows % 16 == 0
    pieces = 2 * len(orders_of(grid))
    f32, low = jnp.float32, jnp.bfloat16
    kept, _ = generator_scratch(hyper_width, w_in.shape[1])
    kern_shape = (bands, rows * n, half) if direct else (n, bands, rows, half)
    shapes = [
        (kern_shape, low),
        ((n,) + attn.shape, low),
        ((n,) + mlp.shape, low),
        ((n,) + facts_own.shape, f32),
        ((SPAN, patch_w.shape[1]), f32),
        ((n * SPAN, hyper_width), low),
    ] + [(k, f32) for k in kept]
    out = pl.pallas_call(
        partial(front_kernel, n, grid, direct, bands),
        out_shape=[jax.ShapeDtypeStruct(*s) for s in shapes],
        in_specs=[VMEM] * 7 + [ANY, VMEM, ANY, ANY],
        out_specs=[ANY] * 3 + [VMEM] * 6,
        scratch_shapes=[
            pltpu.VMEM((n * SPAN, hyper_width), f32),
            pltpu.VMEM((hyper_width, tiled(rows), half), f32),
            pltpu.VMEM((rows, half), f32),
            pltpu.VMEM((n, SPAN, tiled(rows), half), f32),
            pltpu.VMEM((n, bands, rows, half), low),
            pltpu.SemaphoreType.DMA((4,)),
            pltpu.SemaphoreType.DMA((n - 1,)),
            pltpu.SemaphoreType.DMA((n - 1,)),
            pltpu.SemaphoreType.DMA((n - 1,)),
            pltpu.SemaphoreType.DMA((n - 1,)),
            pltpu.SemaphoreType.DMA((pieces, n - 1)),
            pltpu.SemaphoreType.DMA((pieces, n)),
        ],
        compiler_params=params(1, BIG_VMEM),
        name="front",
    )(facts_own, w_attn, w_in, w_out, gain, shift, patch_w, kern_w, kern_b, attn, mlp)
    kernel = out[0]
    if not direct:
        kernel = kernel.transpose(1, 0, 2, 3).reshape(bands, rows * n, half)
    return [kernel, out[1].reshape(n * rows, -1), out[2].reshape(n * rows, -1)] + list(out[3:])


def layer_body(
    inner, after_mlp, after_attn,
    pix, kern, attn, mlp, cot, band_mask, key_mask, row_scale, patch_bias, gains, shifts, in_bias, out_bias, up_bias, down_bias,
    out_o, emb_grad_o, attn_grad, mlp_grad, small_o, small_up_o, small_in_o,
    emb, mid, part, inbox, norm_a, norm_b, qkv, prob, ctx, act, slope, d_out, d_pre, d_mid, d_att, d_ctx, d_qkv, turned, send, recv,
):
    me, mp = lax.axis_index("dp"), lax.axis_index("mp")
    partner = (me, 1 - mp)
    low = jnp.bfloat16
    bands, tokens, _ = pix.shape
    width = emb.shape[1]
    units = act.shape[1]
    halves = 2
    span = tokens // halves
    tile = 256
    copies = {}

    def swap(i, compute):
        for h in range(halves):
            r = pl.ds(h * span, span)
            if i >= 2:
                copies[i - 2, h].wait_send()

            @pl.loop(0, width // tile)
            def _(j):
                part[i % 2, r, lanes_at(j, tile)] = compute(r, j)

            copies[i, h] = remote(part.at[i % 2, r], inbox.at[i % 2, r], send.at[i, h], recv.at[i, h], partner)

    def swapped(i, h):
        copies[i, h].wait_recv()
        r = pl.ds(h * span, span)
        return part[i % 2, r] + inbox[i % 2, r]

    def embed_terms(r, j):
        total = jnp.zeros((span, tile), jnp.float32)
        for b in range(bands):
            total = total + dot(pix[b, r] * band_mask[b : b + 1].astype(low), kern[b, lanes_at(j, tile)], NT)
        return total

    swap(0, embed_terms)
    d_out[...] = (cot[...].astype(jnp.float32) * row_scale[...]).astype(low)
    turned[0] = d_out[...].T
    for h in range(halves):
        r = pl.ds(h * span, span)
        emb[r] = swapped(0, h) + patch_bias[...]
        hat, _ = normed(emb[r], vit_epsilon)
        norm_a[r] = (hat * gains[0:1] + shifts[0:1]).astype(low)

    @pl.loop(0, 3 * inner // 384)
    def _(j):
        cols = lanes_at(j, 384)
        qkv[:, cols] = (dot(norm_a[...], attn[:, cols], NN) + in_bias[:, cols]).astype(low)

    wide = 2 * HEAD_DIM
    lane = lax.broadcasted_iota(jnp.int32, (1, wide), 1)
    in_head = [(lane < HEAD_DIM).astype(low), (lane >= HEAD_DIM).astype(low)]
    scale = 1.0 / math.sqrt(HEAD_DIM)
    pairs = inner // wide

    def head_lanes(j, which):
        return pl.ds(pl.multiple_of(which * inner + j * wide, wide), wide)

    @pl.loop(0, pairs)
    def _(j):
        q, k, v = (qkv[:, head_lanes(j, w)] for w in range(3))
        total = jnp.zeros((tokens, wide), jnp.float32)
        for h in range(2):
            scores = jnp.where(key_mask[...] > 0.0, dot(q * in_head[h], k, NT) * scale, -1e30)
            raised = jnp.exp(scores - jnp.max(scores, axis=-1, keepdims=True))
            p = raised / row_sum(raised)
            prob[2 * j + h] = p
            total = total + dot(p.astype(low), v * in_head[h], NN)
        ctx[:, lanes_at(j, wide)] = total.astype(low)

    def out_terms(r, j):
        return dot(ctx[r], attn[lanes_at(j, tile), pl.ds(3 * inner, inner)], NT)

    swap(1, out_terms)
    turned[1] = norm_a[...].T
    for h in range(halves):
        r = pl.ds(h * span, span)
        mid[r] = emb[r] + swapped(1, h) + out_bias[...]
        hat, _ = normed(mid[r], vit_epsilon)
        norm_b[r] = (hat * gains[1:2] + shifts[1:2]).astype(low)

    @pl.loop(0, units // tile)
    def _(j):
        cols = lanes_at(j, tile)
        pre = dot(norm_b[...], mlp[:, cols], NN) + up_bias[:, cols]
        phi, density = normal_parts(pre)
        act[:, cols] = (pre * phi).astype(low)
        slope[:, cols] = phi + pre * density

    def down_terms(r, j):
        return dot(act[r], mlp[lanes_at(j, tile), pl.ds(units, units)], NT)

    @pl.loop(0, units // tile)
    def _(j):
        cols = lanes_at(j, tile)
        d_act = dot(d_out[...], mlp[:, pl.ds(pl.multiple_of(units + j * tile, tile), tile)], NN).astype(low)
        d_pre[:, cols] = (d_act.astype(jnp.float32) * slope[:, cols]).astype(low)

    def up_terms(r, j):
        return dot(d_pre[r], mlp[lanes_at(j, tile), pl.ds(0, units)], NT)

    def weight_grad(turned_ref, x, out, start):
        @pl.loop(0, width // tile)
        def _(i):
            for j in range(x.shape[1] // 384):
                out[lanes_at(i, tile), pl.ds(start + j * 384, 384)] = dot(
                    turned_ref[lanes_at(i, tile)], x[:, j * 384 : (j + 1) * 384], NN
                ).astype(low)

    swap(2, up_terms)
    turned[2] = norm_b[...].T
    weight_grad(turned.at[2], d_pre, mlp_grad, 0)
    weight_grad(turned.at[0], act, mlp_grad, units)
    after_mlp()
    small_up_o[...] = column_sums(d_pre[...])
    small_o[5:6] = column_sums(d_out[...])

    def back_through(x, i, h, which):
        hat, r = normed(x, vit_epsilon)
        return norm_back(hat, r, swapped(i, h), gains[which : which + 1])

    sums = []
    for h in range(halves):
        r = pl.ds(h * span, span)
        d_x, gain, shift = back_through(mid[r], 2, h, 1)
        d_x = d_x + d_out[r].astype(jnp.float32)
        d_mid[r] = d_x
        d_att[r] = d_x.astype(low)
        sums.append((gain, shift))
    small_o[1:2] = sums[0][0] + sums[1][0]
    small_o[3:4] = sums[0][1] + sums[1][1]
    small_o[4:5] = column_sums(d_att[...])

    @pl.loop(0, inner // 384)
    def _(j):
        d_ctx[:, lanes_at(j, 384)] = dot(
            d_att[...], attn[:, pl.ds(pl.multiple_of(3 * inner + j * 384, 384), 384)], NN
        ).astype(low)

    @pl.loop(0, pairs)
    def _(j):
        q, k, v = (qkv[:, head_lanes(j, w)] for w in range(3))
        d_c = d_ctx[:, lanes_at(j, wide)]
        d_q = jnp.zeros((tokens, wide), jnp.float32)
        d_k, d_v = d_q, d_q
        for h in range(2):
            p = prob[2 * j + h]
            d_p = dot(d_c * in_head[h], v, NT)
            d_s = (p * (d_p - row_sum(p * d_p))).astype(low)
            d_q = d_q + dot(d_s, k * in_head[h], NN)
            d_k = d_k + dot(d_s, q * in_head[h], TN)
            d_v = d_v + dot(p.astype(low), d_c * in_head[h], TN)
        d_qkv[:, head_lanes(j, 0)] = (d_q * scale).astype(low)
        d_qkv[:, head_lanes(j, 1)] = (d_k * scale).astype(low)
        d_qkv[:, head_lanes(j, 2)] = d_v.astype(low)

    def in_terms(r, j):
        return dot(d_qkv[r], attn[lanes_at(j, tile), pl.ds(0, 3 * inner)], NT)

    swap(3, in_terms)
    weight_grad(turned.at[1], d_qkv, attn_grad, 0)
    turned[2] = d_att[...].T
    weight_grad(turned.at[2], ctx, attn_grad, 3 * inner)
    after_attn()
    sums = []
    for h in range(halves):
        r = pl.ds(h * span, span)
        d_x, gain, shift = back_through(emb[r], 3, h, 0)
        emb_grad_o[r] = (d_x + d_mid[r]).astype(low)
        sums.append((gain, shift))
    small_o[0:1] = sums[0][0] + sums[1][0]
    small_o[2:3] = sums[0][1] + sums[1][1]
    small_o[6:7] = column_sums(emb_grad_o[...])
    small_o[7:8] = jnp.zeros((1, width), jnp.float32)
    small_in_o[...] = column_sums(d_qkv[...])

    def finish():
        swap(4, down_terms)
        for h in range(halves):
            r = pl.ds(h * span, span)
            out_o[r] = ((mid[r] + swapped(4, h) + down_bias[...]) * row_scale[r]).astype(low)
        for i in range(3, 5):
            for h in range(halves):
                copies[i, h].wait_send()

    return finish


def layer_buffers(inner, units, tokens, width):
    f32, low = jnp.float32, jnp.bfloat16
    return [
        pltpu.VMEM((tokens, width), f32),
        pltpu.VMEM((tokens, width), f32),
        pltpu.VMEM((2, tokens, width), f32),
        pltpu.VMEM((2, tokens, width), f32),
        pltpu.VMEM((tokens, width), low),
        pltpu.VMEM((tokens, width), low),
        pltpu.VMEM((tokens, 3 * inner), low),
        pltpu.VMEM((inner // HEAD_DIM, tokens, tokens), f32),
        pltpu.VMEM((tokens, inner), low),
        pltpu.VMEM((tokens, units), low),
        pltpu.VMEM((tokens, units), f32),
        pltpu.VMEM((tokens, width), low),
        pltpu.VMEM((tokens, units), low),
        pltpu.VMEM((tokens, width), f32),
        pltpu.VMEM((tokens, width), low),
        pltpu.VMEM((tokens, inner), low),
        pltpu.VMEM((tokens, 3 * inner), low),
        pltpu.VMEM((3, width, tokens), low),
        pltpu.SemaphoreType.DMA((5, 2)),
        pltpu.SemaphoreType.DMA((5, 2)),
    ]


LAYER_INS, LAYER_BUFFERS, TURNED = 15, 20, 17


class Scatter:
    def __init__(self, n, grid, rows, attn, mlp, attn_acc, mlp_acc, attn_box, mlp_box, outs, send, recv):
        self.me, self.mp = lax.axis_index("dp"), lax.axis_index("mp")
        self.here, self.grid, self.depth, self.rows = coords(self.me, grid), grid, len(grid), rows
        self.orders = [order[::-1] for order in orders_of(grid)]
        self.send_sem, self.recv_sem, self.sends = send, recv, []
        self.pieces = []
        for src, acc, box, out in ((attn, attn_acc, attn_box, outs[:4]), (mlp, mlp_acc, mlp_box, outs[4:])):
            width, share = src.shape[-1] // len(self.orders), len(out) // len(self.orders)
            for i, order in enumerate(self.orders):
                cols, to = pl.ds(i * width, width), out[i * share : (i + 1) * share]
                self.pieces.append((src, acc, box, to, cols, order, len(self.pieces)))
        self.slots = {}
        for which, order in enumerate(self.orders):
            number = 0
            for t in range(self.depth):
                for shard in self.rest(order, t):
                    for k in range(1, grid[order[t]]):
                        self.slots[which, t, shard, k] = number
                        number += 1

    def rest(self, order, t):
        return sorted(offsets_in(self.grid, order[t + 1 :]), key=sum, reverse=True)

    def shard(self, ref, owner, cols):
        if len(ref.shape) == 2:
            return ref.at[pl.ds(pl.multiple_of(self.rows * owner, 16), self.rows), cols]
        return ref.at[owner, :, cols]

    def start(self, t, piece):
        src, acc, box, _, cols, order, p = piece
        held = src if t == 0 else acc
        for shard in self.rest(order, t):
            for k in range(1, self.grid[order[t]]):
                step = along(self.grid, order[t], k)
                owner = device_at(self.here, self.grid, tuple(i + j for i, j in zip(shard, step)))
                slot = self.slots[p % len(self.orders), t, shard, self.grid[order[t]] - k]
                there = (device_at(self.here, self.grid, step), self.mp)
                block = self.shard(held, owner, cols)
                self.sends.append(
                    remote(block, box.at[slot, :, cols], self.send_sem.at[p, slot], self.recv_sem.at[p, slot], there)
                )

    def add(self, t, piece):
        src, acc, box, outs, cols, order, p = piece
        held = src if t == 0 else acc
        for shard in self.rest(order, t):
            owner = device_at(self.here, self.grid, shard)
            total = self.shard(held, owner, cols)[...].astype(jnp.float32)
            for k in range(1, self.grid[order[t]]):
                slot = self.slots[p % len(self.orders), t, shard, k]
                arrived(box.at[slot, :, cols], self.recv_sem.at[p, slot])
                total = total + box[slot, :, cols].astype(jnp.float32)
            if t < self.depth - 1:
                self.shard(acc, owner, cols)[...] = total.astype(acc.dtype)
            else:
                width = total.shape[1] // len(outs)
                for i, out in enumerate(outs):
                    out[...] = total[:, i * width : (i + 1) * width]


BACK_BUFFERS = 20


def back_body(
    n, grid, scatter, ordered, finish, block_for,
    pix, kern, band_mask, emb_grad, small, small_up, small_in, patch_w,
    pixel_o, local_o, blocks_o, bias_o,
    w_half, d_pix, got, got32, code, terms, term_box, bias_half, load, local, a_send, a_recv, f_send, f_recv,
    c_send, c_recv, b_send, b_recv,
):
    me, mp = lax.axis_index("dp"), lax.axis_index("mp")
    here = coords(me, grid)
    depth = len(grid)
    partner = (me, 1 - mp)
    low = jnp.bfloat16
    bands, tokens, half = pix.shape
    rows = got.shape[2]
    lanes = lanes_at(mp, half)
    far = sorted(offsets_in(grid, range(depth))[1:], key=sum, reverse=True)
    first, second = ordered
    own, to_partner = [], []

    exchange = []
    for i, step in enumerate(far):
        there = device_at(here, grid, step)
        exchange.append(remote(block_for(there), got.at[me], a_send.at[i], a_recv.at[i], (there, mp)))
    own.append(pltpu.make_async_copy(block_for(me), got.at[me], local.at[0]))
    own[-1].start()
    finish()

    @pl.loop(0, bands)
    def _(b):
        made = dot(emb_grad[...], kern[b], NN) * band_mask[pl.ds(b, 1)]
        d_pix[b] = made.astype(low)

    own.append(pltpu.make_async_copy(d_pix, pixel_o.at[:, :, lanes], local.at[1]))
    own[-1].start()
    to_partner.append(remote(d_pix, pixel_o.at[:, :, lanes], f_send.at[0], f_recv.at[0], partner))

    lane = 128
    per_slot = terms.shape[1] - SPAN
    terms[...] = jnp.zeros_like(terms)
    chunks = []
    for r in range(4):
        chunks += [small[r : r + 1, i * lane : (i + 1) * lane] for i in range(small.shape[1] // lane)]
    inner = small_in.shape[1] // 3
    for start in (0, 2 * inner):
        chunks += [small_in[:, start + i * lane : start + (i + 1) * lane] for i in range(inner // lane)]
    chunks += [small[4:5, i * lane : (i + 1) * lane] for i in range(small.shape[1] // lane)]
    chunks += [small_up[:, i * lane : (i + 1) * lane] for i in range(small_up.shape[1] // lane)]
    chunks += [small[5:6, i * lane : (i + 1) * lane] for i in range(small.shape[1] // lane)]
    each = -(-len(chunks) // n)
    for i, chunk in enumerate(chunks):
        terms[i // each, SPAN + i % each : SPAN + i % each + 1] = chunk
    patch_grad = small[6:7]
    d_tail = exact(jnp.broadcast_to(patch_grad, (8, patch_grad.shape[1])), patch_w[...], NT)[:1]

    for t in range(depth):
        for piece in first:
            scatter.add(t, piece)
            if t + 1 < depth:
                scatter.start(t + 1, piece)
        for piece in second:
            scatter.add(t, piece)
            if t + 1 < depth:
                scatter.start(t + 1, piece)

    bias_half[...] = jnp.zeros_like(bias_half)

    def take(source):
        block = got[source].astype(jnp.float32)
        got32[source, :bands, :rows] = block
        got32[source, bands:, :rows] = jnp.zeros((SPAN - bands,) + block.shape[1:], jnp.float32)
        bias_half[...] = bias_half[...] + jnp.sum(block, axis=0)

    own[0].wait()
    take(me)
    for i in reversed(range(n - 1)):
        source = device_at(here, grid, minus((0,) * depth, far[i], grid))
        exchange[i].wait_recv()
        take(source)
    to_partner.append(remote(got, local_o.at[mp], f_send.at[1], f_recv.at[1], partner))
    own.append(pltpu.make_async_copy(got, local_o.at[mp], local.at[2]))
    own[-1].start()
    bias_o[:, lanes] = bias_half[...]
    to_partner.append(remote(bias_half, bias_o.at[:, lanes], f_send.at[2], f_recv.at[2], partner))

    load.wait()
    step = tiled(rows)
    w_rows = w_half.reshape(w_half.shape[0] * step, half)
    g_rows = got32.reshape(n * SPAN * step, half)
    code[...] = jnp.zeros_like(code)

    @pl.loop(0, rows // 2)
    def _(j):
        taken = [g_rows[pl.ds(2 * j + i, n * SPAN, stride=step), :].astype(low) for i in range(2)]
        weights = [w_rows[pl.ds(2 * j + i, w_half.shape[0], stride=step), :].astype(low) for i in range(2)]
        code[...] = code[...] + dot(jnp.concatenate(taken, axis=1), jnp.concatenate(weights, axis=1), NT)

    terms[:, :SPAN] = code[...].reshape(n, SPAN, code.shape[1])
    sums = []
    for k in range(1, n):
        there = lax.rem(me + k, n)
        slot = n - k
        sums.append(remote(terms.at[there], term_box.at[mp, slot], c_send.at[k], c_recv.at[slot], (there, mp)))
    for k in range(n):
        there = lax.rem(me + k, n)
        slot = (n - k) % n
        sums.append(
            remote(terms.at[there], term_box.at[mp, slot], c_send.at[n + k], c_recv.at[n + slot], (there, 1 - mp))
        )
    term_box[mp, 0] = terms[me]
    for copy in sums:
        copy.wait_recv()
    total = term_box[0, 0, :SPAN]
    for i in range(1, 2 * n):
        total = total + term_box[i // n, i % n, :SPAN]
    vectors = term_box[mp, 0, SPAN:]
    for k in range(1, n):
        vectors = vectors + term_box[mp, k, SPAN:]
    is_tail = lax.broadcasted_iota(jnp.int32, total.shape, 0) == bands
    blocks_o[me, :SPAN] = jnp.where(is_tail, d_tail, total)
    blocks_o[me, SPAN : SPAN + per_slot] = vectors
    for i in range(patch_grad.shape[1] // lane):
        r = SPAN + per_slot + i
        blocks_o[me, r : r + 1] = patch_grad[:, i * lane : (i + 1) * lane]
    back = []
    for k in range(1, n):
        there = lax.rem(me + k, n)
        back.append(remote(blocks_o.at[me], blocks_o.at[me], b_send.at[k - 1], b_recv.at[k - 1], (there, mp)))
    for copy in back + to_partner:
        copy.wait()
    for copy in sums + exchange + scatter.sends:
        copy.wait_send()
    for copy in own[1:]:
        copy.wait()


def back_shapes(n, bands, tokens, rows, half, width, inner, units, hyper_width):
    f32, low = jnp.float32, jnp.bfloat16
    chunks = (6 * width + 2 * inner + units) // 128
    per_slot = -(-(-(-chunks // n)) // 8) * 8
    block = SPAN + per_slot + width // 128 + -(width // 128) % 8
    outs = [((rows, inner), f32)] * 4 + [((rows, units), f32)] * 2
    outs += [
        ((bands, tokens, 2 * half), low),
        ((2, n, bands, rows, half), low),
        ((n, block, 128), f32),
        ((rows, 2 * half), f32),
    ]
    specs = [VMEM] * 6 + [ANY, ANY, VMEM, VMEM]
    buffers = [
        pltpu.VMEM((hyper_width, tiled(rows), half), f32),
        pltpu.VMEM((bands, tokens, half), low),
        pltpu.VMEM((n, bands, rows, half), low),
        pltpu.VMEM((n, SPAN, tiled(rows), half), f32),
        pltpu.VMEM((n * SPAN, hyper_width), f32),
        pltpu.VMEM((n, SPAN + per_slot, 128), f32),
        pltpu.VMEM((2, n, SPAN + per_slot, 128), f32),
        pltpu.VMEM((rows, half), f32),
        pltpu.SemaphoreType.DMA,
        pltpu.SemaphoreType.DMA((3,)),
        pltpu.SemaphoreType.DMA((n - 1,)),
        pltpu.SemaphoreType.DMA((n - 1,)),
        pltpu.SemaphoreType.DMA((3,)),
        pltpu.SemaphoreType.DMA((3,)),
        pltpu.SemaphoreType.DMA((2 * n,)),
        pltpu.SemaphoreType.DMA((2 * n,)),
        pltpu.SemaphoreType.DMA((n - 1,)),
        pltpu.SemaphoreType.DMA((n - 1,)),
    ]
    return outs, specs, buffers


def scatter_buffers(n, grid, rows, attn_lanes, mlp_lanes):
    low, pieces = jnp.bfloat16, 2 * len(orders_of(grid))
    return [
        pltpu.VMEM((n - 1, rows, attn_lanes), low),
        pltpu.VMEM((n - 1, rows, mlp_lanes), low),
        pltpu.SemaphoreType.DMA((pieces, n - 1)),
        pltpu.SemaphoreType.DMA((pieces, n - 1)),
    ]


def weight_load(kern_w, w_half, sem, mp):
    half = w_half.shape[2]
    copy = pltpu.make_async_copy(kern_w.at[:, :, lanes_at(mp, half)], first_rows(w_half, kern_w.shape[1]), sem)
    copy.start()
    return copy


def whole_kernel(n, grid, inner, *refs):
    ins, refs = refs[: LAYER_INS + 2], refs[LAYER_INS + 2 :]
    outs, refs = refs[:11], refs[11:]
    layer, refs = refs[:LAYER_BUFFERS], refs[LAYER_BUFFERS:]
    (emb_grad, attn_grad, mlp_grad, small, small_up, small_in, d_kern), refs = refs[:7], refs[7:]
    turned = layer[TURNED].at[2]
    (attn_box, mlp_box, g_send, g_recv), back = refs[:4], refs[4:]
    kern_w, patch_w = ins[LAYER_INS:]
    pix, kern, band_mask = ins[0], ins[1], ins[5]
    me, mp = lax.axis_index("dp"), lax.axis_index("mp")
    rows = back[2].shape[2]
    load = weight_load(kern_w, back[0], back[8], mp)
    greet(n, me, mp, True)
    scatter = Scatter(
        n, grid, rows, attn_grad, mlp_grad, attn_grad, mlp_grad, attn_box, mlp_box, outs[1:7], g_send, g_recv
    )
    half = len(scatter.pieces) // 2
    attn_pieces, mlp_pieces = scatter.pieces[:half], scatter.pieces[half:]

    def begin(pieces):
        for piece in pieces:
            scatter.start(0, piece)

    finish = layer_body(
        inner, lambda: begin(mlp_pieces), lambda: begin(attn_pieces), *ins[:LAYER_INS],
        outs[0], emb_grad, attn_grad, mlp_grad, small, small_up, small_in, *layer,
    )
    turned[...] = emb_grad[...].T
    tile = 256

    @pl.loop(0, pix.shape[0])
    def _(b):
        masked = pix[b] * band_mask[pl.ds(b, 1)].astype(pix.dtype)
        for i in range(turned.shape[0] // tile):
            part = slice(i * tile, (i + 1) * tile)
            d_kern[b, part] = dot(turned[part], masked, NN).astype(d_kern.dtype)

    def block_for(there):
        return d_kern.at[:, pl.ds(pl.multiple_of(rows * there, 16), rows)]

    back_body(
        n, grid, scatter, (mlp_pieces, attn_pieces), finish, block_for,
        pix, kern, band_mask, emb_grad, small, small_up, small_in, patch_w, *outs[7:], *back[:8], load, *back[9:],
    )


def layer_kernel(inner, *refs):
    me, mp = lax.axis_index("dp"), lax.axis_index("mp")
    sem = pltpu.get_barrier_semaphore()
    pl.semaphore_signal(sem, inc=1, device_id=(me, 1 - mp), device_id_type=MESH)
    pl.semaphore_wait(sem, 1)
    layer_body(inner, lambda: None, lambda: None, *refs)()


def back_kernel(n, grid, *refs):
    (pix, kern, band_mask, emb_grad, small, small_up, small_in, attn, mlp, d_kern, kern_w, patch_w), refs = refs[:12], refs[12:]
    outs, refs = refs[:10], refs[10:]
    (attn_acc, mlp_acc, attn_box, mlp_box, g_send, g_recv), back = refs[:6], refs[6:]
    me, mp = lax.axis_index("dp"), lax.axis_index("mp")
    load = weight_load(kern_w, back[0], back[8], mp)
    greet(n, me, mp, True)
    scatter = Scatter(
        n, grid, attn.shape[1], attn, mlp, attn_acc, mlp_acc, attn_box, mlp_box, outs[:6], g_send, g_recv
    )
    for piece in scatter.pieces:
        scatter.start(0, piece)
    back_body(
        n, grid, scatter, (scatter.pieces, []), lambda: None, lambda there: d_kern.at[there],
        pix, kern, band_mask, emb_grad, small, small_up, small_in, patch_w, *outs[6:], *back[:8], load, *back[9:],
    )


def layer_and_back(n, inner, kern_w, patch_w, layer_ins):
    pix, kern, attn, mlp, _, band_mask = layer_ins[:6]
    grid = factors_of(n)
    bands, tokens, half = pix.shape
    width, units = attn.shape[0], mlp.shape[1] // 2
    hyper_width, rows, _ = kern_w.shape
    f32, low = jnp.float32, jnp.bfloat16
    shape = jax.ShapeDtypeStruct
    outs, specs, buffers = back_shapes(n, bands, tokens, rows, half, width, inner, units, hyper_width)
    layer = layer_buffers(inner, units, tokens, width)
    layer_outs = [
        ((tokens, width), low),
        (attn.shape, low),
        (mlp.shape, low),
        ((8, width), f32),
        ((1, units), f32),
        ((1, 3 * inner), f32),
    ]
    flops = 2 * tokens * width * (3 * bands * half + 9 * inner * 2 + 9 * units)
    cost = pl.CostEstimate(flops=flops, bytes_accessed=3 * 10**7, transcendentals=10**6)
    scattered = scatter_buffers(n, grid, rows, attn.shape[1], mlp.shape[1])
    if rows % 16 == 0:
        return pl.pallas_call(
            partial(whole_kernel, n, grid, inner),
            out_shape=[shape((tokens, width), low)] + [shape(*o) for o in outs],
            in_specs=[VMEM] * LAYER_INS + [ANY, VMEM],
            out_specs=[VMEM] + specs,
            scratch_shapes=layer
            + [pltpu.VMEM(*o) for o in layer_outs]
            + [pltpu.VMEM((bands, width, half), low)]
            + scattered
            + buffers,
            compiler_params=params(2, BIG_VMEM),
            cost_estimate=cost,
            name="layer",
        )(*layer_ins, kern_w, patch_w)
    layer_out, emb_grad, attn_grad, mlp_grad, small, small_up, small_in = pl.pallas_call(
        partial(layer_kernel, inner),
        out_shape=[shape((tokens, width), low)] + [shape(*o) for o in layer_outs],
        in_specs=[VMEM] * LAYER_INS,
        out_specs=[VMEM] * 7,
        scratch_shapes=layer,
        compiler_params=params(3, BIG_VMEM),
        cost_estimate=cost,
        name="layer",
    )(*layer_ins)
    d_kern = fast_einsum("tc,btp->bcp", emb_grad, pix * band_mask[:bands, None].astype(low)).astype(low)
    d_kern = d_kern.reshape(bands, n, rows, half).transpose(1, 0, 2, 3)
    attn_grad, mlp_grad = attn_grad.reshape(n, rows, -1), mlp_grad.reshape(n, rows, -1)
    out = pl.pallas_call(
        partial(back_kernel, n, grid),
        out_shape=[shape(*o) for o in outs],
        in_specs=[VMEM] * 9 + [ANY, ANY, VMEM],
        out_specs=specs,
        scratch_shapes=[pltpu.VMEM(attn_grad.shape, low), pltpu.VMEM(mlp_grad.shape, low)] + scattered + buffers,
        compiler_params=params(2, BIG_VMEM),
        name="back",
    )(pix, kern, band_mask, emb_grad, small, small_up, small_in, attn_grad, mlp_grad, d_kern, kern_w, patch_w)
    return [layer_out] + list(out)


def tail_kernel(
    n, bands, per_slot, recompute,
    blocks, codes, facts, rows_k, wide_k, prob_k, w_attn, w_in, w_out, gain, shift, patch_w, local_grad,
    g_attn, g_in, g_out, g_gain, g_shift, g_token, g_patch, g_kern, n_gain, n_shift, in_bias, out_bias, up_bias, down_bias,
    rows_s, wide_s, prob_s, d_mlp, tails, got, got32, made, sem, store,
):
    low = jnp.bfloat16
    rows, half = got.shape[3], got.shape[4]
    step = tiled(rows)
    loads = []
    for i in range(2):
        loads.append(pltpu.make_async_copy(local_grad.at[i], got.at[i], sem.at[i]))
        loads[-1].start()

    stores = []
    for i in range(2):
        loads[i].wait()

        @pl.loop(0, n)
        def _(s):
            block = got[i, s].astype(jnp.float32)
            got32[s, :bands, :rows] = block
            got32[s, bands:, :rows] = jnp.zeros((SPAN - bands,) + block.shape[1:], jnp.float32)

        g_rows = got32.reshape(n * SPAN * step, half)
        m_rows = made.at[i].reshape(made.shape[1] * step, half)

        @pl.loop(0, rows // 2)
        def _(j):
            taken = [g_rows[pl.ds(2 * j + c, n * SPAN, stride=step), :].astype(low) for c in range(2)]
            both = dot(codes[...], jnp.concatenate(taken, axis=1), TN)
            for c in range(2):
                m_rows[pl.ds(2 * j + c, made.shape[1], stride=step), :] = both[:, c * half : (c + 1) * half]

        stores.append(pltpu.make_async_copy(first_rows(made.at[i], rows), g_kern.at[:, :, pl.ds(i * half, half)], store.at[i]))
        stores[-1].start()

    groups = n // GROUP

    def put(ref, where, value):
        ref[where] = value if groups == 1 else ref[where] + value

    outs = (g_attn, g_in, g_out, g_gain, g_shift)
    if groups > 1:
        for ref in outs:
            ref[...] = jnp.zeros_like(ref)
    token = jnp.zeros_like(g_token)
    for g in range(groups):
        kept = (rows_k, wide_k, prob_k)
        if recompute:
            kept = (rows_s, wide_s, prob_s)
            generator_forward(facts, g, w_attn, w_in, w_out, gain, shift, *kept)
        count = GROUP * SPAN
        d_second = blocks[pl.ds(g * GROUP, GROUP), :SPAN].reshape(count, blocks.shape[2])
        generator_backward(d_second, put, w_attn, w_in, w_out, gain, *kept, d_mlp, outs + (g_token,))
        tails[pl.ds(g * GROUP, GROUP)] = kept[0].at[SECOND][pl.ds(bands, GROUP, stride=SPAN), :]
        token = token + all_rows(d_mlp.at[0][pl.ds(bands, GROUP, stride=SPAN), :])
    g_token[...] = token
    lane = 128
    for i in range(g_patch.shape[1] // lane):
        g_patch[:, i * lane : (i + 1) * lane] = exact(tails[...], blocks[:, SPAN + per_slot + i, :], TN)

    chunks = []
    for ref, r in ((n_gain, 0), (n_gain, 1), (n_shift, 0), (n_shift, 1), (in_bias, 0), (in_bias, 1)):
        chunks += [(ref, r, i) for i in range(ref.shape[1] // lane)]
    for ref in (out_bias, up_bias, down_bias):
        chunks += [(ref, 0, i) for i in range(ref.shape[1] // lane)]
    each = -(-len(chunks) // n)
    for k, (ref, r, i) in enumerate(chunks):
        row = SPAN + k % each
        ref[r : r + 1, i * lane : (i + 1) * lane] = blocks[k // each, row : row + 1]
    for copy in stores:
        copy.wait()


def tail(n, bands, inner, units, blocks, codes, facts, kept, weights, patch_w, local_grad):
    w_attn, w_in, w_out, gain, shift = weights
    width = patch_w.shape[1]
    hyper_width = w_attn.shape[1]
    rows, half = local_grad.shape[3:]
    f32 = jnp.float32
    chunks = (6 * width + 2 * inner + units) // 128
    per_slot = -(-(-(-chunks // n)) // 8) * 8
    recompute = n > GROUP
    kept_shapes, _ = generator_scratch(hyper_width, w_in.shape[1])
    shapes = [
        w_attn.shape, w_in.shape, w_out.shape, gain.shape, shift.shape, (1, hyper_width), patch_w.shape,
        (hyper_width, rows, 2 * half), (2, width), (2, width), (2, inner), (1, width), (1, units), (1, width),
    ]
    return pl.pallas_call(
        partial(tail_kernel, n, bands, per_slot, recompute),
        out_shape=[jax.ShapeDtypeStruct(s, f32) for s in shapes],
        in_specs=[VMEM] * 12 + [ANY],
        out_specs=[VMEM] * 7 + [ANY] + [VMEM] * 6,
        scratch_shapes=[pltpu.VMEM(k if recompute else (8, 128), f32) for k in kept_shapes]
        + [
            pltpu.VMEM((2, GROUP * SPAN, hyper_width), f32),
            pltpu.VMEM((n, hyper_width), f32),
            pltpu.VMEM(local_grad.shape, local_grad.dtype),
            pltpu.VMEM((n, SPAN, tiled(rows), half), f32),
            pltpu.VMEM((2, hyper_width, tiled(rows), half), f32),
            pltpu.SemaphoreType.DMA((2,)),
            pltpu.SemaphoreType.DMA((2,)),
        ],
        compiler_params=pltpu.CompilerParams(vmem_limit_bytes=BIG_VMEM),
        name="tail",
    )(blocks, codes, facts, *kept, w_attn, w_in, w_out, gain, shift, patch_w, local_grad)


def fast_einsum(pattern, left_side, right_side):
    return jnp.einsum(pattern, left_side, right_side, preferred_element_type=jnp.float32)


def wave_embedding(wavelengths, model_width):
    half_width = model_width // 2
    frequency = 10000.0 ** (-jnp.arange(half_width, dtype=jnp.float32) * 2.0 / model_width)
    angles = wavelengths.astype(jnp.float32)[..., None] * frequency
    return jnp.concatenate([jnp.sin(angles), jnp.cos(angles)], axis=-1)


def per_device(
    n,
    pixels,
    band_count,
    wavelengths,
    size_class,
    token_keep,
    hyp_attn,
    hyp_mlp_in,
    hyp_mlp_out,
    hyp_gain,
    hyp_shift,
    bias_token,
    kern_weight,
    kern_bias,
    patch_bias_weight,
    norm_gain,
    norm_shift,
    attn_in,
    attn_in_bias,
    attn_out,
    attn_out_bias,
    mlp_in,
    mlp_in_bias,
    mlp_out,
    mlp_out_bias,
    cotangent,
):
    mp = lax.axis_index("mp")
    slot_count, bands, tokens, pix_size = pixels.shape
    assert slot_count == 1 and n % GROUP == 0 and bands + 1 <= SPAN
    hyper_width = hyp_attn.shape[1]
    half = pix_size // 2
    low = jnp.bfloat16
    inner, units = attn_in.shape[2], mlp_in.shape[1]

    band_valid = jnp.arange(SPAN) < band_count[0]
    sequence = jnp.concatenate([wave_embedding(wavelengths[0], hyper_width), bias_token[None]], axis=0)
    sequence = jnp.pad(sequence, ((0, SPAN - bands - 1), (0, 0)))
    usable = (band_valid & (jnp.arange(SPAN) < bands)) | (jnp.arange(SPAN) == bands)
    usable = jnp.broadcast_to(usable.astype(jnp.float32)[:, None], (SPAN, hyper_width))
    facts_own = jnp.concatenate([sequence, usable], axis=0)

    attn_shard = jnp.concatenate([attn_in[0], attn_in[1], attn_in[2], attn_out], axis=1).astype(low)
    mlp_shard = jnp.concatenate([mlp_in, mlp_out], axis=1).astype(low)
    weights = (hyp_attn, hyp_mlp_in, hyp_mlp_out, hyp_gain, hyp_shift)
    kernel, attn_all, mlp_all, facts, patch_rows, codes, *kept = front(
        n, bands, facts_own, *weights, patch_bias_weight, kern_weight, kern_bias, attn_shard, mlp_shard
    )

    live_rows = jnp.where(
        size_class[0] == 0, tokens * 49 // 256, jnp.where(size_class[0] == 1, tokens * 196 // 256, tokens)
    )
    position = jnp.arange(tokens)
    row_valid = position < live_rows
    key_valid = row_valid & ((token_keep[0] == 1) | (position == 0))
    input_bias = jnp.concatenate([attn_in_bias[0], jnp.zeros_like(attn_in_bias[0]), attn_in_bias[1]])
    layer_ins = (
        lax.dynamic_slice_in_dim(pixels[0], mp * half, half, 2),
        kernel,
        attn_all,
        mlp_all,
        cotangent[0],
        jnp.broadcast_to(band_valid.astype(jnp.float32)[:, None], (SPAN, half)),
        key_valid.astype(jnp.float32)[None],
        row_valid.astype(jnp.float32)[:, None],
        patch_rows[bands : bands + 1],
        norm_gain,
        norm_shift,
        input_bias[None],
        attn_out_bias[None],
        mlp_in_bias[None],
        mlp_out_bias[None],
    )
    (
        layer_out,
        grad_q,
        grad_k,
        grad_v,
        grad_attn_out,
        grad_mlp_in,
        grad_mlp_out,
        pixel_grad,
        local_grad,
        blocks,
        grad_kern_bias,
    ) = layer_and_back(n, inner, kern_weight, patch_bias_weight, layer_ins)
    (
        g_attn,
        g_in,
        g_out,
        g_gain,
        g_shift,
        g_token,
        g_patch,
        grad_kern_weight,
        grad_norm_gain,
        grad_norm_shift,
        grad_in_bias,
        grad_attn_out_bias,
        grad_mlp_in_bias,
        grad_mlp_out_bias,
    ) = tail(n, bands, inner, units, blocks, codes, facts, kept, weights, patch_bias_weight, local_grad)
    return (
        layer_out[None],
        pixel_grad[None],
        g_attn,
        g_in,
        g_out,
        g_gain,
        g_shift,
        g_token[0],
        grad_kern_weight,
        grad_kern_bias,
        g_patch,
        grad_norm_gain,
        grad_norm_shift,
        jnp.stack([grad_q, grad_k, grad_v]),
        grad_in_bias,
        grad_attn_out,
        grad_attn_out_bias[0],
        grad_mlp_in,
        grad_mlp_in_bias[0],
        grad_mlp_out,
        grad_mlp_out_bias[0],
    )


def solution(mesh):
    return jax.shard_map(
        partial(per_device, mesh.shape["dp"]),
        mesh=mesh,
        in_specs=(
            P("dp", None, None, None),
            P("dp"),
            P("dp", None),
            P("dp"),
            P("dp", None),
            P(),
            P(),
            P(),
            P(),
            P(),
            P(),
            P(None, "dp", None),
            P("dp", None),
            P(),
            P(),
            P(),
            P(None, "dp", "mp"),
            P(None, "mp"),
            P("dp", "mp"),
            P(),
            P("dp", "mp"),
            P("mp"),
            P("dp", "mp"),
            P(),
            P("dp", None, None),
        ),
        out_specs=(
            P("dp", None, None),
            P("dp", None, None, None),
            P(),
            P(),
            P(),
            P(),
            P(),
            P(),
            P(None, "dp", None),
            P("dp", None),
            P(),
            P(),
            P(),
            P(None, "dp", "mp"),
            P(None, "mp"),
            P("dp", "mp"),
            P(),
            P("dp", "mp"),
            P("mp"),
            P("dp", "mp"),
            P(),
        ),
        check_vma=False,
    )
```

time: 1400 us -> 367 us (0.26)
  waiting for transfers between devices: 849 us -> 0 us
  Pallas kernels: 0 us -> 335 us
  blocking collectives: 318 us -> 0 us
  matrix products: 79.3 us -> 0 us
  local copies, waits for them, and re-layouts: 73.3 us -> 14.1 us
  starting transfers between devices: 19.3 us -> 0 us
  between operations: 18.5 us -> 2.19 us
  other arithmetic: 30.8 us -> 14.9 us
    reduce_scatter x3 -> x0, waiting for transfers between devices: 411 us -> none  [the longest x1 142 us: per_device(): lax.psum_scatter(grad_up, 'dp', scatter_dimension=0, tiled=True)]
    pallas_call x0 -> x3, Pallas kernels: none -> 335 us  [the longest x1 186 us: layer_and_back(): pl.pallas_call(partial(whole_kernel, n, grid, inner), out_shape=[shape((t...]
    psum x5 -> x0, waiting for transfers between devices: 211 us -> none  [the longest x1 126 us: per_device(): lax.psum((local_hyper[0], local_hyper[1], local_hyper[2], local_hyper[3],...]
    all_gather x2 -> x0, blocking collectives: 177 us -> none  [the longest x1 134 us: per_device(): lax.all_gather(weight_shards[1], 'dp', axis=0, tiled=True)]
    all_gather x3 -> x0, waiting for transfers between devices: 122 us -> none  [the longest x1 63.8 us: per_device(): lax.all_gather(weight_shards[2], 'dp', axis=0, tiled=True)]
    all_to_all x2 -> x0, waiting for transfers between devices: 105 us -> none  [the longest x1 105 us: per_device(): lax.all_to_all(kernel_grad, 'dp', split_axis=1, concat_axis=0, tiled=True)]
    dot_general x50 -> x0, matrix products: 79.3 us -> none  [the longest x24 62.3 us: fast_einsum(): jnp.einsum(pattern, left_side, right_side, preferred_element_type=jnp.flo...]
    psum x1 -> x0, blocking collectives: 79.3 us -> none  [per_device(): lax.psum((local_hyper[0], local_hyper[1], local_hyper[2], local_hyper[3],...]
  transfers between devices with their start and end apart: 16 -> 0, of which waited for: 12 -> 0; matrix products, arithmetic and copies ran while one was open for 5% -> 0% of each run, Pallas kernels for 0% -> 0%
where the time goes in v2:
time: 367 us; the launch traced here: 366 us
  Pallas kernels  335 us (91%)
  other arithmetic  14.9 us (4%)
  local copies, waits for them, and re-layouts  14.1 us (4%)
    pallas_call x1, Pallas kernels, layer_and_back(): pl.pallas_call(partial(whole_kernel, n, grid, inner), out_shape=[shape((t...  186 us
    pallas_call x1, Pallas kernels, front(): pl.pallas_call(partial(front_kernel, n, grid, direct, bands), out_shape=[...  116 us
    pallas_call x1, Pallas kernels, tail(): pl.pallas_call(partial(tail_kernel, n, bands, per_slot, recompute), out_s...  32.5 us

profile of v2, /device:TPU:0, one launch (start us, length us, event | category | flops | bytes accessed | tf_op | source)
XLA Modules:
  0.0 365.8 jit_solution(18149541991579565061)
XLA Ops:
  0.7 0.0 copy-start
  2.1 0.7 convert_bitcast_fusion
  2.8 0.1 pad.18.clone
  2.9 1.2 and_convert_fusion.refs_6_
  4.1 1.3 broadcast_in_dim.45.refs_12_
  5.4 1.3 broadcast_in_dim.47.refs_14_
  6.6 0.8 slice_reduce_fusion.1
  7.4 0.6 broadcast_in_dim.44.refs_11_
  8.0 1.3 broadcast_in_dim.46.refs_13_
  9.3 0.7 broadcast_in_dim.42.refs_5_
  10.0 0.1 multiply_sine_fusion
  10.1 0.7 select_maximum_fusion
  10.9 0.7 pad_maximum_fusion.3.facts_own
  11.5 0.9 convert.21
  12.4 0.9 convert.20
  13.4 0.7 pad_maximum_fusion.2.attn
  14.1 0.7 fusion.refs_7_
  14.7 1.0 convert.22
  15.7 1.0 convert.23
  16.7 0.7 pad_maximum_fusion.mlp
  17.4 0.0 copy-done
  17.4 1.1 dynamic-slice_bitcast_fusion.refs_0_
  18.5 116.2 %front.1 = (bf16[13,768,128]{2,1,0:T(8,128)(2,1)}, bf16[16,48,1536]{2,1,0:T(8,128)(2,1)}, bf16[16,48,3072]{2,1,0:T(8,128)(2,1)}, f32[16,32,128]{2,1,0:T(8,128)},...) custom-call(f32[32,128]{1,0:T(8,128)} %pad_maximum_fusion.3.facts_ow, ...), custom_call_target="tpu_custom_call" | custom-call | tf_op jit(solution)/shard_map/front/pallas_call | solution.py:389
  134.8 1.3 slice.24.refs_8_
  136.1 185.9 %layer.1 = (bf16[256,768]{1,0:T(8,128)(2,1)}, f32[48,384]{1,0:T(8,128)}, f32[48,384]{1,0:T(8,128)}, f32[48,384]{1,0:T(8,128)}, f32[48,384]{1,0:T(8,128)}, /*inde...) custom-call(bf16[13,256,128]{2,1,0:T(8,128)(2,1)} %dynamic-slice_bit, ...), custom_call_target="tpu_custom_call" | custom-call | flops 10116661248 | bytes 30000000 | tf_op jit(solution)/shard_map/layer/pallas_call | solution.py:985
  322.0 1.7 pad_maximum_fusion.1
  323.7 0.0 copy-start.1
  323.7 32.5 %tail.1 = (f32[4,128,128]{2,1,0:T(8,128)}, f32[128,2048]{1,0:T(8,128)}, f32[2048,128]{1,0:T(8,128)}, f32[2,128]{1,0:T(2,128)}, f32[2,128]{1,0:T(2,128)}, /*index...) custom-call(f32[16,32,128]{2,1,0:T(8,128)} %get-tuple-element.61.blo, ...), custom_call_target="tpu_custom_call" | custom-call | tf_op jit(solution)/shard_map/tail/pallas_call | solution.py:1113
  356.2 0.0 copy-start.5
  356.2 0.0 copy-start.4
  356.2 1.3 reduce.2
  357.5 1.3 reduce.4
  358.8 1.3 reduce.3
  360.1 0.0 copy-start.3
  360.1 0.0 copy-start.2
  360.1 1.8 copy.54
  361.9 0.0 copy-done.1
  361.9 1.2 copy.55
  363.1 0.0 copy-done.5
  363.1 0.6 copy.56
  363.8 0.0 copy-done.4
  363.8 0.6 copy.57
  364.4 0.0 copy-done.3
  364.4 0.7 copy.58
  365.1 0.0 copy-done.2
  365.1 0.7 copy.59
  (5 shorter events, 0.0 us)
Async XLA Ops:
  0.7 16.8 %copy-start = (bf16[1,13,256,256]{3,2,1,0:T(8,128)(2,1)S(1)}, bf16[1,13,256,256]{3,2,1,0:T(8,128)(2,1)}, u32[]{:S(2)}) copy-start(bf16[1,13,256,256]{3,2,1,0:T(8,128)(2,1)} %param.25) | copy-start | bytes 5111812
  323.7 38.3 %copy-start.1 = (bf16[13,256,256]{2,1,0:T(8,128)(2,1)S(1)}, bf16[13,256,256]{2,1,0:T(8,128)(2,1)}, u32[]{:S(2)}) copy-start(bf16[13,256,256]{2,1,0:T(8,128)(2,1)} %get-tuple-element.60) | copy-start | bytes 5111812
  356.2 7.0 %copy-start.5 = (f32[48,256]{1,0:T(8,128)S(1)}, f32[48,256]{1,0:T(8,128)}, u32[]{:S(2)}) copy-start(f32[48,256]{1,0:T(8,128)} %get-tuple-element.128) | copy-start | bytes 147460
  356.2 7.6 %copy-start.4 = (f32[48,384]{1,0:T(8,128)S(1)}, f32[48,384]{1,0:T(8,128)}, u32[]{:S(2)}) copy-start(f32[48,384]{1,0:T(8,128)} %get-tuple-element.134) | copy-start | bytes 221188
  360.1 4.3 %copy-start.3 = (f32[48,1536]{1,0:T(8,128)S(1)}, f32[48,1536]{1,0:T(8,128)}, u32[]{:S(2)}) copy-start(f32[48,1536]{1,0:T(8,128)} %get-tuple-element.136) | copy-start | bytes 884740
  360.1 5.0 %copy-start.2 = (f32[48,1536]{1,0:T(8,128)S(1)}, f32[48,1536]{1,0:T(8,128)}, u32[]{:S(2)}) copy-start(f32[48,1536]{1,0:T(8,128)} %get-tuple-element.138) | copy-start | bytes 884740

commit v3 on v2

--- a/solution.py
+++ b/solution.py
@@ -90,7 +90,7 @@
 
 def exact(a, b, contract=NN):
     return lax.dot_general(
-        a, b, (contract, ((), ())), precision=lax.Precision.HIGHEST, preferred_element_type=jnp.float32
+        a, b, (contract, ((), ())), precision=lax.Precision.HIGH, preferred_element_type=jnp.float32
     )
 
 
@@ -135,6 +135,13 @@
 
 def first_rows(ref, rows):
     return ref if ref.shape[-2] == rows else ref.at[:, pl.ds(0, rows)]
+
+
+def under(conditions, step):
+    if conditions:
+        pl.when(conditions[0])(lambda: under(conditions[1:], step))
+    else:
+        step()
 
 
 def arrived(block, sem):
@@ -256,7 +263,6 @@
     orders = orders_of(grid)
     depth = len(grid)
     everyone = offsets_in(grid, range(depth))
-    index = {o: i for i, o in enumerate(everyone)}
     zero = (0,) * depth
 
     def kern_slot():
@@ -284,36 +290,73 @@
         width = src.shape[1] // len(orders)
         for part, order in enumerate(orders):
             pieces.append((src, dst, pl.ds(part * width, width), order, len(pieces)))
-    sends, count, seen = [], [0] * len(pieces), set()
-
-    def send(piece, shard, step):
+    sends, count = [], [0] * len(pieces)
+    size = grid[0]
+    place = here[0]
+
+    def send(piece, owner, there, conditions):
         src, dst, cols, _, p = piece
-        owner = device_at(here, grid, shard)
-        there = device_at(here, grid, step)
-        held = dst.at[owner, :, cols] if any(shard) else src.at[:, cols]
-        slot = index[minus(shard, step, grid)]
-        sends.append(
-            remote(held, dst.at[owner, :, cols], g_send.at[p, count[p]], g_recv.at[p, slot], (there, mp))
-        )
+        held = src.at[:, cols] if owner is None else dst.at[owner, :, cols]
+        owner = me if owner is None else owner
+        remote(held, dst.at[owner, :, cols], g_send.at[p, count[p]], g_recv.at[p, owner], (there, mp))
+        sends.append((conditions, src, cols, p, count[p]))
         count[p] += 1
 
-    def arrive(piece, shard):
+    def spread(piece, owner, number, conditions):
+        for dim in piece[3][number:]:
+            for k in range(1, grid[dim]):
+                send(piece, owner, device_at(here, grid, along(grid, dim, k)), conditions)
+
+    def beside(piece, step, k):
+        offset = along(grid, piece[3][1], k) if k else zero
+        position = [place + step] + here[1:]
+        return device_at(position, grid, offset)
+
+    def arrive(piece, owner):
         _, dst, cols, _, p = piece
-        if any(shard) and (p, shard) not in seen:
-            seen.add((p, shard))
-            arrived(dst.at[device_at(here, grid, shard), :, cols], g_recv.at[p, index[shard]])
-
-    def stage(number, piece, own_shard):
-        order = piece[3]
-        for shard in sorted(offsets_in(grid, order[:number]), key=sum):
-            if any(shard) != own_shard:
-                arrive(piece, shard)
-                for k in range(1, grid[order[number]]):
-                    send(piece, shard, along(grid, order[number], k))
+        arrived(dst.at[owner, :, cols], g_recv.at[p, owner])
+
+    def neighbour(step):
+        return device_at([place + step] + here[1:], grid, zero)
+
+    def line(piece, d):
+        for side in (-1, 1):
+            inside = (place >= d) if side < 0 else (place + d < size)
+            onward = (place + 1 < size) if side < 0 else (place > 0)
+
+            @pl.when(inside)
+            def _():
+                owner = beside(piece, side * d, 0)
+                arrive(piece, owner)
+
+                @pl.when(onward)
+                def _():
+                    send(piece, owner, neighbour(-side), (inside, onward))
+
+                spread(piece, owner, 1, (inside,))
+
+    def other_lines(piece, d):
+        if depth == 1:
+            return
+        for k in range(1, grid[piece[3][1]]):
+            for side in (-1, 1) if d else (1,):
+                inside = (place >= d) if side < 0 else (place + d < size)
+
+                @pl.when(inside)
+                def _():
+                    owner = beside(piece, side * d, k)
+                    arrive(piece, owner)
+                    spread(piece, owner, 2, (inside,))
 
     for piece in pieces:
-        for number in range(depth):
-            stage(number, piece, True)
+        for side in (-1, 1):
+            onward = (place + 1 < size) if side < 0 else (place > 0)
+
+            @pl.when(onward)
+            def _():
+                send(piece, None, neighbour(-side), (onward,))
+
+        spread(piece, None, 1, ())
 
     for copy in shares:
         copy.wait_recv()
@@ -326,9 +369,8 @@
         codes_o[group] = jnp.where(is_band, rows_o[SECOND] + rows_o[SEQ], 0.0).astype(low)
     patch_o[...] = exact(second[pl.ds(pl.multiple_of(me * SPAN, SPAN), SPAN)], patch_w[...])
 
-    half_pieces = len(pieces) // 2
-    for piece in pieces[:half_pieces]:
-        stage(1, piece, False)
+    for piece in pieces:
+        line(piece, 1)
 
     load.wait()
     b_half[...] = kern_b[:, lanes]
@@ -353,15 +395,22 @@
     own.append(pltpu.make_async_copy(k16.at[me], kern_slot(), local.at[3]))
     own[-1].start()
 
-    for piece in pieces[half_pieces:]:
-        stage(1, piece, False)
-    for number in range(2, depth):
+    for d in range(2, size):
         for piece in pieces:
-            stage(number, piece, False)
+            line(piece, d)
+            other_lines(piece, d - 2)
+    for d in range(max(size - 2, 0), size):
+        for piece in pieces:
+            other_lines(piece, d)
     for piece in pieces:
-        for shard in everyone:
-            arrive(piece, shard)
-    for copy in sends + shares:
+        order = piece[3]
+        for shard in offsets_in(grid, order[2:]) if depth > 2 else []:
+            if any(shard):
+                for rest in offsets_in(grid, order[:2]):
+                    arrive(piece, device_at(here, grid, tuple(i + j for i, j in zip(shard, rest))))
+    for conditions, src, cols, p, i in sends:
+        under(conditions, lambda: arrived(src.at[:, cols], g_send.at[p, i]))
+    for copy in shares:
         copy.wait_send()
     for copy in exchange:
         copy.wait()
@@ -402,7 +451,7 @@
             pltpu.SemaphoreType.DMA((n - 1,)),
             pltpu.SemaphoreType.DMA((n - 1,)),
             pltpu.SemaphoreType.DMA((n - 1,)),
-            pltpu.SemaphoreType.DMA((pieces, n - 1)),
+            pltpu.SemaphoreType.DMA((pieces, n + 2 * sum(grid) * grid[-1])),
             pltpu.SemaphoreType.DMA((pieces, n)),
         ],
         compiler_params=params(1, BIG_VMEM),
@@ -639,8 +688,10 @@
 class Scatter:
     def __init__(self, n, grid, rows, attn, mlp, attn_acc, mlp_acc, attn_box, mlp_box, outs, send, recv):
         self.me, self.mp = lax.axis_index("dp"), lax.axis_index("mp")
-        self.here, self.grid, self.depth, self.rows = coords(self.me, grid), grid, len(grid), rows
-        self.orders = [order[::-1] for order in orders_of(grid)]
+        self.here, self.grid, self.rows = coords(self.me, grid), grid, rows
+        self.size, self.place = grid[0], self.here[0]
+        self.orders = [order[:0:-1] for order in orders_of(grid)]
+        self.stages = len(grid) - 1
         self.send_sem, self.recv_sem, self.sends = send, recv, []
         self.pieces = []
         for src, acc, box, out in ((attn, attn_acc, attn_box, outs[:4]), (mlp, mlp_acc, mlp_box, outs[4:])):
@@ -651,50 +702,98 @@
         self.slots = {}
         for which, order in enumerate(self.orders):
             number = 0
-            for t in range(self.depth):
+            for t in range(self.stages):
                 for shard in self.rest(order, t):
                     for k in range(1, grid[order[t]]):
                         self.slots[which, t, shard, k] = number
                         number += 1
+        self.line_slots = number if self.stages else 0
 
     def rest(self, order, t):
-        return sorted(offsets_in(self.grid, order[t + 1 :]), key=sum, reverse=True)
+        return sorted(offsets_in(self.grid, (0,) + order[t + 1 :]), key=sum, reverse=True)
 
     def shard(self, ref, owner, cols):
         if len(ref.shape) == 2:
             return ref.at[pl.ds(pl.multiple_of(self.rows * owner, 16), self.rows), cols]
         return ref.at[owner, :, cols]
 
+    def send(self, block, piece, index, slot, there, conditions=()):
+        _, _, box, _, cols, _, p = piece
+        remote(block, box.at[slot, :, cols], self.send_sem.at[p, index], self.recv_sem.at[p, slot], (there, self.mp))
+        self.sends.append((conditions, box, cols, p, index))
+
+    def receive(self, piece, slot):
+        _, _, box, _, cols, _, p = piece
+        arrived(box.at[slot, :, cols], self.recv_sem.at[p, slot])
+        return box[slot, :, cols].astype(jnp.float32)
+
     def start(self, t, piece):
-        src, acc, box, _, cols, order, p = piece
+        src, acc, _, _, cols, order, p = piece
         held = src if t == 0 else acc
         for shard in self.rest(order, t):
             for k in range(1, self.grid[order[t]]):
                 step = along(self.grid, order[t], k)
                 owner = device_at(self.here, self.grid, tuple(i + j for i, j in zip(shard, step)))
                 slot = self.slots[p % len(self.orders), t, shard, self.grid[order[t]] - k]
-                there = (device_at(self.here, self.grid, step), self.mp)
-                block = self.shard(held, owner, cols)
-                self.sends.append(
-                    remote(block, box.at[slot, :, cols], self.send_sem.at[p, slot], self.recv_sem.at[p, slot], there)
-                )
+                self.send(self.shard(held, owner, cols), piece, slot, slot, device_at(self.here, self.grid, step))
 
     def add(self, t, piece):
-        src, acc, box, outs, cols, order, p = piece
+        src, acc, _, _, cols, order, p = piece
         held = src if t == 0 else acc
         for shard in self.rest(order, t):
             owner = device_at(self.here, self.grid, shard)
             total = self.shard(held, owner, cols)[...].astype(jnp.float32)
             for k in range(1, self.grid[order[t]]):
-                slot = self.slots[p % len(self.orders), t, shard, k]
-                arrived(box.at[slot, :, cols], self.recv_sem.at[p, slot])
-                total = total + box[slot, :, cols].astype(jnp.float32)
-            if t < self.depth - 1:
-                self.shard(acc, owner, cols)[...] = total.astype(acc.dtype)
-            else:
-                width = total.shape[1] // len(outs)
+                total = total + self.receive(piece, self.slots[p % len(self.orders), t, shard, k])
+            self.shard(acc, owner, cols)[...] = total.astype(acc.dtype)
+
+    def on_line(self, step):
+        return device_at([self.place + step] + self.here[1:], self.grid, (0,) * len(self.grid))
+
+    def pass_on(self, piece, j):
+        src, acc, _, _, cols, _, p = piece
+        held = acc if self.stages else src
+        for side in (1, -1):
+            inside = (self.place + j < self.size) if side > 0 else (self.place >= j)
+            behind = (self.place > 0) if side > 0 else (self.place + 1 < self.size)
+
+            @pl.when(inside)
+            def _():
+                mine = self.shard(held, self.on_line(side * j), cols)
+                target = self.shard(acc, self.on_line(side * j), cols)
+                slot = self.line_slots + self.place + side * j
+
+                @pl.when(behind)
+                def _():
+                    target[...] = (mine[...].astype(jnp.float32) + self.receive(piece, slot)).astype(acc.dtype)
+
+                if not self.stages:
+
+                    @pl.when(jnp.logical_not(behind))
+                    def _():
+                        target[...] = mine[...]
+
+                to = self.line_slots + self.size if side < 0 and j == 1 else slot
+                index = self.line_slots + 2 * j + (side > 0) - 2
+                self.send(target, piece, index, to, self.on_line(side), (inside,))
+
+    def end(self, piece):
+        src, acc, box, outs, cols, _, _ = piece
+        held = acc if self.stages else src
+        total = self.shard(held, self.me, cols)[...].astype(jnp.float32)
+        width = total.shape[1] // len(outs)
+        for i, out in enumerate(outs):
+            out[...] = total[:, i * width : (i + 1) * width]
+        for condition, slot in (
+            (self.place > 0, self.line_slots + self.place),
+            (self.place + 1 < self.size, self.line_slots + self.size),
+        ):
+
+            @pl.when(condition)
+            def _():
+                more = self.receive(piece, slot)
                 for i, out in enumerate(outs):
-                    out[...] = total[:, i * width : (i + 1) * width]
+                    out[...] = out[...] + more[:, i * width : (i + 1) * width]
 
 
 BACK_BUFFERS = 20
@@ -716,7 +815,6 @@
     rows = got.shape[2]
     lanes = lanes_at(mp, half)
     far = sorted(offsets_in(grid, range(depth))[1:], key=sum, reverse=True)
-    first, second = ordered
     own, to_partner = [], []
 
     exchange = []
@@ -754,15 +852,13 @@
     patch_grad = small[6:7]
     d_tail = exact(jnp.broadcast_to(patch_grad, (8, patch_grad.shape[1])), patch_w[...], NT)[:1]
 
-    for t in range(depth):
-        for piece in first:
+    for t in range(scatter.stages):
+        for piece in ordered:
             scatter.add(t, piece)
-            if t + 1 < depth:
+            if t + 1 < scatter.stages:
                 scatter.start(t + 1, piece)
-        for piece in second:
-            scatter.add(t, piece)
-            if t + 1 < depth:
-                scatter.start(t + 1, piece)
+    for piece in ordered:
+        scatter.pass_on(piece, scatter.size - 1)
 
     bias_half[...] = jnp.zeros_like(bias_half)
 
@@ -827,10 +923,17 @@
     for k in range(1, n):
         there = lax.rem(me + k, n)
         back.append(remote(blocks_o.at[me], blocks_o.at[me], b_send.at[k - 1], b_recv.at[k - 1], (there, mp)))
+    for j in reversed(range(1, scatter.size - 1)):
+        for piece in ordered:
+            scatter.pass_on(piece, j)
+    for piece in ordered:
+        scatter.end(piece)
     for copy in back + to_partner:
         copy.wait()
-    for copy in sums + exchange + scatter.sends:
+    for copy in sums + exchange:
         copy.wait_send()
+    for conditions, box, cols, p, i in scatter.sends:
+        under(conditions, lambda: arrived(box.at[0, :, cols], scatter.send_sem.at[p, i]))
     for copy in own[1:]:
         copy.wait()
 
@@ -873,11 +976,12 @@
 
 def scatter_buffers(n, grid, rows, attn_lanes, mlp_lanes):
     low, pieces = jnp.bfloat16, 2 * len(orders_of(grid))
+    slots = n - grid[0] + grid[0] + 1
     return [
-        pltpu.VMEM((n - 1, rows, attn_lanes), low),
-        pltpu.VMEM((n - 1, rows, mlp_lanes), low),
-        pltpu.SemaphoreType.DMA((pieces, n - 1)),
-        pltpu.SemaphoreType.DMA((pieces, n - 1)),
+        pltpu.VMEM((slots, rows, attn_lanes), low),
+        pltpu.VMEM((slots, rows, mlp_lanes), low),
+        pltpu.SemaphoreType.DMA((pieces, slots + grid[0])),
+        pltpu.SemaphoreType.DMA((pieces, slots)),
     ]
 
 
@@ -909,7 +1013,8 @@
 
     def begin(pieces):
         for piece in pieces:
-            scatter.start(0, piece)
+            if scatter.stages:
+                scatter.start(0, piece)
 
     finish = layer_body(
         inner, lambda: begin(mlp_pieces), lambda: begin(attn_pieces), *ins[:LAYER_INS],
@@ -929,7 +1034,7 @@
         return d_kern.at[:, pl.ds(pl.multiple_of(rows * there, 16), rows)]
 
     back_body(
-        n, grid, scatter, (mlp_pieces, attn_pieces), finish, block_for,
+        n, grid, scatter, mlp_pieces + attn_pieces, finish, block_for,
         pix, kern, band_mask, emb_grad, small, small_up, small_in, patch_w, *outs[7:], *back[:8], load, *back[9:],
     )
 
@@ -953,9 +1058,10 @@
         n, grid, attn.shape[1], attn, mlp, attn_acc, mlp_acc, attn_box, mlp_box, outs[:6], g_send, g_recv
     )
     for piece in scatter.pieces:
-        scatter.start(0, piece)
+        if scatter.stages:
+            scatter.start(0, piece)
     back_body(
-        n, grid, scatter, (scatter.pieces, []), lambda: None, lambda there: d_kern.at[there],
+        n, grid, scatter, scatter.pieces, lambda: None, lambda there: d_kern.at[there],
         pix, kern, band_mask, emb_grad, small, small_up, small_in, patch_w, *outs[6:], *back[:8], load, *back[9:],
     )
 
@@ -1025,7 +1131,7 @@
     n, bands, per_slot, recompute,
     blocks, codes, facts, rows_k, wide_k, prob_k, w_attn, w_in, w_out, gain, shift, patch_w, local_grad,
     g_attn, g_in, g_out, g_gain, g_shift, g_token, g_patch, g_kern, n_gain, n_shift, in_bias, out_bias, up_bias, down_bias,
-    rows_s, wide_s, prob_s, d_mlp, tails, got, got32, made, sem, store,
+    rows_s, wide_s, prob_s, d_mlp, tails, turned, got, got32, made, sem, store,
 ):
     low = jnp.bfloat16
     rows, half = got.shape[3], got.shape[4]
@@ -1035,6 +1141,8 @@
         loads.append(pltpu.make_async_copy(local_grad.at[i], got.at[i], sem.at[i]))
         loads[-1].start()
 
+    turned[...] = codes[...].T
+
     stores = []
     for i in range(2):
         loads[i].wait()
@@ -1048,10 +1156,10 @@
         g_rows = got32.reshape(n * SPAN * step, half)
         m_rows = made.at[i].reshape(made.shape[1] * step, half)
 
-        @pl.loop(0, rows // 2)
+        @pl.loop(0, rows // 2, unroll=3)
         def _(j):
             taken = [g_rows[pl.ds(2 * j + c, n * SPAN, stride=step), :].astype(low) for c in range(2)]
-            both = dot(codes[...], jnp.concatenate(taken, axis=1), TN)
+            both = dot(turned[...], jnp.concatenate(taken, axis=1), NN)
             for c in range(2):
                 m_rows[pl.ds(2 * j + c, made.shape[1], stride=step), :] = both[:, c * half : (c + 1) * half]
 
@@ -1119,6 +1227,7 @@
         + [
             pltpu.VMEM((2, GROUP * SPAN, hyper_width), f32),
             pltpu.VMEM((n, hyper_width), f32),
+            pltpu.VMEM((hyper_width, n * SPAN), jnp.bfloat16),
             pltpu.VMEM(local_grad.shape, local_grad.dtype),
             pltpu.VMEM((n, SPAN, tiled(rows), half), f32),
             pltpu.VMEM((2, hyper_width, tiled(rows), half), f32),

time: 367 us -> 318 us (0.87)
  Pallas kernels: 335 us -> 282 us
    pallas_call x1, Pallas kernels: 186 us -> 155 us  [layer_and_back(): pl.pallas_call(partial(whole_kernel, n, grid, inner), out_shape=[shape((t...]
    pallas_call x1, Pallas kernels: 32.5 us -> 21.9 us  [tail(): pl.pallas_call(partial(tail_kernel, n, bands, per_slot, recompute), out_s...]
    pallas_call x1, Pallas kernels: 116 us -> 106 us  [front(): pl.pallas_call(partial(front_kernel, n, grid, direct, bands), out_shape=[...]
where the time goes in v3:
time: 318 us; the launch traced here: 313 us
  Pallas kernels  282 us (89%)
  other arithmetic  14.9 us (5%)
  local copies, waits for them, and re-layouts  14.1 us (4%)
    pallas_call x1, Pallas kernels, layer_and_back(): pl.pallas_call(partial(whole_kernel, n, grid, inner), out_shape=[shape((t...  155 us
    pallas_call x1, Pallas kernels, front(): pl.pallas_call(partial(front_kernel, n, grid, direct, bands), out_shape=[...  106 us
    pallas_call x1, Pallas kernels, tail(): pl.pallas_call(partial(tail_kernel, n, bands, per_slot, recompute), out_s...  21.9 us

profile of v3, /device:TPU:0, one launch (start us, length us, event | category | flops | bytes accessed | tf_op | source)
XLA Modules:
  0.0 313.4 jit_solution(17691285523167570460)
XLA Ops:
  0.7 0.0 copy-start
  2.1 0.7 convert_bitcast_fusion
  2.8 0.1 pad.18.clone
  2.9 1.2 and_convert_fusion.refs_6_
  4.1 1.3 broadcast_in_dim.45.refs_12_
  5.4 1.3 broadcast_in_dim.47.refs_14_
  6.6 0.8 slice_reduce_fusion.1
  7.4 0.6 broadcast_in_dim.44.refs_11_
  8.0 1.3 broadcast_in_dim.46.refs_13_
  9.3 0.7 broadcast_in_dim.42.refs_5_
  10.0 0.1 multiply_sine_fusion
  10.1 0.7 select_maximum_fusion
  10.9 0.7 pad_maximum_fusion.3.facts_own
  11.5 0.9 convert.21
  12.4 0.9 convert.20
  13.4 0.7 pad_maximum_fusion.2.attn
  14.1 0.7 fusion.refs_7_
  14.7 1.0 convert.22
  15.7 1.0 convert.23
  16.7 0.7 pad_maximum_fusion.mlp
  17.4 0.0 copy-done
  17.4 1.1 dynamic-slice_bitcast_fusion.refs_0_
  18.5 105.8 %front.1 = (bf16[13,768,128]{2,1,0:T(8,128)(2,1)}, bf16[16,48,1536]{2,1,0:T(8,128)(2,1)}, bf16[16,48,3072]{2,1,0:T(8,128)(2,1)}, f32[16,32,128]{2,1,0:T(8,128)},...) custom-call(f32[32,128]{1,0:T(8,128)} %pad_maximum_fusion.3.facts_ow, ...), custom_call_target="tpu_custom_call" | custom-call | tf_op jit(solution)/shard_map/front/pallas_call | solution.py:438
  124.3 1.3 slice.24.refs_8_
  125.6 154.6 %layer.1 = (bf16[256,768]{1,0:T(8,128)(2,1)}, f32[48,384]{1,0:T(8,128)}, f32[48,384]{1,0:T(8,128)}, f32[48,384]{1,0:T(8,128)}, f32[48,384]{1,0:T(8,128)}, /*inde...) custom-call(bf16[13,256,128]{2,1,0:T(8,128)(2,1)} %dynamic-slice_bit, ...), custom_call_target="tpu_custom_call" | custom-call | flops 10116661248 | bytes 30000000 | tf_op jit(solution)/shard_map/layer/pallas_call | solution.py:1091
  280.2 1.7 pad_maximum_fusion.1
  281.8 0.0 copy-start.1
  281.8 21.9 %tail.1 = (f32[4,128,128]{2,1,0:T(8,128)}, f32[128,2048]{1,0:T(8,128)}, f32[2048,128]{1,0:T(8,128)}, f32[2,128]{1,0:T(2,128)}, f32[2,128]{1,0:T(2,128)}, /*index...) custom-call(f32[16,32,128]{2,1,0:T(8,128)} %get-tuple-element.61.blo, ...), custom_call_target="tpu_custom_call" | custom-call | tf_op jit(solution)/shard_map/tail/pallas_call | solution.py:1221
  303.8 0.0 copy-start.5
  303.8 0.0 copy-start.4
  303.8 1.3 reduce.2
  305.1 1.3 reduce.4
  306.4 1.3 reduce.3
  307.7 0.0 copy-start.3
  307.7 0.0 copy-start.2
  307.7 1.8 copy.54
  309.6 0.0 copy-done.1
  309.6 1.2 copy.55
  310.7 0.0 copy-done.5
  310.8 0.6 copy.56
  311.4 0.0 copy-done.4
  311.4 0.6 copy.57
  312.0 0.0 copy-done.3
  312.0 0.7 copy.58
  312.7 0.0 copy-done.2
  312.7 0.7 copy.59
  (5 shorter events, 0.0 us)
Async XLA Ops:
  0.7 16.8 %copy-start = (bf16[1,13,256,256]{3,2,1,0:T(8,128)(2,1)S(1)}, bf16[1,13,256,256]{3,2,1,0:T(8,128)(2,1)}, u32[]{:S(2)}) copy-start(bf16[1,13,256,256]{3,2,1,0:T(8,128)(2,1)} %param.25) | copy-start | bytes 5111812
  281.8 27.7 %copy-start.1 = (bf16[13,256,256]{2,1,0:T(8,128)(2,1)S(1)}, bf16[13,256,256]{2,1,0:T(8,128)(2,1)}, u32[]{:S(2)}) copy-start(bf16[13,256,256]{2,1,0:T(8,128)(2,1)} %get-tuple-element.60) | copy-start | bytes 5111812
  303.8 7.0 %copy-start.5 = (f32[48,256]{1,0:T(8,128)S(1)}, f32[48,256]{1,0:T(8,128)}, u32[]{:S(2)}) copy-start(f32[48,256]{1,0:T(8,128)} %get-tuple-element.128) | copy-start | bytes 147460
  303.8 7.6 %copy-start.4 = (f32[48,384]{1,0:T(8,128)S(1)}, f32[48,384]{1,0:T(8,128)}, u32[]{:S(2)}) copy-start(f32[48,384]{1,0:T(8,128)} %get-tuple-element.134) | copy-start | bytes 221188
  307.7 4.3 %copy-start.3 = (f32[48,1536]{1,0:T(8,128)S(1)}, f32[48,1536]{1,0:T(8,128)}, u32[]{:S(2)}) copy-start(f32[48,1536]{1,0:T(8,128)} %get-tuple-element.136) | copy-start | bytes 884740
  307.7 5.0 %copy-start.2 = (f32[48,1536]{1,0:T(8,128)S(1)}, f32[48,1536]{1,0:T(8,128)}, u32[]{:S(2)}) copy-start(f32[48,1536]{1,0:T(8,128)} %get-tuple-element.138) | copy-start | bytes 884740

commit v4 on v2

v4 whole, which is shorter than its diff:
```python
from functools import partial
import math

import jax
import jax.numpy as jnp
import numpy as np
from jax import lax
from jax.experimental import pallas as pl
from jax.experimental.pallas import tpu as pltpu
from jax.sharding import PartitionSpec as P

HEAD_DIM = 64
HYP_HEADS = 4
MESH = pl.DeviceIdType.MESH
ANY = pl.BlockSpec(memory_space=pl.ANY)
VMEM = pl.BlockSpec(memory_space=pltpu.VMEM)
BIG_VMEM = 61 * 1024 * 1024

vit_epsilon = 1e-06
hyper_epsilon = 1e-05


def factors_of(n):
    return {16: (2, 2, 2, 2), 128: (2, 2, 8, 4)}.get(n, (n,))


def coords(me, grid):
    out = []
    for size in reversed(grid):
        out.append(lax.rem(me, size))
        me = me // size
    return out[::-1]


def device_at(position, grid, offset):
    index = 0
    for place, size, step in zip(position, grid, offset):
        index = index * size + (lax.rem(place + step, size) if step else place)
    return index


def offsets_in(grid, dims):
    out = [()]
    for dim, size in enumerate(grid):
        out = [o + (i,) for o in out for i in range(size if dim in dims else 1)]
    return out


def along(grid, dim, step):
    return tuple(step if d == dim else 0 for d in range(len(grid)))


def minus(a, b, grid):
    return tuple((i - j) % size for i, j, size in zip(a, b, grid))


def orders_of(grid):
    dims = tuple(range(len(grid)))
    return [dims, dims[:-2] + (dims[-1], dims[-2])] if len(grid) > 2 else [dims]


def greet(n, me, mp, both):
    sem = pltpu.get_barrier_semaphore()
    for k in range(1, n):
        pl.semaphore_signal(sem, inc=1, device_id=(lax.rem(me + k, n), mp), device_id_type=MESH)
    if both:
        for k in range(n):
            pl.semaphore_signal(sem, inc=1, device_id=(lax.rem(me + k, n), 1 - mp), device_id_type=MESH)
    pl.semaphore_wait(sem, 2 * n - 1 if both else n - 1)


def remote(src, dst, send, recv, device):
    copy = pltpu.make_async_remote_copy(
        src_ref=src, dst_ref=dst, send_sem=send, recv_sem=recv, device_id=device, device_id_type=MESH
    )
    copy.start()
    return copy


def params(collective, limit=None):
    return pltpu.CompilerParams(collective_id=collective, has_side_effects=True, vmem_limit_bytes=limit)


NN, NT, TN = ((1,), (0,)), ((1,), (1,)), ((0,), (0,))
GROUP = 16
SPAN = 16


def dot(a, b, contract):
    return lax.dot_general(a, b, (contract, ((), ())), preferred_element_type=jnp.float32)


def exact(a, b, contract=NN):
    return lax.dot_general(
        a, b, (contract, ((), ())), precision=lax.Precision.HIGH, preferred_element_type=jnp.float32
    )


def lanes_at(i, width):
    return pl.ds(pl.multiple_of(i * width, width), width)


def row_mean(x):
    return jnp.mean(x, axis=-1, keepdims=True)


def row_sum(x):
    return jnp.sum(x, axis=-1, keepdims=True)


def all_rows(x):
    return jnp.sum(x, axis=0, keepdims=True)


def column_sums(x):
    return dot(jnp.ones((8, x.shape[0]), x.dtype), x, NN)[:1]


def normal_parts(x):
    return 0.5 + 0.5 * lax.erf(x * math.sqrt(0.5)), jnp.exp(-0.5 * x * x) * (1.0 / math.sqrt(2.0 * math.pi))


def normed(x, epsilon):
    center = x - row_mean(x)
    r = lax.rsqrt(row_mean(center * center) + epsilon)
    return center * r, r


def norm_back(hat, r, d_y, gain_row):
    u = d_y * gain_row
    return r * (u - row_mean(u) - hat * row_mean(u * hat)), all_rows(d_y * hat), all_rows(d_y)


def tiled(rows):
    return -(-rows // 8) * 8


def first_rows(ref, rows):
    return ref if ref.shape[-2] == rows else ref.at[:, pl.ds(0, rows)]


def arrived(block, sem):
    pltpu.make_async_copy(block, block, sem).wait()


class Refs:
    def __init__(self, names, refs):
        for name, ref in zip(names, refs, strict=True):
            setattr(self, name, ref)


SEQ, QUERY, KEY, VALUE, MIXED, HAT_A, FIRST, HAT_B, SECOND, SCALE_A, SCALE_B = range(11)


def head_masks(width):
    lane = lax.broadcasted_iota(jnp.int32, (1, width), 1)
    size = width // HYP_HEADS
    return [((lane >= h * size) & (lane < (h + 1) * size)).astype(jnp.float32) for h in range(HYP_HEADS)]


def wave_rows(waves, count):
    bands = len(waves)
    row = lax.broadcasted_iota(jnp.int32, (SPAN, 128), 0)
    values = jnp.zeros((SPAN, 128), jnp.float32)
    for b, wave in enumerate(waves):
        values = jnp.where(row == b, wave.astype(jnp.float32), values)
    return jnp.where(row < jnp.minimum(count, bands), values, -values).astype(jnp.bfloat16)


def generator_forward(bands, facts, frequency, token, g, w_attn, w_in, w_out, gain, shift, rows, wide, prob):
    count, width = GROUP * SPAN, facts.shape[-1]
    waves = facts[pl.ds(g * GROUP, GROUP)].astype(jnp.float32).reshape(count, width)
    angles = jnp.abs(waves) * frequency[...]
    lane = lax.broadcasted_iota(jnp.int32, (count, width), 1)
    row = lax.rem(lax.broadcasted_iota(jnp.int32, (count, width), 0), SPAN)
    embedding = jnp.where(lane < width // 2, jnp.sin(angles), jnp.cos(angles))
    last = jnp.where(row == bands, token[...].reshape(1, width), 0.0)
    seq = jnp.where(row < bands, embedding, last)
    valid = ((waves > 0.0) | (row == bands)).astype(jnp.float32)
    columns = dot(jnp.ones((8, width), jnp.bfloat16), valid.astype(jnp.bfloat16), NT)[:1]
    slot = [lax.shift_right_logical(lax.broadcasted_iota(jnp.int32, (count, count), d), 4) for d in range(2)]
    allowed = (slot[0] == slot[1]) & (columns > 0.5)
    rows[SEQ] = seq
    for i in range(3):
        rows[QUERY + i] = exact(seq, w_attn[i])
    scale = 1.0 / math.sqrt(width // HYP_HEADS)
    mixed = jnp.zeros((count, width), jnp.float32)
    for h, mask in enumerate(head_masks(width)):
        scores = jnp.where(allowed, exact(rows[QUERY] * mask, rows[KEY], NT) * scale, -1e30)
        raised = jnp.exp(scores - jnp.max(scores, axis=-1, keepdims=True))
        weights = raised / row_sum(raised)
        prob[h] = weights
        mixed = mixed + exact(weights, rows[VALUE] * mask)
    rows[MIXED] = mixed
    hat, r = normed(seq + exact(mixed, w_attn[3]), hyper_epsilon)
    rows[HAT_A] = hat
    rows[SCALE_A] = jnp.broadcast_to(r, (count, width))
    rows[FIRST] = hat * gain[0:1] + shift[0:1]
    tile = 512

    @pl.loop(0, w_in.shape[1] // tile)
    def _(j):
        cols = lanes_at(j, tile)
        pre = exact(rows[FIRST], w_in[:, cols])
        phi, density = normal_parts(pre)
        wide[0, :, cols] = pre * phi
        wide[1, :, cols] = phi + pre * density

    rows[SECOND] = rows[FIRST]

    @pl.loop(0, w_in.shape[1] // tile)
    def _(j):
        cols = lanes_at(j, tile)
        rows[SECOND] = rows[SECOND] + exact(wide[0, :, cols], w_out[cols])

    hat, r = normed(rows[SECOND], hyper_epsilon)
    rows[HAT_B] = hat
    rows[SCALE_B] = jnp.broadcast_to(r, (count, width))
    rows[SECOND] = hat * gain[1:2] + shift[1:2]


def generator_backward(d_second, put, w_attn, w_in, w_out, gain, rows, wide, prob, d_mlp, outs):
    g_attn, g_in, g_out, g_gain, g_shift = outs
    width = d_second.shape[1]
    d_sum, gain_b, shift_b = norm_back(rows[HAT_B], rows[SCALE_B], d_second, gain[1:2])
    put(g_gain, slice(1, 2), gain_b)
    put(g_shift, slice(1, 2), shift_b)
    d_mlp[0] = d_sum
    d_mlp[1] = d_sum
    tile = 512

    @pl.loop(0, w_in.shape[1] // tile)
    def _(j):
        cols = lanes_at(j, tile)
        put(g_out, cols, exact(wide[0, :, cols], d_mlp[0], TN))
        d_pre = exact(d_mlp[0], w_out[cols], NT) * wide[1, :, cols]
        put(g_in, (slice(None), cols), exact(rows[FIRST], d_pre, TN))
        d_mlp[1] = d_mlp[1] + exact(d_pre, w_in[:, cols], NT)

    d_res, gain_a, shift_a = norm_back(rows[HAT_A], rows[SCALE_A], d_mlp[1], gain[0:1])
    put(g_gain, slice(0, 1), gain_a)
    put(g_shift, slice(0, 1), shift_a)
    put(g_attn, 3, exact(rows[MIXED], d_res, TN))
    d_mixed = exact(d_res, w_attn[3], NT)
    scale = 1.0 / math.sqrt(width // HYP_HEADS)
    d_q = jnp.zeros_like(d_res)
    d_k, d_v = d_q, d_q
    for h, mask in enumerate(head_masks(width)):
        p, d_m = prob[h], d_mixed * mask
        d_p = exact(d_m, rows[VALUE], NT)
        d_s = p * (d_p - row_sum(p * d_p)) * scale
        d_q = d_q + exact(d_s, rows[KEY] * mask)
        d_k = d_k + exact(d_s, rows[QUERY] * mask, TN)
        d_v = d_v + exact(p, d_m, TN)
    d_seq = d_res
    for i, grad in enumerate((d_q, d_k, d_v)):
        put(g_attn, i, exact(rows[SEQ], grad, TN))
        d_seq = d_seq + exact(grad, w_attn[i], NT)
    d_mlp[0] = d_seq


def generator_scratch(width, units):
    f32, count = jnp.float32, GROUP * SPAN
    return [(11, count, width), (2, count, units), (HYP_HEADS, count, count)], f32


def shard_of(ref, owner, rows, cols):
    if len(ref.shape) == 2:
        return ref.at[pl.ds(pl.multiple_of(rows * owner, 16), rows), cols]
    return ref.at[owner, :, cols]


class Gather:
    def __init__(self, grid, rows, arrays, send, recv):
        self.me, self.mp = lax.axis_index("dp"), lax.axis_index("mp")
        self.grid, self.rows, self.here = grid, rows, coords(self.me, grid)
        self.send_sem, self.recv_sem, self.sends = send, recv, {}
        self.pieces = []
        orders = orders_of(grid)
        for array in arrays:
            width = array.shape[-1] // len(orders)
            for i, order in enumerate(orders):
                self.sends[len(self.pieces)] = []
                self.pieces.append((array, pl.ds(i * width, width), order, len(self.pieces)))

    def pass_on(self, piece, owner, number):
        array, cols, order, p = piece
        block = shard_of(array, owner, self.rows, cols)
        for dim in order[number:]:
            for k in range(1, self.grid[dim]):
                there = device_at(self.here, self.grid, along(self.grid, dim, k))
                sem = self.send_sem.at[p, len(self.sends[p])]
                self.sends[p].append(remote(block, block, sem, self.recv_sem.at[p, owner], (there, self.mp)))

    def begin(self, piece):
        self.pass_on(piece, self.me, 0)

    def step(self, piece, number):
        array, cols, order, p = piece
        for offset in offsets_in(self.grid, order[:number]):
            if offset[order[number - 1]]:
                owner = device_at(self.here, self.grid, offset)
                arrived(shard_of(array, owner, self.rows, cols), self.recv_sem.at[p, owner])
                self.pass_on(piece, owner, number)

    def sent(self, pieces):
        for piece in pieces:
            for copy in self.sends[piece[3]]:
                copy.wait_send()


class Exchange:
    def __init__(self, n, grid, blocks, slot, send, recv, own_sem):
        self.me, self.mp = lax.axis_index("dp"), lax.axis_index("mp")
        self.blocks, self.slot, self.sends = blocks, slot, []
        self.send_sem, self.recv_sem, self.own_sem = send, recv, own_sem
        self.grid, self.here = grid, coords(self.me, grid)
        self.near_first = sorted(offsets_in(grid, range(len(grid)))[1:], key=sum)

    def start(self):
        for i, away in enumerate(reversed(self.near_first)):
            there = device_at(self.here, self.grid, away)
            block = self.blocks.at[there]
            self.sends.append(
                remote(block, self.slot(self.me), self.send_sem.at[i], self.recv_sem.at[self.me], (there, self.mp))
            )
        self.own = pltpu.make_async_copy(self.blocks.at[self.me], self.slot(self.me), self.own_sem)
        self.own.start()

    def sources(self):
        for away in self.near_first:
            yield device_at(self.here, self.grid, away)

    def arrive(self, source):
        arrived(self.slot(source), self.recv_sem.at[source])

    def sent(self):
        for copy in self.sends:
            copy.wait_send()


def exchange_sems(n):
    dma = pltpu.SemaphoreType.DMA
    return [dma((n - 1,)), dma((n,)), dma]


class Front:
    def __init__(self, n, grid, bands, facts, frequency, token, w_half, b_half, k32, k16):
        self.n, self.grid, self.bands, self.facts = n, grid, bands, facts
        self.frequency, self.token = frequency, token
        self.w_half, self.b_half, self.k32, self.k16 = w_half, b_half, k32, k16
        self.me, self.mp = lax.axis_index("dp"), lax.axis_index("mp")
        self.shares = []

    def share(self, facts_own, send, recv):
        for k in range(1, self.n):
            there = (lax.rem(self.me + k, self.n), self.mp)
            self.shares.append(remote(facts_own, self.facts.at[self.me], send.at[k - 1], recv.at[k - 1], there))
        self.facts[self.me] = facts_own[...]

    def generate(self, weights, patch_w, second, codes, patch, kept):
        for copy in self.shares:
            copy.wait_recv()
        count = GROUP * SPAN
        position = lax.broadcasted_iota(jnp.int32, (count, self.facts.shape[-1]), 0)
        is_band = lax.rem(position, SPAN) < self.bands
        for g in range(self.n // GROUP):
            generator_forward(self.bands, self.facts, self.frequency, self.token, g, *weights, *kept)
            group = pl.ds(g * count, count)
            second[group] = kept[0][SECOND]
            codes[group] = jnp.where(is_band, kept[0][SECOND] + kept[0][SEQ], 0.0).astype(codes.dtype)
        own = second[pl.ds(pl.multiple_of(self.me * SPAN, SPAN), SPAN)]
        patch[...] = exact(own, patch_w[...])[self.bands : self.bands + 1]

    def make(self, codes, rows):
        n, half, low = self.n, self.w_half.shape[2], jnp.bfloat16
        step = tiled(rows)
        w_rows = self.w_half.reshape(self.w_half.shape[0] * step, half)
        k_rows = self.k32.reshape(n * SPAN * step, half)

        @pl.loop(0, rows // 2)
        def _(j):
            both = [w_rows[pl.ds(2 * j + i, self.w_half.shape[0], stride=step), :].astype(low) for i in range(2)]
            made = dot(codes[...], jnp.concatenate(both, axis=1), NN)
            for i in range(2):
                c = 2 * j + i
                bias = self.b_half[pl.ds(c, 1)]
                k_rows[pl.ds(c, n * SPAN, stride=step), :] = made[:, i * half : (i + 1) * half] + bias

    def ready(self, rows):
        @pl.loop(0, self.n)
        def _(t):
            self.k16[t] = self.k32[t, : self.bands, :rows].astype(self.k16.dtype)

    def sent(self):
        for copy in self.shares:
            copy.wait_send()


def front_kernel(
    n, grid, bands,
    facts_own, frequency, token, w_attn, w_in, w_out, gain, shift, patch_w, kern_w, kern_b, attn, mlp,
    kern_o, attn_o, mlp_o, facts, patch_o, codes_o, rows_o, wide_o, prob_o,
    second, w_half, b_half, k32, k16, local, f_send, f_recv, g_send, g_recv, *a_sems,
):
    me, mp = lax.axis_index("dp"), lax.axis_index("mp")
    rows, half = kern_w.shape[1], kern_w.shape[2] // 2
    load = weight_load(kern_w, w_half, local.at[0], mp)
    own = [
        pltpu.make_async_copy(attn, attn_o.at[me], local.at[1]),
        pltpu.make_async_copy(mlp, mlp_o.at[me], local.at[2]),
    ]
    for copy in own:
        copy.start()
    greet(n, me, mp, False)
    for copy in own:
        copy.wait()
    work = Front(n, grid, bands, facts, frequency, token, w_half, b_half, k32, k16)
    work.share(facts_own, f_send, f_recv)
    gather = Gather(grid, rows, (attn_o, mlp_o), g_send, g_recv)
    for piece in gather.pieces:
        gather.begin(piece)
    work.generate((w_attn, w_in, w_out, gain, shift), patch_w, second, codes_o, patch_o, (rows_o, wide_o, prob_o))
    load.wait()
    b_half[...] = kern_b[:, lanes_at(mp, half)]
    work.make(codes_o, rows)
    work.ready(rows)
    exchange = Exchange(n, grid, k16, lambda source: kern_o.at[source], *a_sems)
    exchange.start()
    for number in range(1, len(grid) + 1):
        for piece in gather.pieces:
            gather.step(piece, number)
    gather.sent(gather.pieces)
    for source in exchange.sources():
        exchange.arrive(source)
    exchange.own.wait()
    exchange.sent()
    work.sent()


def front(n, bands, facts_own, frequency, token, w_attn, w_in, w_out, gain, shift, patch_w, kern_w, kern_b, attn, mlp):
    grid = factors_of(n)
    hyper_width, rows, pixels = kern_w.shape
    half = pixels // 2
    pieces = 2 * len(orders_of(grid))
    f32, low = jnp.float32, jnp.bfloat16
    kept, _ = generator_scratch(hyper_width, w_in.shape[1])
    shapes = [
        ((n, bands, rows, half), low),
        ((n,) + attn.shape, low),
        ((n,) + mlp.shape, low),
        ((n,) + facts_own.shape, low),
        ((1, patch_w.shape[1]), f32),
        ((n * SPAN, hyper_width), low),
    ] + [(k, f32) for k in kept]
    out = pl.pallas_call(
        partial(front_kernel, n, grid, bands),
        out_shape=[jax.ShapeDtypeStruct(*s) for s in shapes],
        in_specs=[VMEM] * 9 + [ANY, VMEM, ANY, ANY],
        out_specs=[ANY] * 3 + [VMEM] * 6,
        scratch_shapes=[
            pltpu.VMEM((n * SPAN, hyper_width), f32),
            pltpu.VMEM((hyper_width, tiled(rows), half), f32),
            pltpu.VMEM((rows, half), f32),
            pltpu.VMEM((n, SPAN, tiled(rows), half), f32),
            pltpu.VMEM((n, bands, rows, half), low),
            pltpu.SemaphoreType.DMA((3,)),
            pltpu.SemaphoreType.DMA((n - 1,)),
            pltpu.SemaphoreType.DMA((n - 1,)),
            pltpu.SemaphoreType.DMA((pieces, n - 1)),
            pltpu.SemaphoreType.DMA((pieces, n)),
        ]
        + exchange_sems(n),
        compiler_params=params(1, BIG_VMEM),
        name="front",
    )(facts_own, frequency, token, w_attn, w_in, w_out, gain, shift, patch_w, kern_w, kern_b, attn, mlp)
    kernel = out[0].transpose(1, 0, 2, 3).reshape(bands, rows * n, half)
    return [kernel, out[1].reshape(n * rows, -1), out[2].reshape(n * rows, -1)] + list(out[3:])


def layer_body(
    inner, hook,
    pix, kern, attn, mlp, cot, band_mask, key_mask, row_scale, patch_bias, gains, shifts, in_bias, out_bias, up_bias, down_bias,
    out_o, emb_grad_o, attn_grad, mlp_grad, small_o, small_up_o, small_in_o,
    emb, mid, part, inbox, norm_a, norm_b, qkv, prob, ctx, act, slope, d_out, d_pre, d_mid, d_att, d_ctx, d_qkv, turned, send, recv,
):
    me, mp = lax.axis_index("dp"), lax.axis_index("mp")
    partner = (me, 1 - mp)
    low = jnp.bfloat16
    bands, tokens, _ = pix.shape
    width = emb.shape[1]
    units = act.shape[1]
    halves = 2
    span = tokens // halves
    tile = 256
    copies = {}

    def swap(i, compute):
        for h in range(halves):
            r = pl.ds(h * span, span)
            if i >= 3:
                copies[i - 3, h].wait_send()

            @pl.loop(0, width // tile)
            def _(j):
                part[i % 3, r, lanes_at(j, tile)] = compute(r, j)

            copies[i, h] = remote(part.at[i % 3, r], inbox.at[i % 3, r], send.at[i, h], recv.at[i, h], partner)

    def swapped(i, h):
        copies[i, h].wait_recv()
        r = pl.ds(h * span, span)
        return part[i % 3, r] + inbox[i % 3, r]

    def embed_terms(r, j):
        total = jnp.zeros((span, tile), jnp.float32)
        for b in range(0, bands, 2):
            both = range(b, min(b + 2, bands))
            left = jnp.concatenate([pix[i, r] * band_mask[i : i + 1].astype(low) for i in both], axis=1)
            right = jnp.concatenate([kern[i, lanes_at(j, tile)] for i in both], axis=1)
            total = total + dot(left, right, NT)
        return total

    hook("start")
    swap(0, embed_terms)
    hook("embedded")
    d_out[...] = (cot[...].astype(jnp.float32) * row_scale[...]).astype(low)
    turned[0] = d_out[...].T
    for h in range(halves):
        r = pl.ds(h * span, span)
        emb[r] = swapped(0, h) + patch_bias[...]
        hat, _ = normed(emb[r], vit_epsilon)
        norm_a[r] = (hat * gains[0:1] + shifts[0:1]).astype(low)

    @pl.loop(0, 3 * inner // 384)
    def _(j):
        cols = lanes_at(j, 384)
        qkv[:, cols] = (dot(norm_a[...], attn[:, cols], NN) + in_bias[:, cols]).astype(low)

    hook("projected")
    wide = 2 * HEAD_DIM
    lane = lax.broadcasted_iota(jnp.int32, (1, wide), 1)
    in_head = [(lane < HEAD_DIM).astype(low), (lane >= HEAD_DIM).astype(low)]
    scale = 1.0 / math.sqrt(HEAD_DIM)
    pairs = inner // wide

    def head_lanes(j, which):
        return pl.ds(pl.multiple_of(which * inner + j * wide, wide), wide)

    @pl.loop(0, pairs)
    def _(j):
        q, k, v = (qkv[:, head_lanes(j, w)] for w in range(3))
        total = jnp.zeros((tokens, wide), jnp.float32)
        for h in range(2):
            scores = jnp.where(key_mask[...] > 0.0, dot(q * in_head[h], k, NT) * scale, -1e30)
            raised = jnp.exp(scores - jnp.max(scores, axis=-1, keepdims=True))
            p = raised / row_sum(raised)
            prob[2 * j + h] = p
            total = total + dot(p.astype(low), v * in_head[h], NN)
        ctx[:, lanes_at(j, wide)] = total.astype(low)

    def out_terms(r, j):
        return dot(ctx[r], attn[lanes_at(j, tile), pl.ds(3 * inner, inner)], NT)

    swap(1, out_terms)
    hook("attended")
    turned[1] = norm_a[...].T
    for h in range(halves):
        r = pl.ds(h * span, span)
        mid[r] = emb[r] + swapped(1, h) + out_bias[...]
        hat, _ = normed(mid[r], vit_epsilon)
        norm_b[r] = (hat * gains[1:2] + shifts[1:2]).astype(low)

    @pl.loop(0, units // tile)
    def _(j):
        cols = lanes_at(j, tile)
        pre = dot(norm_b[...], mlp[:, cols], NN) + up_bias[:, cols]
        phi, density = normal_parts(pre)
        act[:, cols] = (pre * phi).astype(low)
        slope[:, cols] = phi + pre * density

    def down_terms(r, j):
        return dot(act[r], mlp[lanes_at(j, tile), pl.ds(units, units)], NT)

    @pl.loop(0, units // tile)
    def _(j):
        cols = lanes_at(j, tile)
        d_act = dot(d_out[...], mlp[:, pl.ds(pl.multiple_of(units + j * tile, tile), tile)], NN).astype(low)
        d_pre[:, cols] = (d_act.astype(jnp.float32) * slope[:, cols]).astype(low)

    def up_terms(r, j):
        return dot(d_pre[r], mlp[lanes_at(j, tile), pl.ds(0, units)], NT)

    def weight_grad(turned_ref, x, out, start):
        @pl.loop(0, width // tile)
        def _(i):
            for j in range(x.shape[1] // 384):
                out[lanes_at(i, tile), pl.ds(start + j * 384, 384)] = dot(
                    turned_ref[lanes_at(i, tile)], x[:, j * 384 : (j + 1) * 384], NN
                ).astype(low)

    swap(2, up_terms)
    swap(3, down_terms)
    turned[2] = norm_b[...].T
    hook("before feed")
    weight_grad(turned.at[2], d_pre, mlp_grad, 0)
    weight_grad(turned.at[0], act, mlp_grad, units)
    hook("fed")
    small_up_o[...] = column_sums(d_pre[...])
    small_o[5:6] = column_sums(d_out[...])

    def back_through(x, i, h, which):
        hat, r = normed(x, vit_epsilon)
        return norm_back(hat, r, swapped(i, h), gains[which : which + 1])

    sums = []
    for h in range(halves):
        r = pl.ds(h * span, span)
        d_x, gain, shift = back_through(mid[r], 2, h, 1)
        d_x = d_x + d_out[r].astype(jnp.float32)
        d_mid[r] = d_x
        d_att[r] = d_x.astype(low)
        sums.append((gain, shift))
    small_o[1:2] = sums[0][0] + sums[1][0]
    small_o[3:4] = sums[0][1] + sums[1][1]
    small_o[4:5] = column_sums(d_att[...])

    @pl.loop(0, inner // 384)
    def _(j):
        d_ctx[:, lanes_at(j, 384)] = dot(
            d_att[...], attn[:, pl.ds(pl.multiple_of(3 * inner + j * 384, 384), 384)], NN
        ).astype(low)

    @pl.loop(0, pairs)
    def _(j):
        q, k, v = (qkv[:, head_lanes(j, w)] for w in range(3))
        d_c = d_ctx[:, lanes_at(j, wide)]
        d_q = jnp.zeros((tokens, wide), jnp.float32)
        d_k, d_v = d_q, d_q
        for h in range(2):
            p = prob[2 * j + h]
            d_p = dot(d_c * in_head[h], v, NT)
            d_s = (p * (d_p - row_sum(p * d_p))).astype(low)
            d_q = d_q + dot(d_s, k * in_head[h], NN)
            d_k = d_k + dot(d_s, q * in_head[h], TN)
            d_v = d_v + dot(p.astype(low), d_c * in_head[h], TN)
        d_qkv[:, head_lanes(j, 0)] = (d_q * scale).astype(low)
        d_qkv[:, head_lanes(j, 1)] = (d_k * scale).astype(low)
        d_qkv[:, head_lanes(j, 2)] = d_v.astype(low)

    def in_terms(r, j):
        return dot(d_qkv[r], attn[lanes_at(j, tile), pl.ds(0, 3 * inner)], NT)

    swap(4, in_terms)
    hook("before attention")
    weight_grad(turned.at[1], d_qkv, attn_grad, 0)
    turned[2] = d_att[...].T
    weight_grad(turned.at[2], ctx, attn_grad, 3 * inner)
    hook("attention")
    sums = []
    for h in range(halves):
        r = pl.ds(h * span, span)
        d_x, gain, shift = back_through(emb[r], 4, h, 0)
        emb_grad_o[r] = (d_x + d_mid[r]).astype(low)
        sums.append((gain, shift))
    small_o[0:1] = sums[0][0] + sums[1][0]
    small_o[2:3] = sums[0][1] + sums[1][1]
    small_o[6:7] = column_sums(emb_grad_o[...])
    small_o[7:8] = jnp.zeros((1, width), jnp.float32)
    small_in_o[...] = column_sums(d_qkv[...])

    def finish():
        for h in range(halves):
            r = pl.ds(h * span, span)
            out_o[r] = ((mid[r] + swapped(3, h) + down_bias[...]) * row_scale[r]).astype(low)
        for i in range(2, 5):
            for h in range(halves):
                copies[i, h].wait_send()

    return finish


def layer_buffers(inner, units, tokens, width):
    f32, low = jnp.float32, jnp.bfloat16
    return [
        pltpu.VMEM((tokens, width), f32),
        pltpu.VMEM((tokens, width), f32),
        pltpu.VMEM((3, tokens, width), f32),
        pltpu.VMEM((3, tokens, width), f32),
        pltpu.VMEM((tokens, width), low),
        pltpu.VMEM((tokens, width), low),
        pltpu.VMEM((tokens, 3 * inner), low),
        pltpu.VMEM((inner // HEAD_DIM, tokens, tokens), f32),
        pltpu.VMEM((tokens, inner), low),
        pltpu.VMEM((tokens, units), low),
        pltpu.VMEM((tokens, units), f32),
        pltpu.VMEM((tokens, width), low),
        pltpu.VMEM((tokens, units), low),
        pltpu.VMEM((tokens, width), f32),
        pltpu.VMEM((tokens, width), low),
        pltpu.VMEM((tokens, inner), low),
        pltpu.VMEM((tokens, 3 * inner), low),
        pltpu.VMEM((3, width, tokens), low),
        pltpu.SemaphoreType.DMA((5, 2)),
        pltpu.SemaphoreType.DMA((5, 2)),
    ]


LAYER_INS, LAYER_BUFFERS, TURNED = 15, 20, 17


class Scatter:
    def __init__(self, n, grid, rows, attn, mlp, attn_box, mlp_box, outs, send, recv):
        self.me, self.mp = lax.axis_index("dp"), lax.axis_index("mp")
        self.here, self.grid, self.rows = coords(self.me, grid), grid, rows
        self.orders = [order[::-1] for order in orders_of(grid)]
        self.stages = len(grid)
        self.send_sem, self.recv_sem, self.sends = send, recv, []
        self.pieces = []
        for terms, box, out in ((attn, attn_box, outs[:4]), (mlp, mlp_box, outs[4:])):
            width, share = terms.shape[-1] // len(self.orders), len(out) // len(self.orders)
            for i, order in enumerate(self.orders):
                cols, to = pl.ds(i * width, width), out[i * share : (i + 1) * share]
                self.pieces.append((terms, box, to, cols, order, len(self.pieces)))
        self.slots = {}
        for which, order in enumerate(self.orders):
            number = 0
            for t in range(self.stages):
                for shard in self.rest(order, t):
                    for k in range(1, grid[order[t]]):
                        self.slots[which, t, shard, k] = number
                        number += 1

    def rest(self, order, t):
        return sorted(offsets_in(self.grid, order[t + 1 :]), key=sum, reverse=True)

    def start(self, t, pieces):
        for terms, box, _, cols, order, p in pieces:
            for shard in self.rest(order, t):
                for k in range(1, self.grid[order[t]]):
                    step = along(self.grid, order[t], k)
                    owner = device_at(self.here, self.grid, tuple(i + j for i, j in zip(shard, step)))
                    slot = self.slots[p % len(self.orders), t, shard, self.grid[order[t]] - k]
                    there = (device_at(self.here, self.grid, step), self.mp)
                    block = shard_of(terms, owner, self.rows, cols)
                    self.sends.append(
                        remote(block, box.at[slot, :, cols], self.send_sem.at[p, slot], self.recv_sem.at[p, slot], there)
                    )

    def add(self, t, pieces):
        for terms, box, outs, cols, order, p in pieces:
            for shard in self.rest(order, t):
                block = shard_of(terms, device_at(self.here, self.grid, shard), self.rows, cols)
                total = block[...].astype(jnp.float32)
                for k in range(1, self.grid[order[t]]):
                    slot = self.slots[p % len(self.orders), t, shard, k]
                    arrived(box.at[slot, :, cols], self.recv_sem.at[p, slot])
                    total = total + box[slot, :, cols].astype(jnp.float32)
                if t < self.stages - 1:
                    block[...] = total.astype(terms.dtype)
                else:
                    width = total.shape[1] // len(outs)
                    for i, out in enumerate(outs):
                        out[...] = total[:, i * width : (i + 1) * width]

    def go_on(self, t, pieces):
        if t < self.stages:
            self.add(t, pieces)
            if t + 1 < self.stages:
                self.start(t + 1, pieces)


def generator_gradients(n, bands, recompute, blocks, patch_at, w_attn, w_in, w_out, gain, shift, kept, d_mlp, tails, outs):
    g_attn, g_in, g_out, g_gain, g_shift, g_token, g_patch = outs
    groups = n // GROUP

    def put(ref, where, value):
        ref[where] = value if groups == 1 else ref[where] + value

    if groups > 1:
        for ref in (g_attn, g_in, g_out, g_gain, g_shift):
            ref[...] = jnp.zeros_like(ref)
    width = blocks.shape[2]
    token = jnp.zeros((1, width), jnp.float32)
    for g in range(groups):
        recompute(g)
        d_second = blocks[pl.ds(g * GROUP, GROUP), :SPAN].reshape(GROUP * SPAN, width)
        generator_backward(
            d_second, put, w_attn, w_in, w_out, gain, *kept, d_mlp, (g_attn, g_in, g_out, g_gain, g_shift)
        )
        tails[pl.ds(g * GROUP, GROUP)] = kept[0].at[SECOND][pl.ds(bands, GROUP, stride=SPAN), :]
        token = token + all_rows(d_mlp.at[0][pl.ds(bands, GROUP, stride=SPAN), :])
    g_token[...] = token
    lane = 128
    for i in range(g_patch.shape[1] // lane):
        g_patch[:, i * lane : (i + 1) * lane] = exact(tails[...], blocks[:, patch_at + i, :], TN)


def back_body(
    n, grid, scatter, ordered, finish, gradients, exchange,
    pix, kern, band_mask, emb_grad, small, small_up, small_in, patch_w, codes,
    pixel_o, map_o, blocks_o, bias_o,
    w_half, d_pix, got, got32, code, codes_turned, terms, term_box, vectors, vector_box, bias_half, load, local, f_send, f_recv,
    c_send, c_recv, b_send, b_recv, v_send, v_recv, u_send, u_recv,
):
    me, mp = lax.axis_index("dp"), lax.axis_index("mp")
    partner = (me, 1 - mp)
    low = jnp.bfloat16
    bands, tokens, half = pix.shape
    rows = got.shape[2]
    lanes = lanes_at(mp, half)
    own, to_partner = [], []
    mine, rest = ordered

    exchange.start()
    scatter.start(0, rest)
    scatter.go_on(0, mine)
    finish()

    def pixel_gradients(b, count):
        made = dot(emb_grad[...], jnp.concatenate([kern[b + i] for i in range(count)], axis=1), NN)
        for i in range(count):
            d_pix[b + i] = (made[:, i * half : (i + 1) * half] * band_mask[pl.ds(b + i, 1)]).astype(low)

    pl.loop(0, bands // 2)(lambda j: pixel_gradients(2 * j, 2))
    if bands % 2:
        pixel_gradients(bands - 1, 1)

    own.append(pltpu.make_async_copy(d_pix, pixel_o.at[:, :, lanes], local.at[0]))
    own[-1].start()
    to_partner.append(remote(d_pix, pixel_o.at[:, :, lanes], f_send.at[0], f_recv.at[0], partner))

    lane = 128
    per_slot = vectors.shape[1]
    vectors[...] = jnp.zeros_like(vectors)
    chunks = []
    for r in range(4):
        chunks += [small[r : r + 1, i * lane : (i + 1) * lane] for i in range(small.shape[1] // lane)]
    inner = small_in.shape[1] // 3
    for start in (0, 2 * inner):
        chunks += [small_in[:, start + i * lane : start + (i + 1) * lane] for i in range(inner // lane)]
    chunks += [small[4:5, i * lane : (i + 1) * lane] for i in range(small.shape[1] // lane)]
    chunks += [small_up[:, i * lane : (i + 1) * lane] for i in range(small_up.shape[1] // lane)]
    chunks += [small[5:6, i * lane : (i + 1) * lane] for i in range(small.shape[1] // lane)]
    each = -(-len(chunks) // n)
    for i, chunk in enumerate(chunks):
        vectors[i // each, i % each : i % each + 1] = chunk
    patch_grad = small[6:7]
    d_tail = exact(jnp.broadcast_to(patch_grad, (8, patch_grad.shape[1])), patch_w[...], NT)[:1]
    adding = []
    for k in range(1, n):
        there = lax.rem(me + k, n)
        adding.append(remote(vectors.at[there], vector_box.at[n - k], v_send.at[k], v_recv.at[n - k], (there, mp)))
    codes_turned[...] = codes[...].T

    scatter.go_on(0, rest)
    scatter.go_on(1, mine)
    scatter.go_on(1, rest)

    for copy in adding:
        copy.wait_recv()
    total = vectors[me]
    for k in range(1, n):
        total = total + vector_box[k]
    blocks_o[me, SPAN : SPAN + per_slot] = total
    for i in range(patch_grad.shape[1] // lane):
        r = SPAN + per_slot + i
        blocks_o[me, r : r + 1] = patch_grad[:, i * lane : (i + 1) * lane]
    back = []
    beyond = pl.ds(SPAN, blocks_o.shape[1] - SPAN)
    for k in range(1, n):
        there = lax.rem(me + k, n)
        block = blocks_o.at[me, beyond]
        back.append(remote(block, block, u_send.at[k - 1], u_recv.at[k - 1], (there, mp)))

    bias_half[...] = jnp.zeros_like(bias_half)

    def take(source):
        block = got[source].astype(jnp.float32)
        got32[source, :bands, :rows] = block
        got32[source, bands:, :rows] = jnp.zeros((SPAN - bands,) + block.shape[1:], jnp.float32)
        bias_half[...] = bias_half[...] + jnp.sum(block, axis=0)

    exchange.own.wait()
    take(me)
    for source in exchange.sources():
        exchange.arrive(source)
        take(source)

    if load is not None:
        load.wait()
    step = tiled(rows)
    w_rows = w_half.reshape(w_half.shape[0] * step, half)
    g_rows = got32.reshape(n * SPAN * step, half)
    code[...] = jnp.zeros_like(code)

    @pl.loop(0, rows // 2)
    def _(j):
        taken = [g_rows[pl.ds(2 * j + i, n * SPAN, stride=step), :].astype(low) for i in range(2)]
        weights = [w_rows[pl.ds(2 * j + i, w_half.shape[0], stride=step), :].astype(low) for i in range(2)]
        code[...] = code[...] + dot(jnp.concatenate(taken, axis=1), jnp.concatenate(weights, axis=1), NT)

    terms[...] = code[...].reshape(n, SPAN, code.shape[1]).astype(low)
    sums = []
    for k in range(1, n):
        there = lax.rem(me + k, n)
        slot = n - k
        sums.append(remote(terms.at[there], term_box.at[mp, slot], c_send.at[k], c_recv.at[slot], (there, mp)))
    for k in range(n):
        there = lax.rem(me + k, n)
        slot = (n - k) % n
        sums.append(
            remote(terms.at[there], term_box.at[mp, slot], c_send.at[n + k], c_recv.at[n + slot], (there, 1 - mp))
        )
    term_box[mp, 0] = terms[me]
    bias_o[:, lanes] = bias_half[...]
    to_partner.append(remote(bias_half, bias_o.at[:, lanes], f_send.at[2], f_recv.at[2], partner))

    scatter.go_on(2, mine)
    scatter.go_on(2, rest)
    @pl.loop(0, rows // 2)
    def _(j):
        taken = [g_rows[pl.ds(2 * j + c, n * SPAN, stride=step), :].astype(low) for c in range(2)]
        both = dot(codes_turned[...], jnp.concatenate(taken, axis=1), NN)
        for c in range(2):
            w_rows[pl.ds(2 * j + c, w_half.shape[0], stride=step), :] = both[:, c * half : (c + 1) * half]

    filled = first_rows(w_half, rows)
    to_partner.append(remote(filled, map_o.at[mp], f_send.at[1], f_recv.at[1], partner))
    own.append(pltpu.make_async_copy(filled, map_o.at[mp], local.at[1]))
    own[-1].start()

    for copy in sums:
        copy.wait_recv()
    total = term_box[0, 0].astype(jnp.float32)
    for i in range(1, 2 * n):
        total = total + term_box[i // n, i % n].astype(jnp.float32)
    is_tail = lax.broadcasted_iota(jnp.int32, total.shape, 0) == bands
    blocks_o[me, :SPAN] = jnp.where(is_tail, d_tail, total)
    for k in range(1, n):
        there = lax.rem(me + k, n)
        block = blocks_o.at[me, pl.ds(0, SPAN)]
        back.append(remote(block, block, b_send.at[k - 1], b_recv.at[k - 1], (there, mp)))
    for copy in back:
        copy.wait_recv()
    gradients(blocks_o, SPAN + per_slot)
    for t in range(3, scatter.stages):
        scatter.go_on(t, mine + rest)
    for copy in to_partner:
        copy.wait()
    for copy in sums + adding + back + scatter.sends:
        copy.wait_send()
    exchange.sent()
    for copy in own:
        copy.wait()


GENERATOR_OUTS = tuple(dict(
    g_attn=0, g_in=0, g_out=0, g_gain=0, g_shift=0, g_token=0, g_patch=0,
))


def rows_per_slot(n, width, inner, units):
    chunks = (6 * width + 2 * inner + units) // 128
    return -(-(-(-chunks // n)) // 8) * 8


def back_shapes(n, bands, tokens, rows, half, width, inner, units, hyper_width, hyper_units):
    f32, low = jnp.float32, jnp.bfloat16
    per_slot = rows_per_slot(n, width, inner, units)
    block = SPAN + per_slot + width // 128 + -(width // 128) % 8
    part, whole_row = ((rows, inner), f32), ((rows, units), f32)
    outs = dict(
        g_q=part, g_k=part, g_v=part, g_proj=part, g_up=whole_row, g_down=whole_row, pixel_o=((bands, tokens, 2 * half), low),
        map_o=((2, hyper_width, rows, half), f32), blocks_o=((n, block, 128), f32), bias_o=((rows, 2 * half), f32),
    )
    square = (2, hyper_width)
    shapes = [(4, hyper_width, hyper_width), (hyper_width, hyper_units), (hyper_units, hyper_width), square, square]
    shapes += [(1, hyper_width), (hyper_width, width)]
    outs.update({k: (v, f32) for k, v in zip(GENERATOR_OUTS, shapes)})
    specs = [ANY if k in dict(pixel_o=0, map_o=0) else VMEM for k in outs]
    buffers = dict(
        w_half=pltpu.VMEM((hyper_width, tiled(rows), half), f32),
        d_pix=pltpu.VMEM((bands, tokens, half), low),
        got=pltpu.VMEM((n, bands, rows, half), low),
        got32=pltpu.VMEM((n, SPAN, tiled(rows), half), f32),
        code=pltpu.VMEM((n * SPAN, hyper_width), f32),
        codes_turned=pltpu.VMEM((hyper_width, n * SPAN), low),
        terms=pltpu.VMEM((n, SPAN, hyper_width), low),
        term_box=pltpu.VMEM((2, n, SPAN, hyper_width), low),
        vectors=pltpu.VMEM((n, per_slot, 128), f32),
        vector_box=pltpu.VMEM((n, per_slot, 128), f32),
        bias_half=pltpu.VMEM((rows, half), f32),
    )
    sems = dict(
        blocal=(2,), p_send=(3,), p_recv=(3,), c_send=(2 * n,), c_recv=(2 * n,), b_send=(n - 1,),
        b_recv=(n - 1,), v_send=(n,), v_recv=(n,), u_send=(n - 1,), u_recv=(n - 1,),
    )
    buffers.update({k: pltpu.SemaphoreType.DMA(v) for k, v in sems.items()})
    return outs, specs, buffers


BACK = tuple(dict(
    w_half=0, d_pix=0, got=0, got32=0, code=0, codes_turned=0, terms=0, term_box=0, vectors=0, vector_box=0,
    bias_half=0,
))
BACK_SEMS = tuple(dict(
    blocal=0, p_send=0, p_recv=0, c_send=0, c_recv=0, b_send=0, b_recv=0, v_send=0, v_recv=0, u_send=0, u_recv=0,
))


def scatter_buffers(n, grid, rows, attn_lanes, mlp_lanes):
    low, pieces = jnp.bfloat16, 2 * len(orders_of(grid))
    slots = n - 1
    return [
        pltpu.VMEM((slots, rows, attn_lanes), low),
        pltpu.VMEM((slots, rows, mlp_lanes), low),
        pltpu.SemaphoreType.DMA((pieces, slots)),
        pltpu.SemaphoreType.DMA((pieces, slots)),
    ]


def weight_load(kern_w, w_half, sem, mp):
    half = w_half.shape[2]
    copy = pltpu.make_async_copy(kern_w.at[:, :, lanes_at(mp, half)], first_rows(w_half, kern_w.shape[1]), sem)
    copy.start()
    return copy


def whole_kernel(n, grid, names, *refs):
    r = Refs(names, refs)
    me, mp = lax.axis_index("dp"), lax.axis_index("mp")
    low, f32 = jnp.bfloat16, jnp.float32
    bands, tokens, half = r.pix.shape
    rows, inner = r.attn_out.shape
    units = r.mlp_in.shape[1]
    load = weight_load(r.kern_weight, r.w_half, r.local.at[0], mp)
    lanes = lanes_at(mp, half)
    pix_load = pltpu.make_async_copy(r.pixels.at[0, :, :, lanes], r.pix, r.local.at[1])
    pix_load.start()

    mine = pl.ds(pl.multiple_of(me * rows, 16), rows)
    for i in range(3):
        r.attn[mine, i * inner : (i + 1) * inner] = r.attn_in[i].astype(low)
    r.attn[mine, 3 * inner :] = r.attn_out[...].astype(low)
    r.mlp[mine, :units] = r.mlp_in[...].astype(low)
    r.mlp[mine, units:] = r.mlp_out[...].astype(low)
    count = r.band_count[0]
    r.facts_own[...] = wave_rows([r.wavelengths[0, b] for b in range(bands)], count)

    greet(n, me, mp, True)
    work = Front(n, grid, bands, r.facts, r.frequency, r.bias_token, r.w_half, r.b_half, r.k32, r.k16)
    work.share(r.facts_own, r.f_send, r.f_recv)
    gather = Gather(grid, rows, (r.attn, r.mlp), r.w_send, r.w_recv)
    split = len(gather.pieces) // 2
    attn_pieces, mlp_pieces = gather.pieces[:split], gather.pieces[split:]
    for piece in gather.pieces:
        gather.begin(piece)

    r.in_bias[...] = jnp.zeros_like(r.in_bias)
    r.in_bias[:, :inner] = r.attn_in_bias[0:1]
    r.in_bias[:, 2 * inner :] = r.attn_in_bias[1:2]
    r.out_bias[...] = r.attn_out_bias[...].reshape(r.out_bias.shape)
    r.up_bias[...] = r.mlp_in_bias[...].reshape(r.up_bias.shape)
    r.down_bias[...] = r.mlp_out_bias[...].reshape(r.down_bias.shape)
    r.b_half[...] = r.kern_bias[:, lanes]
    size = r.size_class[0]
    live = jnp.where(size == 0, tokens * 49 // 256, jnp.where(size == 1, tokens * 196 // 256, tokens))
    column = lax.broadcasted_iota(jnp.int32, (1, tokens), 1)
    r.key_mask[...] = ((column < live) & ((r.token_keep[...] == 1) | (column == 0))).astype(f32)
    r.row_scale[...] = (lax.broadcasted_iota(jnp.int32, (tokens, 1), 0) < live).astype(f32)
    r.band_mask[...] = (lax.broadcasted_iota(jnp.int32, r.band_mask.shape, 0) < count).astype(f32)

    kept = (r.rows, r.wide, r.prob.at[pl.ds(0, HYP_HEADS)])
    weights = (r.hyp_attn, r.hyp_mlp_in, r.hyp_mlp_out, r.hyp_gain, r.hyp_shift)
    work.generate(weights, r.patch_w, r.second, r.codes, r.patch_bias, kept)
    saves = []
    for i, (src, dst) in enumerate(zip(kept[1:], (r.wide_o, r.prob_o))):
        saves.append(pltpu.make_async_copy(src, dst, r.local.at[2 + i]))
        saves[-1].start()
    for piece in attn_pieces:
        gather.step(piece, 1)
    for piece in mlp_pieces:
        gather.step(piece, 1)
    load.wait()
    work.make(r.codes, rows)
    work.ready(rows)

    def kern_of(source):
        return r.kern.at[:, pl.ds(pl.multiple_of(rows * source, 16), rows)]

    fetch = Exchange(n, grid, r.k16, kern_of, r.k_send, r.k_recv, r.k_own)
    fetch.start()
    for number in range(2, len(grid) + 1):
        for piece in attn_pieces:
            gather.step(piece, number)
    pix_load.wait()
    for copy in saves:
        copy.wait()
    fetch.own.wait()
    for source in fetch.sources():
        fetch.arrive(source)

    scatter = Scatter(
        n, grid, rows, r.attn, r.mlp, r.attn_box, r.mlp_box,
        (r.g_q, r.g_k, r.g_v, r.g_proj, r.g_up, r.g_down), r.g_send, r.g_recv,
    )
    scatter_attn, scatter_mlp = scatter.pieces[:split], scatter.pieces[split:]

    def hook(at):
        if at in ("start", "embedded", "attended"):
            number = ("start", "embedded", "attended").index(at) + 2
            for number in range(number, number + 1 if at != "attended" else len(grid) + 1):
                for piece in mlp_pieces:
                    gather.step(piece, number)
        if at == "before feed":
            gather.sent(mlp_pieces)
        if at == "fed":
            scatter.start(0, scatter_mlp)
        if at == "before attention":
            gather.sent(attn_pieces)

    model = r.emb.shape[1]
    slope, mid, d_mid = r.wide.at[0, :, pl.ds(0, units)], r.wide.at[1, :, pl.ds(0, model)], r.wide.at[1, :, pl.ds(model, model)]
    finish = layer_body(
        inner, hook,
        r.pix, r.kern, r.attn, r.mlp, r.cotangent.at[0], r.band_mask, r.key_mask, r.row_scale, r.patch_bias, r.norm_gain,
        r.norm_shift, r.in_bias, r.out_bias, r.up_bias, r.down_bias,
        r.out_o, r.emb_grad, r.attn, r.mlp, r.small, r.small_up, r.small_in,
        r.emb, mid, r.part, r.inbox, r.norm_a, r.norm_b, r.qkv, r.prob, r.ctx, r.act, slope, r.d_out, r.d_pre, d_mid, r.d_att,
        r.d_ctx, r.d_qkv, r.turned, r.s_send, r.s_recv,
    )
    work.sent()
    fetch.sent()
    r.turned[2] = r.emb_grad[...].T
    tile = 2 * rows * (256 // (2 * rows)) if model % (2 * rows * (256 // (2 * rows))) == 0 else rows

    def kernel_gradients(b, bands_here):
        masked = [r.pix[b + i] * r.band_mask[pl.ds(b + i, 1)].astype(low) for i in range(bands_here)]
        masked = jnp.concatenate(masked, axis=1)
        for i in range(model // tile):
            made = dot(r.turned[2, i * tile : (i + 1) * tile], masked, NN).astype(low)
            for t in range(tile // rows):
                for c in range(bands_here):
                    part = made[t * rows : (t + 1) * rows, c * half : (c + 1) * half]
                    r.k16[i * (tile // rows) + t, b + c] = part

    pl.loop(0, bands // 2)(lambda j: kernel_gradients(2 * j, 2))
    if bands % 2:
        kernel_gradients(bands - 1, 1)

    exchange = Exchange(n, grid, r.k16, lambda source: r.got.at[source], r.a_send, r.a_recv, r.a_own)
    loads = []

    def finish_layer():
        finish()
        for i, (src, dst) in enumerate(zip((r.wide_o, r.prob_o), kept[1:])):
            loads.append(pltpu.make_async_copy(src, dst, r.local.at[2 + i]))
            loads[-1].start()

    def gradients(blocks, patch_at):
        for copy in loads:
            copy.wait()
        outs = [getattr(r, k) for k in GENERATOR_OUTS]
        generator_gradients(n, bands, recompute, blocks, patch_at, *weights, kept, r.d_mlp, r.tails, outs)

    def recompute(g):
        if n > GROUP:
            generator_forward(bands, r.facts, r.frequency, r.bias_token, g, *weights, *kept)

    back_body(
        n, grid, scatter, (scatter_mlp, scatter_attn), finish_layer, gradients, exchange,
        r.pix, r.kern, r.band_mask, r.emb_grad, r.small, r.small_up, r.small_in, r.patch_w, r.codes,
        r.pixel_o, r.map_o, r.blocks_o, r.bias_o,
        r.w_half, r.pix, r.got, r.k32, *[getattr(r, k) for k in BACK[4:]], None, *[getattr(r, k) for k in BACK_SEMS],
    )


def whole(n, **arguments):
    a = Refs(arguments, arguments.values())
    f32, low, dma = jnp.float32, jnp.bfloat16, pltpu.SemaphoreType.DMA
    grid = factors_of(n)
    _, bands, tokens, pixels = a.pixels.shape
    half = pixels // 2
    rows, inner = a.attn_out.shape
    units = a.mlp_in.shape[1]
    width = a.norm_gain.shape[1]
    hyper_width, hyper_units = a.hyp_mlp_in.shape
    outs, specs, buffers = back_shapes(n, bands, tokens, rows, half, width, inner, units, hyper_width, hyper_units)
    kept, _ = generator_scratch(hyper_width, hyper_units)
    outs = dict(out_o=((tokens, width), low)) | outs | dict(wide_o=(kept[1], f32), prob_o=(kept[2], f32))
    specs = [VMEM] + specs + [ANY, ANY]
    pieces = 2 * len(orders_of(grid))
    slots = n - 1
    scratch = dict(
        pix=((bands, tokens, half), low),
        attn=((width, 4 * inner), low),
        mlp=((width, 2 * units), low),
        kern=((bands, width, half), low),
        facts_own=((SPAN, hyper_width), low),
        facts=((n, SPAN, hyper_width), low),
        b_half=((rows, half), f32),
        k32=((n, SPAN, rows, half), f32),
        k16=((n, bands, rows, half), low),
        rows=(kept[0], f32),
        wide=(kept[1], f32),
        prob=((max(HYP_HEADS, inner // HEAD_DIM), tokens, tokens), f32),
        second=((n * SPAN, hyper_width), f32),
        codes=((n * SPAN, hyper_width), low),
        d_mlp=((2, GROUP * SPAN, hyper_width), f32),
        tails=((n, hyper_width), f32),
        patch_bias=((1, width), f32),
        in_bias=((1, 3 * inner), f32),
        out_bias=((1, width), f32),
        up_bias=((1, units), f32),
        down_bias=((1, width), f32),
        key_mask=((1, tokens), f32),
        row_scale=((tokens, 1), f32),
        band_mask=((SPAN, half), f32),
        emb=((tokens, width), f32),
        part=((3, tokens, width), f32),
        inbox=((3, tokens, width), f32),
        norm_a=((tokens, width), low),
        norm_b=((tokens, width), low),
        qkv=((tokens, 3 * inner), low),
        ctx=((tokens, inner), low),
        act=((tokens, units), low),
        d_out=((tokens, width), low),
        d_pre=((tokens, units), low),
        d_att=((tokens, width), low),
        d_ctx=((tokens, inner), low),
        d_qkv=((tokens, 3 * inner), low),
        turned=((3, width, tokens), low),
        emb_grad=((tokens, width), low),
        small=((8, width), f32),
        small_up=((1, units), f32),
        small_in=((1, 3 * inner), f32),
        attn_box=((slots, rows, 4 * inner), low),
        mlp_box=((slots, rows, 2 * units), low),
    )
    scratch = {k: pltpu.VMEM(*v) for k, v in scratch.items()}
    shared = dict(d_pix=0, got32=0)
    scratch.update({k: v for k, v in buffers.items() if k not in shared})
    scratch.update(zip(dict(k_send=0, k_recv=0, k_own=0), exchange_sems(n)))
    scratch.update(zip(dict(a_send=0, a_recv=0, a_own=0), exchange_sems(n)))
    sems = dict(
        local=(4,), f_send=(n - 1,), f_recv=(n - 1,), w_send=(pieces, n - 1), w_recv=(pieces, n),
        s_send=(5, 2), s_recv=(5, 2), g_send=(pieces, slots), g_recv=(pieces, slots),
    )
    names = [*arguments, *outs, *scratch, *sems]
    smem = pl.BlockSpec(memory_space=pltpu.SMEM)
    places = dict(pixels=ANY, kern_weight=ANY, band_count=smem, wavelengths=smem, size_class=smem)
    flops = 2 * tokens * width * (3 * bands * half + 9 * inner * 2 + 9 * units)
    out = pl.pallas_call(
        partial(whole_kernel, n, grid, names),
        out_shape=[jax.ShapeDtypeStruct(*o) for o in outs.values()],
        in_specs=[places.get(k, VMEM) for k in arguments],
        out_specs=specs,
        scratch_shapes=list(scratch.values()) + [dma(v) for v in sems.values()],
        compiler_params=params(6, BIG_VMEM),
        cost_estimate=pl.CostEstimate(flops=flops, bytes_accessed=3 * 10**7, transcendentals=10**6),
        name="whole",
    )(*arguments.values())
    return dict(zip(outs, out))


def layer_kernel(inner, *refs):
    me, mp = lax.axis_index("dp"), lax.axis_index("mp")
    sem = pltpu.get_barrier_semaphore()
    pl.semaphore_signal(sem, inc=1, device_id=(me, 1 - mp), device_id_type=MESH)
    pl.semaphore_wait(sem, 1)
    layer_body(inner, lambda at: None, *refs)()


BACK_INS = tuple(dict(
    pix=0, kern=0, band_mask=0, emb_grad=0, small=0, small_up=0, small_in=0, patch_w=0, codes=0, facts=0,
    frequency=0, token=0, w_attn=0, w_in=0, w_out=0, gain=0, shift=0, attn=0, mlp=0, d_kern=0, kern_w=0,
))


def back_kernel(n, grid, names, *refs):
    r = Refs(names, refs)
    me, mp = lax.axis_index("dp"), lax.axis_index("mp")
    load = weight_load(r.kern_w, r.w_half, r.load_sem.at[0], mp)
    terms = []
    for i, (src, dst) in enumerate(((r.attn, r.attn_acc), (r.mlp, r.mlp_acc))):
        terms.append(pltpu.make_async_copy(src, dst, r.load_sem.at[1 + i]))
        terms[-1].start()
    greet(n, me, mp, True)
    outs = (r.g_q, r.g_k, r.g_v, r.g_proj, r.g_up, r.g_down)
    for copy in terms:
        copy.wait()
    scatter = Scatter(
        n, grid, r.attn.shape[1], r.attn_acc, r.mlp_acc, r.attn_box, r.mlp_box, outs, r.g_send, r.g_recv
    )
    scatter.start(0, scatter.pieces)
    exchange = Exchange(n, grid, r.d_kern, lambda source: r.got.at[source], r.a_send, r.a_recv, r.a_own)
    weights = (r.w_attn, r.w_in, r.w_out, r.gain, r.shift)
    kept = (r.rows, r.wide, r.prob)
    bands = r.pix.shape[0]

    def recompute(g):
        generator_forward(bands, r.facts, r.frequency, r.token, g, *weights, *kept)

    def gradients(blocks, patch_at):
        outs = [getattr(r, k) for k in GENERATOR_OUTS]
        generator_gradients(n, bands, recompute, blocks, patch_at, *weights, kept, r.d_mlp, r.tails, outs)

    back_body(
        n, grid, scatter, (scatter.pieces, []), lambda: None, gradients, exchange,
        r.pix, r.kern, r.band_mask, r.emb_grad, r.small, r.small_up, r.small_in, r.patch_w, r.codes,
        r.pixel_o, r.map_o, r.blocks_o, r.bias_o, *[getattr(r, k) for k in BACK], load, *[getattr(r, k) for k in BACK_SEMS],
    )


def layer_and_back(n, inner, kern_w, patch_w, layer_ins, generator):
    pix, kern, attn, mlp, _, band_mask = layer_ins[:6]
    grid = factors_of(n)
    bands, tokens, half = pix.shape
    width, units = attn.shape[0], mlp.shape[1] // 2
    hyper_width, rows, _ = kern_w.shape
    hyper_units = generator["w_in"].shape[1]
    f32, low = jnp.float32, jnp.bfloat16
    shape, dma = jax.ShapeDtypeStruct, pltpu.SemaphoreType.DMA
    outs, specs, buffers = back_shapes(n, bands, tokens, rows, half, width, inner, units, hyper_width, hyper_units)
    layer_outs = [
        ((tokens, width), low),
        (attn.shape, low),
        (mlp.shape, low),
        ((8, width), f32),
        ((1, units), f32),
        ((1, 3 * inner), f32),
    ]
    layer_out, emb_grad, attn_grad, mlp_grad, small, small_up, small_in = pl.pallas_call(
        partial(layer_kernel, inner),
        out_shape=[shape((tokens, width), low)] + [shape(*o) for o in layer_outs],
        in_specs=[VMEM] * LAYER_INS,
        out_specs=[VMEM] * 7,
        scratch_shapes=layer_buffers(inner, units, tokens, width),
        compiler_params=params(3, BIG_VMEM),
        name="layer",
    )(*layer_ins)
    d_kern = fast_einsum("tc,btp->bcp", emb_grad, pix * band_mask[:bands, None].astype(low)).astype(low)
    d_kern = d_kern.reshape(bands, n, rows, half).transpose(1, 0, 2, 3)
    attn_grad, mlp_grad = attn_grad.reshape(n, rows, -1), mlp_grad.reshape(n, rows, -1)
    ins = dict(
        pix=pix, kern=kern, band_mask=band_mask, emb_grad=emb_grad, small=small, small_up=small_up, small_in=small_in,
        attn=attn_grad, mlp=mlp_grad, patch_w=patch_w, d_kern=d_kern, kern_w=kern_w, **generator,
    )
    kept, _ = generator_scratch(hyper_width, hyper_units)
    scratch = dict(attn_acc=pltpu.VMEM(attn_grad.shape, low), mlp_acc=pltpu.VMEM(mlp_grad.shape, low))
    scratch.update(
        zip(dict(attn_box=0, mlp_box=0, g_send=0, g_recv=0), scatter_buffers(n, grid, rows, attn.shape[1], mlp.shape[1]))
    )
    scratch.update(zip(dict(a_send=0, a_recv=0, a_own=0), exchange_sems(n)))
    scratch.update({k: pltpu.VMEM(v, f32) for k, v in zip(dict(rows=0, wide=0, prob=0), kept)})
    scratch.update(
        d_mlp=pltpu.VMEM((2, GROUP * SPAN, hyper_width), f32), tails=pltpu.VMEM((n, hyper_width), f32), load_sem=dma((3,))
    )
    scratch.update(buffers)
    out = pl.pallas_call(
        partial(back_kernel, n, grid, [*BACK_INS, *outs, *scratch]),
        out_shape=[shape(*o) for o in outs.values()],
        in_specs=[VMEM] * (len(BACK_INS) - 4) + [ANY] * 4,
        out_specs=specs,
        scratch_shapes=list(scratch.values()),
        compiler_params=params(2, BIG_VMEM),
        name="back",
    )(*[ins[k] for k in BACK_INS])
    return dict(out_o=layer_out) | dict(zip(outs, out))


PASSED = tuple(dict(
    out_o=0, pixel_o=0, g_q=0, g_k=0, g_v=0, g_proj=0, g_up=0, g_down=0, bias_o=0, g_in=0, g_out=0, g_attn=0,
    g_patch=0,
))
SMALL = tuple(dict(
    blocks_o=0, g_gain=0, g_shift=0, g_token=0,
))


def tail_kernel(per_slot, names, *refs):
    r = Refs(names, refs)
    loads, stores = [], []
    for i in range(2):
        loads.append(pltpu.make_async_copy(r.map_o.at[i], r.via_map.at[i], r.load.at[i]))
    for i, name in enumerate(PASSED):
        loads.append(pltpu.make_async_copy(getattr(r, name), getattr(r, "via_" + name), r.load.at[2 + i]))
    for copy in loads:
        copy.start()
    r.gain_p[...] = r.g_gain[...]
    r.shift_p[...] = r.g_shift[...]
    r.token_p[...] = r.g_token[...].reshape(r.token_p.shape)
    lane = 128
    chunks = []
    for ref, which in ((r.n_gain, 0), (r.n_gain, 1), (r.n_shift, 0), (r.n_shift, 1), (r.in_bias, 0), (r.in_bias, 1)):
        chunks += [(ref, which, i) for i in range(ref.shape[1] // lane)]
    for ref in (r.out_bias, r.up_bias, r.down_bias):
        chunks += [(ref, None, i) for i in range(ref.shape[0] // lane)]
    each = -(-len(chunks) // r.blocks_o.shape[0])
    for k, (ref, which, i) in enumerate(chunks):
        at = SPAN + k % each
        if which is None:
            ref[pl.ds(i * lane, lane)] = r.blocks_o[k // each, at]
        else:
            ref[which : which + 1, i * lane : (i + 1) * lane] = r.blocks_o[k // each, at : at + 1]
    half = r.map_p.shape[2] // 2
    sources = [r.via_map.at[0], r.via_map.at[1]] + [getattr(r, "via_" + k) for k in PASSED]
    targets = [r.map_p.at[:, :, pl.ds(i * half, half)] for i in range(2)]
    targets += [r.out_p, r.pixel_p, r.in_p.at[0], r.in_p.at[1], r.in_p.at[2], r.proj_p, r.up_p, r.down_p, r.bias_p]
    targets += [r.w_in_p, r.w_out_p, r.w_attn_p, r.patch_p]
    for i, (load, src, dst) in enumerate(zip(loads, sources, targets, strict=True)):
        load.wait()
        stores.append(pltpu.make_async_copy(src, dst, r.store.at[i]))
        stores[-1].start()
    for copy in stores:
        copy.wait()


def tail(made):
    m = Refs(made, made.values())
    f32, low = jnp.float32, jnp.bfloat16
    n = m.blocks_o.shape[0]
    (rows, inner), units = m.g_proj.shape, m.g_up.shape[1]
    hyper_width, width = m.g_patch.shape
    half = m.map_o.shape[3]
    outs = dict(
        gain_p=m.g_gain.shape, shift_p=m.g_shift.shape, token_p=(hyper_width,), n_gain=(2, width),
        n_shift=(2, width), in_bias=(2, inner), out_bias=(width,), up_bias=(units,), down_bias=(width,),
    )
    outs = {k: (v, f32) for k, v in outs.items()}
    direct = dict(
        map_p=((hyper_width, rows, 2 * half), f32), out_p=(m.out_o.shape, low),
        pixel_p=(m.pixel_o.shape, low), in_p=((3, rows, inner), f32), proj_p=((rows, inner), f32),
        up_p=((rows, units), f32), down_p=((rows, units), f32), bias_p=((rows, 2 * half), f32),
        w_in_p=(m.g_in.shape, f32), w_out_p=(m.g_out.shape, f32), w_attn_p=(m.g_attn.shape, f32),
        patch_p=(m.g_patch.shape, f32),
    )
    scratch = {"via_" + k: (made[k].shape, made[k].dtype) for k in PASSED}
    scratch.update(via_map=(m.map_o.shape, f32))
    far = tuple(dict(map_o=0)) + PASSED
    names = [*SMALL, *far, *outs, *direct, *scratch, "load", "store"]
    results = pl.pallas_call(
        partial(tail_kernel, rows_per_slot(n, width, inner, units), names),
        out_shape=[jax.ShapeDtypeStruct(*v) for v in (outs | direct).values()],
        in_specs=[VMEM] * len(SMALL) + [ANY] * len(far),
        out_specs=[VMEM] * len(outs) + [ANY] * len(direct),
        scratch_shapes=[pltpu.VMEM(*v) for v in scratch.values()] + [pltpu.SemaphoreType.DMA((len(far) + 1,))] * 2,
        compiler_params=pltpu.CompilerParams(vmem_limit_bytes=BIG_VMEM),
        name="tail",
    )(*[made[k] for k in SMALL + far])
    return Refs(outs | direct, results)


def fast_einsum(pattern, left_side, right_side):
    return jnp.einsum(pattern, left_side, right_side, preferred_element_type=jnp.float32)


def in_parts(
    n, pixels, band_count, wavelengths, size_class, token_keep, hyp_attn, hyp_mlp_in, hyp_mlp_out, hyp_gain, hyp_shift, bias_token,
    kern_weight, kern_bias, patch_w, norm_gain, norm_shift, attn_in, attn_in_bias, attn_out, attn_out_bias, mlp_in, mlp_in_bias,
    mlp_out, mlp_out_bias, cotangent, frequency,
):
    mp = lax.axis_index("mp")
    _, bands, tokens, pix_size = pixels.shape
    hyper_width = hyp_attn.shape[1]
    half = pix_size // 2
    low = jnp.bfloat16
    inner = attn_in.shape[2]
    band_valid = jnp.arange(SPAN) < band_count[0]
    facts_own = wave_rows([wavelengths[0, b] for b in range(bands)], band_count[0])

    attn_shard = jnp.concatenate([attn_in[0], attn_in[1], attn_in[2], attn_out], axis=1).astype(low)
    mlp_shard = jnp.concatenate([mlp_in, mlp_out], axis=1).astype(low)
    weights = (hyp_attn, hyp_mlp_in, hyp_mlp_out, hyp_gain, hyp_shift)
    kernel, attn_all, mlp_all, facts, patch_bias, codes, *_ = front(
        n, bands, facts_own, frequency, bias_token, *weights, patch_w, kern_weight, kern_bias, attn_shard, mlp_shard
    )
    live_rows = jnp.where(
        size_class[0] == 0, tokens * 49 // 256, jnp.where(size_class[0] == 1, tokens * 196 // 256, tokens)
    )
    position = jnp.arange(tokens)
    row_valid = position < live_rows
    key_valid = row_valid & ((token_keep[0] == 1) | (position == 0))
    input_bias = jnp.concatenate([attn_in_bias[0], jnp.zeros_like(attn_in_bias[0]), attn_in_bias[1]])
    layer_ins = (
        lax.dynamic_slice_in_dim(pixels[0], mp * half, half, 2),
        kernel,
        attn_all,
        mlp_all,
        cotangent[0],
        jnp.broadcast_to(band_valid.astype(jnp.float32)[:, None], (SPAN, half)),
        key_valid.astype(jnp.float32)[None],
        row_valid.astype(jnp.float32)[:, None],
        patch_bias,
        norm_gain,
        norm_shift,
        input_bias[None],
        attn_out_bias[None],
        mlp_in_bias[None],
        mlp_out_bias[None],
    )
    generator = dict(
        codes=codes, facts=facts, frequency=frequency, token=bias_token, w_attn=hyp_attn, w_in=hyp_mlp_in, w_out=hyp_mlp_out,
        gain=hyp_gain, shift=hyp_shift,
    )
    return layer_and_back(n, inner, kern_weight, patch_w, layer_ins, generator)


def per_device(
    n,
    pixels,
    band_count,
    wavelengths,
    size_class,
    token_keep,
    hyp_attn,
    hyp_mlp_in,
    hyp_mlp_out,
    hyp_gain,
    hyp_shift,
    bias_token,
    kern_weight,
    kern_bias,
    patch_bias_weight,
    norm_gain,
    norm_shift,
    attn_in,
    attn_in_bias,
    attn_out,
    attn_out_bias,
    mlp_in,
    mlp_in_bias,
    mlp_out,
    mlp_out_bias,
    cotangent,
):
    slot_count, bands = pixels.shape[:2]
    assert slot_count == 1 and n % GROUP == 0 and bands + 1 <= SPAN
    arguments = dict(
        pixels=pixels, band_count=band_count, wavelengths=wavelengths, size_class=size_class, token_keep=token_keep,
        hyp_attn=hyp_attn, hyp_mlp_in=hyp_mlp_in, hyp_mlp_out=hyp_mlp_out, hyp_gain=hyp_gain, hyp_shift=hyp_shift,
        bias_token=bias_token, kern_weight=kern_weight, kern_bias=kern_bias, patch_w=patch_bias_weight, norm_gain=norm_gain,
        norm_shift=norm_shift, attn_in=attn_in, attn_in_bias=attn_in_bias, attn_out=attn_out, attn_out_bias=attn_out_bias,
        mlp_in=mlp_in, mlp_in_bias=mlp_in_bias, mlp_out=mlp_out, mlp_out_bias=mlp_out_bias, cotangent=cotangent,
    )
    half_width = hyp_attn.shape[1] // 2
    frequency = 10000.0 ** (-np.arange(half_width, dtype=np.float32) * 2.0 / (2 * half_width))
    frequency = jnp.asarray(np.concatenate([frequency, frequency])[None].astype(np.float32))
    make = whole if kern_weight.shape[1] % 16 == 0 else in_parts
    done = tail(make(n, frequency=frequency, **arguments))
    return (
        done.out_p[None],
        done.pixel_p[None],
        done.w_attn_p,
        done.w_in_p,
        done.w_out_p,
        done.gain_p,
        done.shift_p,
        done.token_p,
        done.map_p,
        done.bias_p,
        done.patch_p,
        done.n_gain,
        done.n_shift,
        done.in_p,
        done.in_bias,
        done.proj_p,
        done.out_bias,
        done.up_p,
        done.up_bias,
        done.down_p,
        done.down_bias,
    )


def solution(mesh):
    return jax.shard_map(
        partial(per_device, mesh.shape["dp"]),
        mesh=mesh,
        in_specs=(
            P("dp", None, None, None),
            P("dp"),
            P("dp", None),
            P("dp"),
            P("dp", None),
            P(),
            P(),
            P(),
            P(),
            P(),
            P(),
            P(None, "dp", None),
            P("dp", None),
            P(),
            P(),
            P(),
            P(None, "dp", "mp"),
            P(None, "mp"),
            P("dp", "mp"),
            P(),
            P("dp", "mp"),
            P("mp"),
            P("dp", "mp"),
            P(),
            P("dp", None, None),
        ),
        out_specs=(
            P("dp", None, None),
            P("dp", None, None, None),
            P(),
            P(),
            P(),
            P(),
            P(),
            P(),
            P(None, "dp", None),
            P("dp", None),
            P(),
            P(),
            P(),
            P(None, "dp", "mp"),
            P(None, "mp"),
            P("dp", "mp"),
            P(),
            P("dp", "mp"),
            P("mp"),
            P("dp", "mp"),
            P(),
        ),
        check_vma=False,
    )
```

time: 367 us -> 275 us (0.75)
  Pallas kernels: 335 us -> 272 us
  other arithmetic: 14.9 us -> 0 us
  local copies, waits for them, and re-layouts: 14.1 us -> 0 us
    pallas_call x3 -> x2, Pallas kernels: 335 us -> 272 us  [the longest x1 262 us: whole(): pl.pallas_call(partial(whole_kernel, n, grid, names), out_shape=[jax.Shap...]
    unnamed x18 -> x0, local copies, waits for them, and re-layouts: 5.72 us -> none
    another operation x5 -> x0, other arithmetic: 5.45 us -> none
    broadcast_in_dim x6 -> x0, local copies, waits for them, and re-layouts: 5.09 us -> none  [the longest x1 1.29 us: per_device(): mlp_in_bias[None]]
    pallas_call x3 -> x0, other arithmetic: 3.92 us -> none  [tail(): pl.pallas_call(partial(tail_kernel, n, bands, per_slot, recompute), out_s...]
where the time goes in v4:
time: 275 us
  Pallas kernels  272 us (99%)
    pallas_call x1, Pallas kernels, whole(): pl.pallas_call(partial(whole_kernel, n, grid, names), out_shape=[jax.Shap...  262 us
    pallas_call x1, Pallas kernels, tail(): pl.pallas_call(partial(tail_kernel, rows_per_slot(n, width, inner, units)...  10.6 us

profile of v4, /device:TPU:0, one launch (start us, length us, event | category | flops | bytes accessed | tf_op | source)
XLA Modules:
  0.0 274.6 jit_solution(6448588948042780589)
XLA Ops:
  2.0 261.9 %whole.1 = (bf16[256,768]{1,0:T(8,128)(2,1)}, f32[48,384]{1,0:T(8,128)}, f32[48,384]{1,0:T(8,128)}, f32[48,384]{1,0:T(8,128)}, f32[48,384]{1,0:T(8,128)}, /*inde...) custom-call(f32[1,128]{1,0:T(1,128)} %constant.2.clone.refs_0_, ...), custom_call_target="tpu_custom_call" | custom-call | flops 10116661248 | bytes 30000000 | tf_op jit(solution)/shard_map/whole/pallas_call | solution.py:1254
  263.8 10.6 %tail.1 = (f32[2,128]{1,0:T(2,128)}, f32[2,128]{1,0:T(2,128)}, f32[128]{0:T(128)}, f32[2,768]{1,0:T(2,128)}, f32[2,768]{1,0:T(2,128)}, /*index=5*/f32[2,384]{1,0...) custom-call(f32[16,32,128]{2,1,0:T(8,128)} %get-tuple-element.60.ref, ...), custom_call_target="tpu_custom_call" | custom-call | tf_op jit(solution)/shard_map/tail/pallas_call | solution.py:1443

commit v5 on v4

--- a/solution.py
+++ b/solution.py
@@ -56,7 +56,16 @@
 
 def orders_of(grid):
     dims = tuple(range(len(grid)))
-    return [dims, dims[:-2] + (dims[-1], dims[-2])] if len(grid) > 2 else [dims]
+    if len(grid) != 4:
+        return [dims]
+    return [(0, 1, 2, 3), (0, 2, 3, 1), (0, 1, 3, 2), (0, 3, 2, 1)]
+
+
+def parts_of(lanes, grid):
+    shares = (5, 1, 5, 1) if len(grid) == 4 else (1,)
+    unit = lanes // sum(shares)
+    assert unit % 128 == 0
+    return [(sum(shares[:i]) * unit, share * unit) for i, share in enumerate(shares)]
 
 
 def greet(n, me, mp, both):
@@ -278,10 +287,9 @@
         self.pieces = []
         orders = orders_of(grid)
         for array in arrays:
-            width = array.shape[-1] // len(orders)
-            for i, order in enumerate(orders):
+            for (first, width), order in zip(parts_of(array.shape[-1], grid), orders):
                 self.sends[len(self.pieces)] = []
-                self.pieces.append((array, pl.ds(i * width, width), order, len(self.pieces)))
+                self.pieces.append((array, pl.ds(first, width), order, len(self.pieces)))
 
     def pass_on(self, piece, owner, number):
         array, cols, order, p = piece
@@ -718,10 +726,14 @@
         self.send_sem, self.recv_sem, self.sends = send, recv, []
         self.pieces = []
         for terms, box, out in ((attn, attn_box, outs[:4]), (mlp, mlp_box, outs[4:])):
-            width, share = terms.shape[-1] // len(self.orders), len(out) // len(self.orders)
-            for i, order in enumerate(self.orders):
-                cols, to = pl.ds(i * width, width), out[i * share : (i + 1) * share]
-                self.pieces.append((terms, box, to, cols, order, len(self.pieces)))
+            for (first, width), order in zip(parts_of(terms.shape[-1], grid), self.orders):
+                start, to = 0, []
+                for ref in out:
+                    low, high = max(start, first), min(start + ref.shape[1], first + width)
+                    if low < high:
+                        to.append((ref, low - start, low - first, high - low))
+                    start += ref.shape[1]
+                self.pieces.append((terms, box, to, pl.ds(first, width), order, len(self.pieces)))
         self.slots = {}
         for which, order in enumerate(self.orders):
             number = 0
@@ -759,9 +771,8 @@
                 if t < self.stages - 1:
                     block[...] = total.astype(terms.dtype)
                 else:
-                    width = total.shape[1] // len(outs)
-                    for i, out in enumerate(outs):
-                        out[...] = total[:, i * width : (i + 1) * width]
+                    for ref, to, first, width in outs:
+                        ref[:, to : to + width] = total[:, first : first + width]
 
     def go_on(self, t, pieces):
         if t < self.stages:
@@ -853,8 +864,8 @@
         adding.append(remote(vectors.at[there], vector_box.at[n - k], v_send.at[k], v_recv.at[n - k], (there, mp)))
     codes_turned[...] = codes[...].T
 
+    scatter.go_on(1, mine)
     scatter.go_on(0, rest)
-    scatter.go_on(1, mine)
     scatter.go_on(1, rest)
 
     for copy in adding:

time: 275 us -> 267 us (0.971)
  Pallas kernels: 272 us -> 264 us
    pallas_call x1, Pallas kernels: 262 us -> 254 us  [whole(): pl.pallas_call(partial(whole_kernel, n, grid, names), out_shape=[jax.Shap...]
where the time goes in v5:
time: 267 us; the launch traced here: 266 us
  Pallas kernels  264 us (99%)
    pallas_call x1, Pallas kernels, whole(): pl.pallas_call(partial(whole_kernel, n, grid, names), out_shape=[jax.Shap...  254 us
    pallas_call x1, Pallas kernels, tail(): pl.pallas_call(partial(tail_kernel, rows_per_slot(n, width, inner, units)...  10.6 us

profile of v5, /device:TPU:0, one launch (start us, length us, event | category | flops | bytes accessed | tf_op | source)
XLA Modules:
  0.0 266.4 jit_solution(12092126939323489161)
XLA Ops:
  2.0 253.6 %whole.1 = (bf16[256,768]{1,0:T(8,128)(2,1)}, f32[48,384]{1,0:T(8,128)}, f32[48,384]{1,0:T(8,128)}, f32[48,384]{1,0:T(8,128)}, f32[48,384]{1,0:T(8,128)}, /*inde...) custom-call(f32[1,128]{1,0:T(1,128)} %constant.2.clone.refs_0_, ...), custom_call_target="tpu_custom_call" | custom-call | flops 10116661248 | bytes 30000000 | tf_op jit(solution)/shard_map/whole/pallas_call | solution.py:1265
  255.6 10.6 %tail.1 = (f32[2,128]{1,0:T(2,128)}, f32[2,128]{1,0:T(2,128)}, f32[128]{0:T(128)}, f32[2,768]{1,0:T(2,128)}, f32[2,768]{1,0:T(2,128)}, /*index=5*/f32[2,384]{1,0...) custom-call(f32[16,32,128]{2,1,0:T(8,128)} %get-tuple-element.60.ref, ...), custom_call_target="tpu_custom_call" | custom-call | tf_op jit(solution)/shard_map/tail/pallas_call | solution.py:1454
